TPU v7x, 128 devices: a whole 4x4x4 slice. The times are simulated.
128 devices in a mesh: head: 4 (over z), page: 32 (over y, x, core).
Axes of the slice: x: 4, y: 4, z: 4, core: 2. Of those that a mesh axis runs over, the one named last changes fastest.
Arguments:
- hidden: bfloat16 [4096, 4096], P('page', 'head'), may hold values from -6 to 6
- group_qkv: bfloat16 [4096, 6144], P('page', 'head'), may hold values from -2400 to 2400
- mlp_branch: bfloat16 [4096, 4096], P('page', 'head'), may hold values from -6 to 6
- key_cache: bfloat16 [416, 128, 2048], P('page', None, 'head'), may hold values from -6 to 6
- paged_value_cache: bfloat16 [416, 128, 2048], P('page', None, 'head'), may hold values from -6 to 6
- cache_lengths: int32 [8], replicated, may hold values from 2 to 4096, as said below
- page_table: int32 [8, 36], replicated, may hold values from 0 to 415, as said below
- dense_weight: bfloat16 [2048, 4096], P('head'), may hold values from -0.125 to 0.125
- dense_bias: float32 [4096], replicated, may hold values from -3 to 3
- norm_gain: float32 [4096], replicated, may hold values from 0.1 to 1.9
- norm_bias: float32 [4096], replicated, may hold values from -3 to 3
- qkv_weight: bfloat16 [4096, 6144], P(None, 'head'), may hold values from -0.09375 to 0.09375
- qkv_bias: float32 [6144], P('head'), may hold values from -3 to 3
Outputs:
- new_hidden: bfloat16 [4096, 4096], P('page', 'head')
- next_qkv: bfloat16 [4096, 6144], P('page', 'head')
- key_out: bfloat16 [416, 128, 2048], P('page', None, 'head')
- value_out: bfloat16 [416, 128, 2048], P('page', None, 'head')
Inputs may be any that keep to these rules, and one draw needn't show every extreme that they name: `cache_lengths`: one request has exactly 4096 cached positions and another exactly 2. `page_table`: all entries are distinct slots; slot s lies on index s // 13 of page.
All inputs are finite; a program needn't handle non-finite values.
Results may differ from a plain program's by a relative error of at most 0.0075.
Values may be sent and summed in bfloat16 or wider, within the bound.
No kernel may reach another device: no remote copies, remote signals or barrier semaphores. Data moves between devices by JAX's collectives and lax.ppermute only.
A program may use at most 192 MiB of HBM per device.

v0:
```python
import math

import jax
import jax.numpy as jnp
from jax import lax
from jax.experimental import pallas as pl
from jax.experimental.pallas import tpu as pltpu
from jax.sharding import PartitionSpec as P

D = 4096
HS = 128
ROT = 32
PT = 128
GROUP = 512
LH = 4
LW = LH * HS
SLOTS = 13
REQS = 8
MAXP = 36
TOK = 128
PIECES = LW + 32
COLS = D // 4
QW = 1536
NEG = -1e30
C2 = math.log2(math.e) / math.sqrt(HS)
F32 = jnp.float32
BF16 = jnp.bfloat16
VMEM = pltpu.VMEM
SMEM = pltpu.SMEM


def whole(space=VMEM):
    return pl.BlockSpec(memory_space=space)


def head_rows(h):
    return slice(h * HS, (h + 1) * HS)


def rotary_kernel(x_ref, cos_ref, sin_ref, q_ref, kv_ref):
    cosine = cos_ref[...]
    sine = sin_ref[...]
    half = ROT // 2
    for h in range(LH):
        for which in range(2):
            base = (3 * h + which) * HS
            turned = x_ref[:, base : base + HS].astype(F32).T
            a = turned[0:half]
            b = turned[half:ROT]
            done = jnp.concatenate(
                [a * cosine - b * sine, b * cosine + a * sine, turned[ROT:]], axis=0
            )
            if which == 0:
                q_ref[head_rows(h), :] = done.astype(BF16)
            else:
                kv_ref[:, head_rows(h)] = done.T.astype(BF16)
        base = (3 * h + 2) * HS
        kv_ref[:, LW + h * HS : LW + (h + 1) * HS] = x_ref[:, base : base + HS]


def rotary(group_qkv, cosine, sine):
    return pl.pallas_call(
        rotary_kernel,
        out_shape=(
            jax.ShapeDtypeStruct((LW, TOK), BF16),
            jax.ShapeDtypeStruct((TOK, 2 * LW), BF16),
        ),
        in_specs=[whole()] * 3,
        out_specs=(whole(), whole()),
        name="rotary",
    )(group_qkv, cosine, sine)


def split3(value):
    top = value.astype(BF16)
    rest = value - top.astype(F32)
    middle = rest.astype(BF16)
    low = (rest - middle.astype(F32)).astype(BF16)
    return top, middle, low


def stat_rows(stats):
    width = stats.shape[1]
    return jnp.concatenate(
        [piece.astype(F32) for piece in split3(stats)] + [jnp.zeros((8, width), F32)], axis=0
    ).astype(BF16)


def attention_kernel(with_fresh, info, lens, table, q_ref, k_own, v_own, k_other, v_other, *rest):
    if with_fresh:
        fresh_own, fresh_other, *rest = rest
    o_ref, kbuf, vbuf, sems, pages, qs, acc, stats = rest
    page = info[0]
    row = info[1]
    x = info[2]
    core = info[3]
    chip = lax.div(page, 2)

    def copies(n, local, k_src, v_src):
        return (
            pltpu.make_async_copy(k_src.at[local], kbuf.at[n], sems.at[n, 0]),
            pltpu.make_async_copy(v_src.at[local], vbuf.at[n], sems.at[n, 1]),
        )

    bounds = []
    count = jnp.int32(0)
    for part in range(2):
        request = 2 * row + part
        used = lax.div(lens[request] + (PT - 1), PT)

        def scan(g, n, request=request):
            slot = table[request, g]
            device = lax.div(slot, SLOTS)
            local = slot - device * SLOTS
            here = lax.div(device, 2) == chip

            @pl.when(here)
            def _():
                pages[n] = g

                @pl.when(device == page)
                def _():
                    for copy in copies(n, local, k_own, v_own):
                        copy.start()

                @pl.when(device != page)
                def _():
                    for copy in copies(n, local, k_other, v_other):
                        copy.start()

            return n + here.astype(jnp.int32)

        first = count
        count = lax.fori_loop(0, used, scan, count)
        bounds.append((first, count))

    key_row = lax.broadcasted_iota(jnp.int32, (PT, 2 * TOK), 0)
    lane = lax.broadcasted_iota(jnp.int32, (PT, 2 * TOK), 1)
    query_index = core * TOK + lane + jnp.where(lane >= TOK, TOK, 0)

    def absorb(key_of, value_of, mask, guard):
        old = stats[...]
        new_rows = []
        for h in range(LH):
            scores = jnp.dot(key_of(h), qs[h], preferred_element_type=F32)
            scores = jnp.where(mask, scores, NEG)
            old_peak = old[h : h + 1]
            peak = jnp.maximum(old_peak, jnp.max(scores, axis=0, keepdims=True))
            weights = jnp.exp2((scores - peak) * C2)
            if guard:
                weights = jnp.where(mask, weights, 0.0)
            decay = jnp.exp2((old_peak - peak) * C2)
            total = old[LH + h : LH + h + 1] * decay + jnp.sum(weights, axis=0, keepdims=True)
            acc[head_rows(h), :] = acc[head_rows(h), :] * decay + lax.dot_general(
                value_of(h), weights.astype(BF16), (((0,), (0,)), ((), ())),
                preferred_element_type=F32,
            )
            new_rows.append((peak, total))
        stats[...] = jnp.concatenate([r[0] for r in new_rows] + [r[1] for r in new_rows], axis=0)

    for part in range(2):
        request = 2 * row + part
        left = lax.bitwise_and(x - 2 * part, 3)
        right = lax.bitwise_and(x - 2 * part - 1, 3)
        for h in range(LH):
            qs[h] = jnp.concatenate(
                [q_ref[left, head_rows(h), :], q_ref[right, head_rows(h), :]], axis=1
            )
        acc[...] = jnp.zeros_like(acc)
        stats[...] = jnp.where(
            lax.broadcasted_iota(jnp.int32, (2 * LH, 2 * TOK), 0) < LH, NEG, 0.0
        )

        def step(n, carry, request=request):
            for copy in copies(n, 0, k_own, v_own):
                copy.wait()
            mask = key_row < lens[request] - pages[n] * PT
            absorb(
                lambda h: kbuf[n, :, head_rows(h)], lambda h: vbuf[n, :, head_rows(h)], mask, False
            )
            return carry

        first, last = bounds[part]
        lax.fori_loop(first, last, step, 0)
        if with_fresh:

            @pl.when(lax.div(x, 2) == part)
            def _():
                for source, index in ((fresh_own, core), (fresh_other, 1 - core)):
                    start = (2 * lax.bitwise_and(x, 1) + index) * TOK
                    absorb(
                        lambda h: source[:, head_rows(h)],
                        lambda h: source[:, LW + h * HS : LW + (h + 1) * HS],
                        start + key_row <= query_index,
                        True,
                    )

        tail = stat_rows(stats[...])
        for block, half in ((left, slice(0, TOK)), (right, slice(TOK, 2 * TOK))):
            for h in range(LH):
                o_ref[block, head_rows(h), :] = acc[head_rows(h), half].astype(BF16)
            o_ref[block, LW:PIECES, :] = tail[:, half]


def attend(info, lens, table, queries, caches, fresh):
    with_fresh = fresh is not None
    operands = [info, lens, table, queries, *caches] + (list(fresh) if with_fresh else [])
    specs = [whole(SMEM)] * 3 + [whole()] + [whole(pl.ANY)] * 4
    specs += [whole()] * 2 if with_fresh else []

    def body(*refs):
        attention_kernel(with_fresh, *refs)

    return pl.pallas_call(
        body,
        out_shape=jax.ShapeDtypeStruct((4, PIECES, TOK), BF16),
        in_specs=specs,
        out_specs=whole(),
        scratch_shapes=[
            VMEM((2 * SLOTS, PT, LW), BF16),
            VMEM((2 * SLOTS, PT, LW), BF16),
            pltpu.SemaphoreType.DMA((2 * SLOTS, 2)),
            SMEM((2 * SLOTS,), jnp.int32),
            VMEM((LH, HS, 2 * TOK), BF16),
            VMEM((LW, 2 * TOK), F32),
            VMEM((2 * LH, 2 * TOK), F32),
        ],
        compiler_params=pltpu.CompilerParams(vmem_limit_bytes=24 << 20),
        cost_estimate=pl.CostEstimate(
            flops=8 * 2 * 2 * PT * LW * 256, transcendentals=8 * PT * 4 * 256,
            bytes_accessed=3 << 20,
        ),
        name="attend_fresh" if with_fresh else "attend",
    )(*operands)


def join(parts):
    read = []
    for part in parts:
        tail = part[LW:PIECES].astype(F32)
        read.append(tail[0:8] + tail[8:16] + tail[16:24])
    peak = read[0][0:LH]
    for value in read[1:]:
        peak = jnp.maximum(peak, value[0:LH])
    factors = [jnp.exp2((value[0:LH] - peak) * C2) for value in read]
    total = sum(value[LH : 2 * LH] * factor for value, factor in zip(read, factors))
    weighted = [
        sum(
            part[head_rows(h)].astype(F32) * factor[h : h + 1]
            for part, factor in zip(parts, factors)
        )
        for h in range(LH)
    ]
    return peak, total, weighted


def join_rows_kernel(a_ref, b_ref, c_ref, d_ref, *outs):
    for block, out in enumerate(outs):
        parts = [ref.at[block] for ref in (a_ref, b_ref, c_ref, d_ref)]
        peak, total, weighted = join(parts)
        for h in range(LH):
            out[head_rows(h), :] = weighted[h].astype(BF16)
        out[LW:PIECES, :] = stat_rows(jnp.concatenate([peak, total], axis=0))


def join_last_kernel(a_ref, b_ref, c_ref, d_ref, out):
    _, total, weighted = join([a_ref, b_ref, c_ref, d_ref])
    inverse = 1.0 / total
    for h in range(LH):
        out[:, head_rows(h)] = (weighted[h] * inverse[h : h + 1]).T.astype(BF16)


def join_rows(parts):
    return pl.pallas_call(
        join_rows_kernel,
        out_shape=tuple(jax.ShapeDtypeStruct((PIECES, TOK), BF16) for _ in range(4)),
        in_specs=[whole()] * 4,
        out_specs=tuple(whole() for _ in range(4)),
        name="join_rows",
    )(*parts)


def join_last(parts):
    return pl.pallas_call(
        join_last_kernel,
        out_shape=jax.ShapeDtypeStruct((TOK, LW), BF16),
        in_specs=[whole()] * 4,
        out_specs=whole(),
        name="join_last",
    )(*parts)


def dense_kernel(*refs):
    attention = refs[0:4]
    weights = refs[4:8]
    bias, hidden, branch, out = refs[8:]
    total = bias[...] + hidden[...].astype(F32) + branch[...].astype(F32)
    product = jnp.dot(attention[0][...], weights[0][...], preferred_element_type=F32)
    for a, w in zip(attention[1:], weights[1:]):
        product = product + jnp.dot(a[...], w[...], preferred_element_type=F32)
    out[...] = (product + total).astype(BF16)


def dense(attention, weights, bias, hidden, branch):
    width = 512
    column = lambda rows: pl.BlockSpec((rows, width), lambda i: (0, i))
    return pl.pallas_call(
        dense_kernel,
        grid=(COLS // width,),
        out_shape=jax.ShapeDtypeStruct((TOK, COLS), BF16),
        in_specs=[pl.BlockSpec((TOK, LW), lambda i: (0, 0))] * 4
        + [column(LW)] * 4
        + [column(1), column(TOK), column(TOK)],
        out_specs=column(TOK),
        compiler_params=pltpu.CompilerParams(vmem_limit_bytes=24 << 20),
        name="dense",
    )(*attention, *weights, bias, hidden, branch)


WROWS = 512


def qkv_kernel(info, x0, x1, x2, x3, gain, shift, weight, bias, out, wbuf, sems):
    head = info[4]
    per = COLS // WROWS
    chunks = []
    for s in range(4):
        origin = lax.bitwise_and(head - s, 3)
        for j in range(per):
            start = pl.multiple_of(origin * COLS + j * WROWS, WROWS)
            n = s * per + j
            chunks.append(
                pltpu.make_async_copy(weight.at[pl.ds(start, WROWS), :], wbuf.at[n], sems.at[n])
            )
    for copy in chunks:
        copy.start()
    blocks = (x0, x1, x2, x3)
    total = 0.0
    square = 0.0
    for block in blocks:
        value = block[...].astype(F32)
        total = total + jnp.sum(value, axis=1, keepdims=True)
        square = square + jnp.sum(value * value, axis=1, keepdims=True)
    mean = total / D
    variance = square / D - mean * mean
    scale = lax.rsqrt(variance + 1e-05)
    result = bias[...] + jnp.zeros((TOK, QW), F32)
    for s, block in enumerate(blocks):
        origin = lax.bitwise_and(head - s, 3)
        normed = (block[...].astype(F32) - mean) * scale * gain[pl.ds(origin, 1), :]
        normed = (normed + shift[pl.ds(origin, 1), :]).astype(BF16)
        for j in range(per):
            n = s * per + j
            chunks[n].wait()
            result = result + jnp.dot(
                normed[:, j * WROWS : (j + 1) * WROWS], wbuf[n], preferred_element_type=F32
            )
    out[...] = result.astype(BF16)


def project_qkv(info, blocks, gain, shift, weight, bias):
    return pl.pallas_call(
        qkv_kernel,
        out_shape=jax.ShapeDtypeStruct((TOK, QW), BF16),
        in_specs=[whole(SMEM)] + [whole()] * 6 + [whole(pl.ANY), whole()],
        out_specs=whole(),
        scratch_shapes=[
            VMEM((D // WROWS, WROWS, QW), BF16),
            pltpu.SemaphoreType.DMA((D // WROWS,)),
        ],
        compiler_params=pltpu.CompilerParams(vmem_limit_bytes=32 << 20),
        name="project_qkv",
    )(info, *blocks, gain, shift, weight, bias)


WINDOW = 256
FRESH_PAGES = GROUP // PT + 1


def patch_kernel(
    info, lens, table, new_ref, k_in, v_in, k_out, v_out, src, kbuf, vbuf, sems, slots, shifts, starts
):
    page = info[0]

    def loads(n, local, start):
        return (
            pltpu.make_async_copy(new_ref.at[pl.ds(start, WINDOW), :], src.at[n], sems.at[n, 0]),
            pltpu.make_async_copy(k_in.at[local], kbuf.at[n], sems.at[n, 1]),
            pltpu.make_async_copy(v_in.at[local], vbuf.at[n], sems.at[n, 2]),
        )

    def stores(n, local):
        return (
            pltpu.make_async_copy(kbuf.at[n], k_out.at[local], sems.at[n, 3]),
            pltpu.make_async_copy(vbuf.at[n], v_out.at[local], sems.at[n, 4]),
        )

    def scan_request(request, count):
        length = lens[request]
        first = lax.div(length, PT)
        last = lax.div(length + (GROUP - 1), PT)

        def scan(g, n):
            slot = table[request, g]
            here = lax.div(slot, SLOTS) == page

            @pl.when(here)
            def _():
                local = slot - page * SLOTS
                offset = g * PT - length
                exact = request * GROUP + jnp.maximum(offset, 0)
                start = jnp.minimum(lax.div(exact, 16) * 16, REQS * GROUP - WINDOW)
                start = pl.multiple_of(start, 16)
                slots[n] = local
                shifts[n] = request * GROUP + offset - start
                starts[n] = offset
                for copy in loads(n, local, start):
                    copy.start()

            return n + here.astype(jnp.int32)

        return lax.fori_loop(first, last + 1, scan, count)

    count = lax.fori_loop(0, REQS, scan_request, jnp.int32(0))
    pick_row = lax.broadcasted_iota(jnp.int32, (PT, WINDOW), 0)
    pick_col = lax.broadcasted_iota(jnp.int32, (PT, WINDOW), 1)
    token = lax.broadcasted_iota(jnp.int32, (PT, LW), 0)

    def update(n, carry):
        for copy in loads(n, 0, 0):
            copy.wait()
        pick = jnp.where(pick_col == pick_row + shifts[n], 1.0, 0.0).astype(BF16)
        index = token + starts[n]
        fresh = (index >= 0) & (index < GROUP)
        for buf, cols in ((kbuf, slice(0, LW)), (vbuf, slice(LW, 2 * LW))):
            moved = jnp.dot(pick, src[n, :, cols], preferred_element_type=F32)
            buf[n] = jnp.where(fresh, moved, buf[n].astype(F32)).astype(BF16)
        for copy in stores(n, slots[n]):
            copy.start()
        return carry

    def finish(n, carry):
        for copy in stores(n, 0):
            copy.wait()
        return carry

    lax.fori_loop(0, count, update, 0)
    lax.fori_loop(0, count, finish, 0)


def patch(info, lens, table, new, key_cache, value_cache):
    shape = jax.ShapeDtypeStruct(key_cache.shape, BF16)
    return pl.pallas_call(
        patch_kernel,
        out_shape=(shape, shape),
        in_specs=[whole(SMEM)] * 3 + [whole(pl.ANY)] * 3,
        out_specs=(whole(pl.ANY), whole(pl.ANY)),
        scratch_shapes=[
            VMEM((SLOTS, WINDOW, 2 * LW), BF16),
            VMEM((SLOTS, PT, LW), BF16),
            VMEM((SLOTS, PT, LW), BF16),
            pltpu.SemaphoreType.DMA((SLOTS, 5)),
            SMEM((SLOTS,), jnp.int32),
            SMEM((SLOTS,), jnp.int32),
            SMEM((SLOTS,), jnp.int32),
        ],
        input_output_aliases={4: 0, 5: 1},
        compiler_params=pltpu.CompilerParams(vmem_limit_bytes=32 << 20),
        name="patch",
    )(info, lens, table, new, key_cache, value_cache)


def plane_shift(dy, dx):
    return [
        (y * 8 + x * 2 + c, ((y + dy) % 4) * 8 + ((x + dx) % 4) * 2 + c)
        for y in range(4)
        for x in range(4)
        for c in range(2)
    ]


CORES = [(p, p ^ 1) for p in range(32)]


def head_shift(s):
    return [(i, (i + s) % 4) for i in range(4)]


def on_device(
    hidden,
    group_qkv,
    mlp_branch,
    key_cache,
    paged_value_cache,
    cache_lengths,
    page_table,
    dense_weight,
    dense_bias,
    norm_gain,
    norm_bias,
    qkv_weight,
    qkv_bias,
):
    page = lax.axis_index("page").astype(jnp.int32)
    head = lax.axis_index("head").astype(jnp.int32)
    y = page // 8
    x = (page // 2) % 4
    core = page % 2

    def info_for(row):
        return jnp.stack([page, row, x, core, head])

    length = lax.dynamic_index_in_dim(cache_lengths, page // 4, 0, keepdims=False)
    positions = length + (page % 4) * TOK + jnp.arange(TOK, dtype=jnp.int32)
    inverse = 1.0 / 10000.0 ** (jnp.arange(0, ROT, 2, dtype=F32) / ROT)
    angles = positions.astype(F32)[None, :] * inverse[:, None]
    queries, fresh = rotary(group_qkv, jnp.cos(angles), jnp.sin(angles))

    row_queries = [queries] + [
        lax.ppermute(queries, "page", plane_shift(0, s)) for s in range(1, 4)
    ]
    row_queries = jnp.stack(row_queries, axis=0)
    all_queries = [row_queries] + [
        lax.ppermute(row_queries, "page", plane_shift(s, 0)) for s in range(1, 4)
    ]

    other_keys = lax.ppermute(key_cache, "page", CORES)
    other_values = lax.ppermute(paged_value_cache, "page", CORES)
    other_fresh = lax.ppermute(fresh, "page", CORES)
    caches = (key_cache, paged_value_cache, other_keys, other_values)

    new_rows = lax.all_gather(fresh, "page", axis=0, tiled=True)

    weights = [
        lax.dynamic_slice_in_dim(dense_weight, ((head + s) % 4) * COLS, COLS, 1) for s in range(4)
    ]
    weights = weights[:1] + [
        lax.ppermute(weights[s], "head", head_shift(s)) for s in range(1, 4)
    ]

    partials = []
    for s in range(4):
        part = attend(
            info_for((y - s) % 4),
            cache_lengths,
            page_table,
            all_queries[s],
            caches,
            (fresh, other_fresh) if s == 0 else None,
        )
        partials.append(part if s == 0 else lax.ppermute(part, "page", plane_shift(-s, 0)))
    blocks = join_rows(partials)
    blocks = [blocks[0]] + [
        lax.ppermute(blocks[s], "page", plane_shift(0, -s)) for s in range(1, 4)
    ]
    attention = join_last(blocks)

    attention = [attention] + [
        lax.ppermute(attention, "head", head_shift(s)) for s in range(1, 4)
    ]
    share_bias = lax.dynamic_slice_in_dim(dense_bias, head * COLS, COLS, 0)[None, :]
    new_hidden = dense(attention, weights, share_bias, hidden, mlp_branch)

    streams = [new_hidden] + [
        lax.ppermute(new_hidden, "head", head_shift(s)) for s in range(1, 4)
    ]
    next_qkv = project_qkv(
        info_for(y),
        streams,
        norm_gain.reshape(4, COLS),
        norm_bias.reshape(4, COLS),
        qkv_weight,
        qkv_bias[None, :],
    )

    key_out, value_out = patch(
        info_for(y), cache_lengths, page_table, new_rows, key_cache, paged_value_cache
    )
    return (new_hidden, next_qkv, key_out, value_out)


def solution(mesh):
    in_specs = (
        P("page", "head"),
        P("page", "head"),
        P("page", "head"),
        P("page", None, "head"),
        P("page", None, "head"),
        P(),
        P(),
        P("head", None),
        P(),
        P(),
        P(),
        P(None, "head"),
        P("head"),
    )
    out_specs = (
        P("page", "head"),
        P("page", "head"),
        P("page", None, "head"),
        P("page", None, "head"),
    )
    return jax.shard_map(
        on_device, mesh=mesh, in_specs=in_specs, out_specs=out_specs, check_vma=False
    )
```

profile of v0, /device:TPU:24, one launch (start us, length us, event | category | flops | bytes accessed | tf_op | source)
XLA Modules:
  0.0 183.6 jit_solution(4878281664756454421)
XLA Ops:
  7.2 1.6 copy.23.refs_4_.k_in
  8.8 0.4 copy-done.16
  9.2 0.2 copy.24.refs_5_.v_in
  9.4 0.4 copy-done.15
  9.8 1.0 dynamic_slice.19
  11.5 0.7 multiply_sine_fusion
  12.2 2.0 %rotary.1 = (bf16[512,128]{1,0:T(8,128)(2,1)}, bf16[128,1024]{1,0:T(8,128)(2,1)}) custom-call(bf16[128,1536]{1,0:T(8,128)(2,1)} %x_ref.1, f32[16,128]{1,0:T(8,128)} %get-tuple-element.25.cos_ref, f32[16,128]{1,0:T(8,128)} %get-tuple-element.24.sin_ref), custom_call_target="tpu_custom_call" | custom-call | tf_op jit(solution)/shard_map/rotary/pallas_call | solution.py:62
  14.2 0.1 collective-permute-start.3
  14.3 0.5 collective-permute-start.4
  14.8 1.5 collective-permute-start
  16.3 2.7 %collective-permute-start.1 = (bf16[512,128]{1,0:T(8,128)(2,1)}, bf16[512,128]{1,0:T(8,128)(2,1)S(1)}, u32[]{:S(2)}, u32[]{:S(2)}) collective-permute-start(bf16[512,128]{1,0:T(8,128)(2,1)} %get-tuple-element.12), channel_id=1, source_target_pairs={{0,4},{1,5},{2,6},{3,7},{4,0},{5,1},{6,2},{7,3},{8,12},{9,13},{10,... | collective-permute-start | bytes 393224 | tf_op jit(solution)/shard_map/ppermute | solution.py:520
  19.0 1.4 collective-permute-start.2
  20.5 1.3 collective-permute-done
  21.7 3.8 %collective-permute-done.1 = bf16[512,128]{1,0:T(8,128)(2,1)S(1)} collective-permute-done((bf16[512,128]{1,0:T(8,128)(2,1)}, bf16[512,128]{1,0:T(8,128)(2,1)S(1)}, u32[]{:S(2)}, u32[]{:S(2)}) %collective-permute-start.1) | collective-permute-done | bytes 131104 | tf_op jit(solution)/shard_map/ppermute | solution.py:520
  25.5 1.8 pad_maximum_fusion.refs_3_
  27.3 0.7 collective-permute-start.10
  28.1 0.9 collective-permute-start.8
  29.0 2.2 %collective-permute-start.6 = (bf16[4,512,128]{2,1,0:T(8,128)(2,1)}, bf16[4,512,128]{2,1,0:T(8,128)(2,1)}, u32[]{:S(2)}, u32[]{:S(2)}) collective-permute-start(bf16[4,512,128]{2,1,0:T(8,128)(2,1)} %pad_maximum_fusion.refs_3_), channel_id=1, source_target_pairs={{0,8},{1,9},{2,10},{3,11},{4,12},{5,13},{6,14},{7,15},{8,16},{9,17... | collective-permute-start | bytes 1572872 | tf_op jit(solution)/shard_map/ppermute | solution.py:524
  31.3 13.2 %collective-permute-done.10.refs_3_ = bf16[4,512,128]{2,1,0:T(8,128)(2,1)} collective-permute-done((bf16[4,512,128]{2,1,0:T(8,128)(2,1)}, bf16[4,512,128]{2,1,0:T(8,128)(2,1)}, u32[]{:S(2)}, u32[]{:S(2)}) %collective-permute-start.10) | collective-permute-done | bytes 524320 | tf_op jit(solution)/shard_map/ppermute | solution.py:524
  44.5 4.0 %attend.5 = bf16[4,544,128]{2,1,0:T(8,128)(2,1)} custom-call(s32[5]{0:T(128)S(1)} %stack.95.refs_0_, s32[8]{0:T(128)S(1)} %copy-done.15, s32[8,36]{1,0:T(8,128)S(1)} %copy-done.14, bf16[4,512,128]{2,1,0:T(8,128)(2,1)} %collective-permute-done.10.refs_3_, bf16[13,128,512]{2,1,0:T(8,128)(2,1)S(1)} %copy.23.refs_4_.k_in, ...), custom_call_target="tpu_custom_call" | custom-call | flops 536870912 | bytes 3145728 | tf_op jit(solution)/shard_map/attend/pallas_call | solution.py:214
  48.5 0.1 collective-permute-start.5
  48.7 4.3 %constant_dynamic-slice_fusion = (bf16[512,1024]{1,0:T(8,128)(2,1)}, bf16[512,1024]{1,0:T(8,128)(2,1)}, bf16[512,1024]{1,0:T(8,128)(2,1)}, bf16[512,1024]{1,0:T(8,128)(2,1)}) fusion(bf16[512,4096]{1,0:T(8,128)(2,1)} %param.20, s32[]{:T(128)S(6)} %select_n.94, s32[]{:T(128)S(6)} %select_n.90, s32[]{:T(128)S(6)} %select_n.88, s32[]{:T(128)S(6)} %select_n.92), kind=kLoop, calls=%fused_computation.3 | loop fusion | bytes 8388624 | tf_op jit(solution)/shard_map/dynamic_slice | solution.py:535
  53.0 2.1 %collective-permute-start.18 = (bf16[512,1024]{1,0:T(8,128)(2,1)}, bf16[512,1024]{1,0:T(8,128)(2,1)}, u32[]{:S(2)}, u32[]{:S(2)}) collective-permute-start(bf16[512,1024]{1,0:T(8,128)(2,1)} %get-tuple-element.21), channel_id=1, source_target_pairs={{0,32},{32,64},{64,96},{96,0},{1,33},{33,65},{65,97},{97,1},{2,34}... | collective-permute-start | bytes 3145736 | tf_op jit(solution)/shard_map/ppermute | solution.py:538
  55.2 0.7 collective-permute-done.8.refs_3_
  55.9 14.3 %collective-permute-start.19 = (bf16[512,1024]{1,0:T(8,128)(2,1)}, bf16[512,1024]{1,0:T(8,128)(2,1)}, u32[]{:S(2)}, u32[]{:S(2)}) collective-permute-start(bf16[512,1024]{1,0:T(8,128)(2,1)} %get-tuple-element.23), channel_id=1, source_target_pairs={{0,64},{32,96},{64,0},{96,32},{1,65},{33,97},{65,1},{97,33},{2,66}... | collective-permute-start | bytes 3145736 | tf_op jit(solution)/shard_map/ppermute | solution.py:538
  70.3 1.0 collective-permute-start.20
  71.3 2.7 %attend.4 = bf16[4,544,128]{2,1,0:T(8,128)(2,1)} custom-call(s32[5]{0:T(128)S(1)} %stack.93.refs_0_, s32[8]{0:T(128)S(1)} %copy-done.15, s32[8,36]{1,0:T(8,128)S(1)} %copy-done.14, bf16[4,512,128]{2,1,0:T(8,128)(2,1)} %collective-permute-done.8.refs_3_, bf16[13,128,512]{2,1,0:T(8,128)(2,1)S(1)} %copy.23.refs_4_.k_in, ...), custom_call_target="tpu_custom_call" | custom-call | flops 536870912 | bytes 3145728 | tf_op jit(solution)/shard_map/attend/pallas_call | solution.py:214
  73.9 4.3 %attend.3 = bf16[4,544,128]{2,1,0:T(8,128)(2,1)} custom-call(s32[5]{0:T(128)S(1)} %stack.91.refs_0_, s32[8]{0:T(128)S(1)} %copy-done.15, s32[8,36]{1,0:T(8,128)S(1)} %copy-done.14, bf16[4,512,128]{2,1,0:T(8,128)(2,1)} %collective-permute-done.6.refs_3_, bf16[13,128,512]{2,1,0:T(8,128)(2,1)S(1)} %copy.23.refs_4_.k_in, ...), custom_call_target="tpu_custom_call" | custom-call | flops 536870912 | bytes 3145728 | tf_op jit(solution)/shard_map/attend/pallas_call | solution.py:214
  78.4 4.5 %collective-permute-start.7 = (bf16[4,544,128]{2,1,0:T(8,128)(2,1)}, bf16[4,544,128]{2,1,0:T(8,128)(2,1)}, u32[]{:S(2)}, u32[]{:S(2)}) collective-permute-start(bf16[4,544,128]{2,1,0:T(8,128)(2,1)} %attend.3), channel_id=1, source_target_pairs={{0,24},{1,25},{2,26},{3,27},{4,28},{5,29},{6,30},{7,31},{8,0},{9,1... | collective-permute-start | bytes 1671176 | tf_op jit(solution)/shard_map/ppermute | solution.py:551
  82.9 4.8 %attend_fresh.1.a_ref = bf16[4,544,128]{2,1,0:T(8,128)(2,1)S(1)} custom-call(s32[5]{0:T(128)S(1)} %stack.84.refs_0_, s32[8]{0:T(128)S(1)} %copy-done.15, s32[8,36]{1,0:T(8,128)S(1)} %copy-done.14, bf16[4,512,128]{2,1,0:T(8,128)(2,1)} %pad_maximum_fusion.refs_3_, bf16[13,128,512]{2,1,0:T(8,128)(2,1)S(1)} %copy.23.refs_4_.k_in, ...), custom_call_target="tpu_custom_call" | custom-call | flops 536870912 | bytes 3145728 | tf_op jit(solution)/shard_map/attend_fresh/pallas_call | solution.py:214
  87.8 0.8 copy-done.5
  88.6 7.6 %collective-permute-done.9.c_ref = bf16[4,544,128]{2,1,0:T(8,128)(2,1)} collective-permute-done((bf16[4,544,128]{2,1,0:T(8,128)(2,1)}, bf16[4,544,128]{2,1,0:T(8,128)(2,1)}, u32[]{:S(2)}, u32[]{:S(2)}) %collective-permute-start.9) | collective-permute-done | bytes 557088 | tf_op jit(solution)/shard_map/ppermute | solution.py:551
  96.1 12.9 %collective-permute-done.7.b_ref = bf16[4,544,128]{2,1,0:T(8,128)(2,1)} collective-permute-done((bf16[4,544,128]{2,1,0:T(8,128)(2,1)}, bf16[4,544,128]{2,1,0:T(8,128)(2,1)}, u32[]{:S(2)}, u32[]{:S(2)}) %collective-permute-start.7) | collective-permute-done | bytes 557088 | tf_op jit(solution)/shard_map/ppermute | solution.py:551
  109.0 2.7 %join_rows.1 = (bf16[544,128]{1,0:T(8,128)(2,1)}, bf16[544,128]{1,0:T(8,128)(2,1)}, bf16[544,128]{1,0:T(8,128)(2,1)}, bf16[544,128]{1,0:T(8,128)(2,1)}) custom-call(bf16[4,544,128]{2,1,0:T(8,128)(2,1)} %copy-done.5, bf16[4,544,128]{2,1,0:T(8,128)(2,1)} %collective-permute-done.7.b_ref, bf16[4,544,128]{2,1,0:T(8,128)(2,1)} %collective-permute-done.9.c_ref, ...), custom_call_target="tpu_custom_call" | custom-call | tf_op jit(solution)/shard_map/join_rows/pallas_call | solution.py:274
  111.7 2.2 %collective-permute-start.12 = (bf16[544,128]{1,0:T(8,128)(2,1)}, bf16[544,128]{1,0:T(8,128)(2,1)S(1)}, u32[]{:S(2)}, u32[]{:S(2)}) collective-permute-start(bf16[544,128]{1,0:T(8,128)(2,1)} %get-tuple-element.15), channel_id=1, source_target_pairs={{0,6},{1,7},{2,0},{3,1},{4,2},{5,3},{6,4},{7,5},{8,14},{9,15},{10,... | collective-permute-start | bytes 417800 | tf_op jit(solution)/shard_map/ppermute | solution.py:554
  113.9 1.3 collective-permute-start.13
  115.2 5.1 %collective-permute-done.12.b_ref = bf16[544,128]{1,0:T(8,128)(2,1)S(1)} collective-permute-done((bf16[544,128]{1,0:T(8,128)(2,1)}, bf16[544,128]{1,0:T(8,128)(2,1)S(1)}, u32[]{:S(2)}, u32[]{:S(2)}) %collective-permute-start.12) | collective-permute-done | bytes 139296 | tf_op jit(solution)/shard_map/ppermute | solution.py:554
  120.2 0.6 collective-permute-done.13.c_ref
  120.8 6.2 %collective-permute-done.14.d_ref = bf16[544,128]{1,0:T(8,128)(2,1)S(1)} collective-permute-done((bf16[544,128]{1,0:T(8,128)(2,1)}, bf16[544,128]{1,0:T(8,128)(2,1)S(1)}, u32[]{:S(2)}, u32[]{:S(2)}) %collective-permute-start.14) | collective-permute-done | bytes 139296 | tf_op jit(solution)/shard_map/ppermute | solution.py:554
  127.0 0.7 copy-done.19
  127.7 2.0 %join_last.1.refs_0_ = bf16[128,512]{1,0:T(8,128)(2,1)} custom-call(bf16[544,128]{1,0:T(8,128)(2,1)} %get-tuple-element.14.a_ref, bf16[544,128]{1,0:T(8,128)(2,1)} %copy-done.17, bf16[544,128]{1,0:T(8,128)(2,1)} %copy-done.18, bf16[544,128]{1,0:T(8,128)(2,1)} %copy-done.19), custom_call_target="tpu_custom_call" | custom-call | tf_op jit(solution)/shard_map/join_last/pallas_call | solution.py:284
  129.6 1.8 collective-permute-start.15
  131.5 3.2 %collective-permute-start.16 = (bf16[128,512]{1,0:T(8,128)(2,1)}, bf16[128,512]{1,0:T(8,128)(2,1)S(1)}, u32[]{:S(2)}, u32[]{:S(2)}) collective-permute-start(bf16[128,512]{1,0:T(8,128)(2,1)} %join_last.1.refs_0_), channel_id=1, source_target_pairs={{0,64},{32,96},{64,0},{96,32},{1,65},{33,97},{65,1},{97,33},{2,66}... | collective-permute-start | bytes 393224 | tf_op jit(solution)/shard_map/ppermute | solution.py:559
  134.7 1.2 collective-permute-start.17
  135.9 0.7 dynamic_slice.24
  136.6 1.2 collective-permute-done.15.refs_1_
  137.8 1.5 collective-permute-done.16.refs_2_
  139.2 0.7 copy-done.10
  139.9 0.7 copy-done.12
  140.6 0.9 copy-done.7
  141.5 0.9 copy-done.9
  142.4 0.9 copy-done.11
  143.3 0.9 copy-done.13
  144.2 3.0 %dense.1.x0 = bf16[128,1024]{1,0:T(8,128)(2,1)} custom-call(bf16[128,512]{1,0:T(8,128)(2,1)S(1)} %copy-done.7, bf16[128,512]{1,0:T(8,128)(2,1)S(1)} %collective-permute-done.15.refs_1_, bf16[128,512]{1,0:T(8,128)(2,1)S(1)} %copy-done.11, bf16[128,512]{1,0:T(8,128)(2,1)S(1)} %copy-done.13, bf16[512,1024]{1,0:T(8,128)(2,1)S(1)} %copy-done.4, ...), custom_call_target="tpu_custom_call" | custom-call | tf_op jit(solution)/shard_map/dense/pallas_call | solution.py:307
  147.2 0.8 collective-permute-start.21
  148.0 3.1 %collective-permute-start.22 = (bf16[128,1024]{1,0:T(8,128)(2,1)}, bf16[128,1024]{1,0:T(8,128)(2,1)S(1)}, u32[]{:S(2)}, u32[]{:S(2)}) collective-permute-start(bf16[128,1024]{1,0:T(8,128)(2,1)} %dense.1.x0), channel_id=1, source_target_pairs={{0,64},{32,96},{64,0},{96,32},{1,65},{33,97},{65,1},{97,33},{2,66}... | collective-permute-start | bytes 786440 | tf_op jit(solution)/shard_map/ppermute | solution.py:565
  151.1 0.9 collective-permute-start.23
  152.1 5.5 %collective-permute-done.21.x1 = bf16[128,1024]{1,0:T(8,128)(2,1)S(1)} collective-permute-done((bf16[128,1024]{1,0:T(8,128)(2,1)}, bf16[128,1024]{1,0:T(8,128)(2,1)S(1)}, u32[]{:S(2)}, u32[]{:S(2)}) %collective-permute-start.21) | collective-permute-done | bytes 262176 | tf_op jit(solution)/shard_map/ppermute | solution.py:565
  157.7 2.8 %collective-permute-done.22.x2 = bf16[128,1024]{1,0:T(8,128)(2,1)S(1)} collective-permute-done((bf16[128,1024]{1,0:T(8,128)(2,1)}, bf16[128,1024]{1,0:T(8,128)(2,1)S(1)}, u32[]{:S(2)}, u32[]{:S(2)}) %collective-permute-start.22) | collective-permute-done | bytes 262176 | tf_op jit(solution)/shard_map/ppermute | solution.py:565
  160.5 4.6 %copy-done.2 = bf16[4096,1536]{1,0:T(8,128)(2,1)S(1)} copy-done((bf16[4096,1536]{1,0:T(8,128)(2,1)S(1)}, bf16[4096,1536]{1,0:T(8,128)(2,1)}, u32[]{:S(2)}) %copy-start.2) | copy-done | bytes 12582936
  165.1 0.9 copy-done.6
  166.0 5.2 %project_qkv.1 = bf16[128,1536]{1,0:T(8,128)(2,1)} custom-call(s32[5]{0:T(128)S(1)} %stack.97.info, bf16[128,1024]{1,0:T(8,128)(2,1)S(1)} %copy-done.6, bf16[128,1024]{1,0:T(8,128)(2,1)S(1)} %collective-permute-done.21.x1, bf16[128,1024]{1,0:T(8,128)(2,1)S(1)} %collective-permute-done.22.x2, bf16[128,1024]{1,0:T(8,128)(2,1)S(1)} %collective-permute-done.23.x3, ...), custom_call_target="tpu_custom_call" | custom-call | tf_op jit(solution)/shard_map/project_qkv/pallas_call | solution.py:362
  171.3 3.4 %copy-done.3 = bf16[4096,1024]{1,0:T(8,128)(2,1)S(1)} copy-done((bf16[4096,1024]{1,0:T(8,128)(2,1)S(1)}, bf16[4096,1024]{1,0:T(8,128)(2,1)}, u32[]{:S(2)}) %copy-start.3) | copy-done | bytes 8388632
  174.6 2.1 %patch.1 = (bf16[13,128,512]{2,1,0:T(8,128)(2,1)}, bf16[13,128,512]{2,1,0:T(8,128)(2,1)}) custom-call(s32[5]{0:T(128)S(1)} %stack.97.info, s32[8]{0:T(128)S(1)} %copy-done.15, s32[8,36]{1,0:T(8,128)S(1)} %copy-done.14, bf16[4096,1024]{1,0:T(8,128)(2,1)S(1)} %copy-done.3, ...), custom_call_target="tpu_custom_call", output_to_operand_aliasing={{0}: (4, {}), {1}: (5, {})} | custom-call | tf_op jit(solution)/shard_map/patch/pallas_call | solution.py:453
  (60 shorter events, 0.8 us)
Async XLA Ops:
  7.2 164.1 %all-gather.2.cloned.1.call-start = ((), (), s32[]{:S(2)}) async-start(), calls=%async_computation | async-start | bytes 8650752 | tf_op jit(solution)/shard_map/all_gather | solution.py:532
  7.2 2.0 %copy-start.16 = (bf16[13,128,512]{2,1,0:T(8,128)(2,1)S(1)}, bf16[13,128,512]{2,1,0:T(8,128)(2,1)}, u32[]{:S(2)}) copy-start(bf16[13,128,512]{2,1,0:T(8,128)(2,1)} %param.17) | copy-start | bytes 5111812
  9.2 73.7 %copy-start = (bf16[13,128,512]{2,1,0:T(8,128)(2,1)}, bf16[13,128,512]{2,1,0:T(8,128)(2,1)S(1)}, u32[]{:S(2)}) copy-start(bf16[13,128,512]{2,1,0:T(8,128)(2,1)S(1)} %copy.23.refs_4_.k_in) | copy-start | bytes 5111812
  9.2 0.7 copy-start.15
  9.4 73.6 %copy-start.1 = (bf16[13,128,512]{2,1,0:T(8,128)(2,1)}, bf16[13,128,512]{2,1,0:T(8,128)(2,1)S(1)}, u32[]{:S(2)}) copy-start(bf16[13,128,512]{2,1,0:T(8,128)(2,1)S(1)} %copy.24.refs_5_.v_in) | copy-start | bytes 5111812
  9.4 35.1 %copy-start.14 = (s32[8,36]{1,0:T(8,128)S(1)}, s32[8,36]{1,0:T(8,128)}, u32[]{:S(2)}) copy-start(s32[8,36]{1,0:T(8,128)} %table.1) | copy-start | bytes 3460
  14.2 30.2 %collective-permute-start.3 = (bf16[13,128,512]{2,1,0:T(8,128)(2,1)S(1)}, bf16[13,128,512]{2,1,0:T(8,128)(2,1)}, u32[]{:S(2)}, u32[]{:S(2)}) collective-permute-start(bf16[13,128,512]{2,1,0:T(8,128)(2,1)S(1)} %copy.23.refs_4_.k_in), channel_id=1, source_target_pairs={{0,1},{1,0},{2,3},{3,2},{4,5},{5,4},{6,7},{7,6},{8,9},{9,8},{10,11... | collective-permute-start | bytes 5111816 | tf_op jit(solution)/shard_map/ppermute | solution.py:527
  14.3 30.1 %collective-permute-start.4 = (bf16[13,128,512]{2,1,0:T(8,128)(2,1)S(1)}, bf16[13,128,512]{2,1,0:T(8,128)(2,1)}, u32[]{:S(2)}, u32[]{:S(2)}) collective-permute-start(bf16[13,128,512]{2,1,0:T(8,128)(2,1)S(1)} %copy.24.refs_5_.v_in), channel_id=1, source_target_pairs={{0,1},{1,0},{2,3},{3,2},{4,5},{5,4},{6,7},{7,6},{8,9},{9,8},{10,11... | collective-permute-start | bytes 5111816 | tf_op jit(solution)/shard_map/ppermute | solution.py:528
  14.8 6.9 %collective-permute-start = (bf16[512,128]{1,0:T(8,128)(2,1)}, bf16[512,128]{1,0:T(8,128)(2,1)S(1)}, u32[]{:S(2)}, u32[]{:S(2)}) collective-permute-start(bf16[512,128]{1,0:T(8,128)(2,1)} %get-tuple-element.12), channel_id=1, source_target_pairs={{0,2},{1,3},{2,4},{3,5},{4,6},{5,7},{6,0},{7,1},{8,10},{9,11},{10,... | collective-permute-start | bytes 393224 | tf_op jit(solution)/shard_map/ppermute | solution.py:520
  16.3 9.2 %collective-permute-start.1 = (bf16[512,128]{1,0:T(8,128)(2,1)}, bf16[512,128]{1,0:T(8,128)(2,1)S(1)}, u32[]{:S(2)}, u32[]{:S(2)}) collective-permute-start(bf16[512,128]{1,0:T(8,128)(2,1)} %get-tuple-element.12), channel_id=1, source_target_pairs={{0,4},{1,5},{2,6},{3,7},{4,0},{5,1},{6,2},{7,3},{8,12},{9,13},{10,... | collective-permute-start | bytes 393224 | tf_op jit(solution)/shard_map/ppermute | solution.py:520
  19.0 6.5 %collective-permute-start.2 = (bf16[512,128]{1,0:T(8,128)(2,1)}, bf16[512,128]{1,0:T(8,128)(2,1)S(1)}, u32[]{:S(2)}, u32[]{:S(2)}) collective-permute-start(bf16[512,128]{1,0:T(8,128)(2,1)} %get-tuple-element.12), channel_id=1, source_target_pairs={{0,6},{1,7},{2,0},{3,1},{4,2},{5,3},{6,4},{7,5},{8,14},{9,15},{10,... | collective-permute-start | bytes 393224 | tf_op jit(solution)/shard_map/ppermute | solution.py:520
  27.3 17.1 %collective-permute-start.10 = (bf16[4,512,128]{2,1,0:T(8,128)(2,1)}, bf16[4,512,128]{2,1,0:T(8,128)(2,1)}, u32[]{:S(2)}, u32[]{:S(2)}) collective-permute-start(bf16[4,512,128]{2,1,0:T(8,128)(2,1)} %pad_maximum_fusion.refs_3_), channel_id=1, source_target_pairs={{0,24},{1,25},{2,26},{3,27},{4,28},{5,29},{6,30},{7,31},{8,0},{9,1... | collective-permute-start | bytes 1572872 | tf_op jit(solution)/shard_map/ppermute | solution.py:524
  28.1 27.9 %collective-permute-start.8 = (bf16[4,512,128]{2,1,0:T(8,128)(2,1)}, bf16[4,512,128]{2,1,0:T(8,128)(2,1)}, u32[]{:S(2)}, u32[]{:S(2)}) collective-permute-start(bf16[4,512,128]{2,1,0:T(8,128)(2,1)} %pad_maximum_fusion.refs_3_), channel_id=1, source_target_pairs={{0,16},{1,17},{2,18},{3,19},{4,20},{5,21},{6,22},{7,23},{8,24},{9,... | collective-permute-start | bytes 1572872 | tf_op jit(solution)/shard_map/ppermute | solution.py:524
  29.0 41.3 %collective-permute-start.6 = (bf16[4,512,128]{2,1,0:T(8,128)(2,1)}, bf16[4,512,128]{2,1,0:T(8,128)(2,1)}, u32[]{:S(2)}, u32[]{:S(2)}) collective-permute-start(bf16[4,512,128]{2,1,0:T(8,128)(2,1)} %pad_maximum_fusion.refs_3_), channel_id=1, source_target_pairs={{0,8},{1,9},{2,10},{3,11},{4,12},{5,13},{6,14},{7,15},{8,16},{9,17... | collective-permute-start | bytes 1572872 | tf_op jit(solution)/shard_map/ppermute | solution.py:524
  48.4 29.9 %collective-permute-start.11 = (bf16[4,544,128]{2,1,0:T(8,128)(2,1)}, bf16[4,544,128]{2,1,0:T(8,128)(2,1)}, u32[]{:S(2)}, u32[]{:S(2)}) collective-permute-start(bf16[4,544,128]{2,1,0:T(8,128)(2,1)} %attend.5), channel_id=1, source_target_pairs={{0,8},{1,9},{2,10},{3,11},{4,12},{5,13},{6,14},{7,15},{8,16},{9,17... | collective-permute-start | bytes 1671176 | tf_op jit(solution)/shard_map/ppermute | solution.py:551
  48.5 29.7 %collective-permute-start.5 = (bf16[128,1024]{1,0:T(8,128)(2,1)}, bf16[128,1024]{1,0:T(8,128)(2,1)}, u32[]{:S(2)}, u32[]{:S(2)}) collective-permute-start(bf16[128,1024]{1,0:T(8,128)(2,1)} %get-tuple-element.13.refs_8_), channel_id=1, source_target_pairs={{0,1},{1,0},{2,3},{3,2},{4,5},{5,4},{6,7},{7,6},{8,9},{9,8},{10,11... | collective-permute-start | bytes 786440 | tf_op jit(solution)/shard_map/ppermute | solution.py:529
  53.0 81.7 %collective-permute-start.18 = (bf16[512,1024]{1,0:T(8,128)(2,1)}, bf16[512,1024]{1,0:T(8,128)(2,1)}, u32[]{:S(2)}, u32[]{:S(2)}) collective-permute-start(bf16[512,1024]{1,0:T(8,128)(2,1)} %get-tuple-element.21), channel_id=1, source_target_pairs={{0,32},{32,64},{64,96},{96,0},{1,33},{33,65},{65,97},{97,1},{2,34}... | collective-permute-start | bytes 3145736 | tf_op jit(solution)/shard_map/ppermute | solution.py:538
  55.9 80.6 %collective-permute-start.19 = (bf16[512,1024]{1,0:T(8,128)(2,1)}, bf16[512,1024]{1,0:T(8,128)(2,1)}, u32[]{:S(2)}, u32[]{:S(2)}) collective-permute-start(bf16[512,1024]{1,0:T(8,128)(2,1)} %get-tuple-element.23), channel_id=1, source_target_pairs={{0,64},{32,96},{64,0},{96,32},{1,65},{33,97},{65,1},{97,33},{2,66}... | collective-permute-start | bytes 3145736 | tf_op jit(solution)/shard_map/ppermute | solution.py:538
  70.3 66.3 %collective-permute-start.20 = (bf16[512,1024]{1,0:T(8,128)(2,1)}, bf16[512,1024]{1,0:T(8,128)(2,1)}, u32[]{:S(2)}, u32[]{:S(2)}) collective-permute-start(bf16[512,1024]{1,0:T(8,128)(2,1)} %get-tuple-element.20), channel_id=1, source_target_pairs={{0,96},{32,0},{64,32},{96,64},{1,97},{33,1},{65,33},{97,65},{2,98}... | collective-permute-start | bytes 3145736 | tf_op jit(solution)/shard_map/ppermute | solution.py:538
  78.2 17.9 %collective-permute-start.9 = (bf16[4,544,128]{2,1,0:T(8,128)(2,1)}, bf16[4,544,128]{2,1,0:T(8,128)(2,1)}, u32[]{:S(2)}, u32[]{:S(2)}) collective-permute-start(bf16[4,544,128]{2,1,0:T(8,128)(2,1)} %attend.4), channel_id=1, source_target_pairs={{0,16},{1,17},{2,18},{3,19},{4,20},{5,21},{6,22},{7,23},{8,24},{9,... | collective-permute-start | bytes 1671176 | tf_op jit(solution)/shard_map/ppermute | solution.py:551
  78.4 30.7 %collective-permute-start.7 = (bf16[4,544,128]{2,1,0:T(8,128)(2,1)}, bf16[4,544,128]{2,1,0:T(8,128)(2,1)}, u32[]{:S(2)}, u32[]{:S(2)}) collective-permute-start(bf16[4,544,128]{2,1,0:T(8,128)(2,1)} %attend.3), channel_id=1, source_target_pairs={{0,24},{1,25},{2,26},{3,27},{4,28},{5,29},{6,30},{7,31},{8,0},{9,1... | collective-permute-start | bytes 1671176 | tf_op jit(solution)/shard_map/ppermute | solution.py:551
  87.8 0.8 copy-start.5
  88.6 52.0 %copy-start.4 = (bf16[512,1024]{1,0:T(8,128)(2,1)S(1)}, bf16[512,1024]{1,0:T(8,128)(2,1)}, u32[]{:S(2)}) copy-start(bf16[512,1024]{1,0:T(8,128)(2,1)} %get-tuple-element.22.refs_4_) | copy-start | bytes 3145732
  88.6 52.0 %copy-start.8 = (bf16[128,1024]{1,0:T(8,128)(2,1)S(1)}, bf16[128,1024]{1,0:T(8,128)(2,1)}, u32[]{:S(2)}) copy-start(bf16[128,1024]{1,0:T(8,128)(2,1)} %refs_9_.1) | copy-start | bytes 786436
  111.7 8.5 %collective-permute-start.12 = (bf16[544,128]{1,0:T(8,128)(2,1)}, bf16[544,128]{1,0:T(8,128)(2,1)S(1)}, u32[]{:S(2)}, u32[]{:S(2)}) collective-permute-start(bf16[544,128]{1,0:T(8,128)(2,1)} %get-tuple-element.15), channel_id=1, source_target_pairs={{0,6},{1,7},{2,0},{3,1},{4,2},{5,3},{6,4},{7,5},{8,14},{9,15},{10,... | collective-permute-start | bytes 417800 | tf_op jit(solution)/shard_map/ppermute | solution.py:554
  113.9 6.9 %collective-permute-start.13 = (bf16[544,128]{1,0:T(8,128)(2,1)}, bf16[544,128]{1,0:T(8,128)(2,1)S(1)}, u32[]{:S(2)}, u32[]{:S(2)}) collective-permute-start(bf16[544,128]{1,0:T(8,128)(2,1)} %get-tuple-element.16), channel_id=1, source_target_pairs={{0,4},{1,5},{2,6},{3,7},{4,0},{5,1},{6,2},{7,3},{8,12},{9,13},{10,... | collective-permute-start | bytes 417800 | tf_op jit(solution)/shard_map/ppermute | solution.py:554
  120.2 6.8 %copy-start.17 = (bf16[544,128]{1,0:T(8,128)(2,1)}, bf16[544,128]{1,0:T(8,128)(2,1)S(1)}, u32[]{:S(2)}) copy-start(bf16[544,128]{1,0:T(8,128)(2,1)S(1)} %collective-permute-done.12.b_ref) | copy-start | bytes 417796
  120.2 6.8 %collective-permute-start.14 = (bf16[544,128]{1,0:T(8,128)(2,1)}, bf16[544,128]{1,0:T(8,128)(2,1)S(1)}, u32[]{:S(2)}, u32[]{:S(2)}) collective-permute-start(bf16[544,128]{1,0:T(8,128)(2,1)} %get-tuple-element.17), channel_id=1, source_target_pairs={{0,2},{1,3},{2,4},{3,5},{4,6},{5,7},{6,0},{7,1},{8,10},{9,11},{10,... | collective-permute-start | bytes 417800 | tf_op jit(solution)/shard_map/ppermute | solution.py:554
  120.8 6.2 %copy-start.18 = (bf16[544,128]{1,0:T(8,128)(2,1)}, bf16[544,128]{1,0:T(8,128)(2,1)S(1)}, u32[]{:S(2)}) copy-start(bf16[544,128]{1,0:T(8,128)(2,1)S(1)} %collective-permute-done.13.c_ref) | copy-start | bytes 417796
  127.0 0.7 copy-start.19
  129.6 8.1 %collective-permute-start.15 = (bf16[128,512]{1,0:T(8,128)(2,1)}, bf16[128,512]{1,0:T(8,128)(2,1)S(1)}, u32[]{:S(2)}, u32[]{:S(2)}) collective-permute-start(bf16[128,512]{1,0:T(8,128)(2,1)} %join_last.1.refs_0_), channel_id=1, source_target_pairs={{0,32},{32,64},{64,96},{96,0},{1,33},{33,65},{65,97},{97,1},{2,34}... | collective-permute-start | bytes 393224 | tf_op jit(solution)/shard_map/ppermute | solution.py:559
  131.5 7.8 %collective-permute-start.16 = (bf16[128,512]{1,0:T(8,128)(2,1)}, bf16[128,512]{1,0:T(8,128)(2,1)S(1)}, u32[]{:S(2)}, u32[]{:S(2)}) collective-permute-start(bf16[128,512]{1,0:T(8,128)(2,1)} %join_last.1.refs_0_), channel_id=1, source_target_pairs={{0,64},{32,96},{64,0},{96,32},{1,65},{33,97},{65,1},{97,33},{2,66}... | collective-permute-start | bytes 393224 | tf_op jit(solution)/shard_map/ppermute | solution.py:559
  134.7 5.2 %collective-permute-start.17 = (bf16[128,512]{1,0:T(8,128)(2,1)}, bf16[128,512]{1,0:T(8,128)(2,1)S(1)}, u32[]{:S(2)}, u32[]{:S(2)}) collective-permute-start(bf16[128,512]{1,0:T(8,128)(2,1)} %join_last.1.refs_0_), channel_id=1, source_target_pairs={{0,96},{32,0},{64,32},{96,64},{1,97},{33,1},{65,33},{97,65},{2,98}... | collective-permute-start | bytes 393224 | tf_op jit(solution)/shard_map/ppermute | solution.py:559
  139.2 0.7 copy-start.10
  139.9 0.7 copy-start.12
  140.6 0.9 copy-start.7
  141.5 0.9 copy-start.9
  142.4 0.9 copy-start.11
  143.3 0.9 copy-start.13
  144.2 7.9 %copy-start.20 = (f32[4096]{0:T(1024)S(1)}, f32[4096]{0:T(1024)}, u32[]{:S(2)}) copy-start(f32[4096]{0:T(1024)} %param.22) | copy-start | bytes 49156
  144.2 7.9 %copy-start.21 = (f32[4096]{0:T(1024)S(1)}, f32[4096]{0:T(1024)}, u32[]{:S(2)}) copy-start(f32[4096]{0:T(1024)} %param.23) | copy-start | bytes 49156
  144.2 7.9 %copy-start.22 = (f32[1536]{0:T(1024)S(1)}, f32[1536]{0:T(1024)}, u32[]{:S(2)}) copy-start(f32[1536]{0:T(1024)} %param.25) | copy-start | bytes 18436
  147.2 10.4 %collective-permute-start.21 = (bf16[128,1024]{1,0:T(8,128)(2,1)}, bf16[128,1024]{1,0:T(8,128)(2,1)S(1)}, u32[]{:S(2)}, u32[]{:S(2)}) collective-permute-start(bf16[128,1024]{1,0:T(8,128)(2,1)} %dense.1.x0), channel_id=1, source_target_pairs={{0,32},{32,64},{64,96},{96,0},{1,33},{33,65},{65,97},{97,1},{2,34}... | collective-permute-start | bytes 786440 | tf_op jit(solution)/shard_map/ppermute | solution.py:565
  148.0 12.5 %collective-permute-start.22 = (bf16[128,1024]{1,0:T(8,128)(2,1)}, bf16[128,1024]{1,0:T(8,128)(2,1)S(1)}, u32[]{:S(2)}, u32[]{:S(2)}) collective-permute-start(bf16[128,1024]{1,0:T(8,128)(2,1)} %dense.1.x0), channel_id=1, source_target_pairs={{0,64},{32,96},{64,0},{96,32},{1,65},{33,97},{65,1},{97,33},{2,66}... | collective-permute-start | bytes 786440 | tf_op jit(solution)/shard_map/ppermute | solution.py:565
  151.1 9.4 %collective-permute-start.23 = (bf16[128,1024]{1,0:T(8,128)(2,1)}, bf16[128,1024]{1,0:T(8,128)(2,1)S(1)}, u32[]{:S(2)}, u32[]{:S(2)}) collective-permute-start(bf16[128,1024]{1,0:T(8,128)(2,1)} %dense.1.x0), channel_id=1, source_target_pairs={{0,96},{32,0},{64,32},{96,64},{1,97},{33,1},{65,33},{97,65},{2,98}... | collective-permute-start | bytes 786440 | tf_op jit(solution)/shard_map/ppermute | solution.py:565
  160.5 4.6 %copy-start.2 = (bf16[4096,1536]{1,0:T(8,128)(2,1)S(1)}, bf16[4096,1536]{1,0:T(8,128)(2,1)}, u32[]{:S(2)}) copy-start(bf16[4096,1536]{1,0:T(8,128)(2,1)} %weight.1) | copy-start | bytes 37748740
  165.1 0.9 copy-start.6
  171.3 3.4 %copy-start.3 = (bf16[4096,1024]{1,0:T(8,128)(2,1)S(1)}, bf16[4096,1024]{1,0:T(8,128)(2,1)}, u32[]{:S(2)}) copy-start(bf16[4096,1024]{1,0:T(8,128)(2,1)} %all-gather.2.cloned.1.call-done.new_ref) | copy-start | bytes 25165828
Sparse Core Ops, SparseCore 0:
  14.3 87.0 all-gather.1
where the time goes:
time: 186 us; the launch traced here: 184 us
  waiting for transfers between devices  62.3 us (33%)
  starting transfers between devices  46.7 us (25%)
  Pallas kernels  32.7 us (18%)
  local copies, waits for them, and re-layouts  24.3 us (13%)
  between operations  15 us (8%)
  other arithmetic  2.53 us (1%)
    ppermute x3, waiting for transfers between devices, on_device(): lax.ppermute(part, 'page', plane_shift(-s, 0))  20.5 us
    unnamed x48, local copies, waits for them, and re-layouts  17.9 us
    ppermute x3, starting transfers between devices, on_device(): lax.ppermute(weights[s], 'head', head_shift(s))  17.4 us
    pallas_call x4, Pallas kernels, attend(): pl.pallas_call(body, out_shape=jax.ShapeDtypeStruct((4, PIECES, TOK), BF1...  15.7 us
    ppermute x3, waiting for transfers between devices, on_device(): lax.ppermute(row_queries, 'page', plane_shift(s, 0))  13.9 us
    ppermute x3, waiting for transfers between devices, on_device(): lax.ppermute(blocks[s], 'page', plane_shift(0, -s))  11.9 us
    ppermute x3, waiting for transfers between devices, on_device(): lax.ppermute(new_hidden, 'head', head_shift(s))  8.33 us
    ppermute x3, starting transfers between devices, on_device(): lax.ppermute(attention, 'head', head_shift(s))  6.24 us
  transfers between devices with their start and end apart: 25, of which 13 were waited for; matrix products, arithmetic and copies ran while one was open for 4% of the time, Pallas kernels for 16%

commit v1 on v0

v1 whole, which is shorter than its diff:
```python
import math

import jax
import jax.numpy as jnp
from jax import lax
from jax.experimental import pallas as pl
from jax.experimental.pallas import tpu as pltpu
from jax.sharding import Mesh
from jax.sharding import PartitionSpec as P

D = 4096
HS = 128
ROT = 32
PT = 128
GROUP = 512
LH = 4
LW = LH * HS
SLOTS = 13
REQS = 8
MAXP = 36
TOK = 128
PIECES = LW + 32
COLS = D // 4
QW = 1536
NEG = -1e30
C2 = math.log2(math.e) / math.sqrt(HS)
F32 = jnp.float32
BF16 = jnp.bfloat16
VMEM = pltpu.VMEM
HBM = pltpu.HBM
SMEM = pltpu.SMEM


def whole(space=VMEM):
    return pl.BlockSpec(memory_space=space)


def limit(mib):
    return pltpu.CompilerParams(vmem_limit_bytes=mib << 20)


def head_rows(h):
    return slice(h * HS, (h + 1) * HS)


def rotary_kernel(info, lens, x_ref, rate_ref, q_ref, kv_ref):
    half = ROT // 2
    page = info[0]
    first = lens[lax.div(page, 4)] + lax.rem(page, 4) * TOK
    lane = lax.broadcasted_iota(jnp.int32, (half, TOK), 1)
    angles = (first + lane).astype(F32) * rate_ref[...]
    cosine = jnp.cos(angles)
    sine = jnp.sin(angles)
    for h in range(LH):
        for which in range(2):
            base = (3 * h + which) * HS
            turned = x_ref[:, base : base + HS].astype(F32).T
            a = turned[0:half]
            b = turned[half:ROT]
            done = jnp.concatenate(
                [a * cosine - b * sine, b * cosine + a * sine, turned[ROT:]], axis=0
            )
            if which == 0:
                q_ref[head_rows(h), :] = done.astype(BF16)
            else:
                kv_ref[:, head_rows(h)] = done.T.astype(BF16)
        base = (3 * h + 2) * HS
        kv_ref[:, LW + h * HS : LW + (h + 1) * HS] = x_ref[:, base : base + HS]


def rotary(info, lens, group_qkv, rates):
    return pl.pallas_call(
        rotary_kernel,
        out_shape=(
            jax.ShapeDtypeStruct((LW, TOK), BF16),
            jax.ShapeDtypeStruct((TOK, 2 * LW), BF16),
        ),
        in_specs=[whole(SMEM)] * 2 + [whole()] * 2,
        out_specs=(whole(), whole()),
        compiler_params=limit(2),
        name="rotary",
    )(info, lens, group_qkv, rates)


def stack_kernel(*refs):
    for i, ref in enumerate(refs[:-1]):
        refs[-1][i] = ref[...]


def stack(parts):
    return pl.pallas_call(
        stack_kernel,
        out_shape=jax.ShapeDtypeStruct((len(parts),) + parts[0].shape, parts[0].dtype),
        in_specs=[whole()] * len(parts),
        out_specs=whole(),
        compiler_params=limit(6),
        name="stack",
    )(*parts)


LIST = 32


def pool_kernel(info, lens, table, k_other, v_other, keys, values, codes, counts, sems):
    page = info[0]
    chip = lax.div(page, 2)
    copies = [
        pltpu.make_async_copy(src.at[i], dst.at[i], sems.at[n, i])
        for n, (src, dst) in enumerate(((k_other, keys), (v_other, values)))
        for i in range(SLOTS)
    ]
    for copy in copies:
        copy.start()

    def scan_request(request, carry):
        def scan(g, n):
            slot = table[request, g]
            device = lax.div(slot, SLOTS)
            here = lax.div(device, 2) == chip

            @pl.when(here)
            def _():
                local = slot - device * SLOTS
                local = jnp.where(device == page, local, local + SLOTS)
                codes[request, n] = g * LIST + local

            return n + here.astype(jnp.int32)

        used = lax.div(lens[request] + (PT - 1), PT)
        counts[request] = lax.fori_loop(0, used, scan, jnp.int32(0))
        return carry

    lax.fori_loop(0, REQS, scan_request, 0)
    for copy in copies:
        copy.wait()


def pool(info, lens, table, k_other, v_other):
    shape = jax.ShapeDtypeStruct(k_other.shape, BF16)
    return pl.pallas_call(
        pool_kernel,
        out_shape=(
            shape,
            shape,
            jax.ShapeDtypeStruct((REQS, LIST), jnp.int32),
            jax.ShapeDtypeStruct((REQS,), jnp.int32),
        ),
        in_specs=[whole(SMEM)] * 3 + [whole(HBM)] * 2,
        out_specs=(whole(), whole(), whole(SMEM), whole(SMEM)),
        scratch_shapes=[pltpu.SemaphoreType.DMA((2, SLOTS))],
        compiler_params=limit(8),
        name="pool",
    )(info, lens, table, k_other, v_other)


PARTS = 32


def load_kernel(src, dst, sems):
    rows = src.shape[0] // PARTS
    copies = [
        pltpu.make_async_copy(
            src.at[pl.ds(i * rows, rows)], dst.at[pl.ds(i * rows, rows)], sems.at[i]
        )
        for i in range(PARTS)
    ]
    for copy in copies:
        copy.start()
    for copy in copies:
        copy.wait()


def load(array):
    return pl.pallas_call(
        load_kernel,
        out_shape=jax.ShapeDtypeStruct(array.shape, array.dtype),
        in_specs=[whole(HBM)],
        out_specs=whole(),
        scratch_shapes=[pltpu.SemaphoreType.DMA((PARTS,))],
        compiler_params=limit(40),
        name="load",
    )(array)


def split3(value):
    top = value.astype(BF16)
    rest = value - top.astype(F32)
    middle = rest.astype(BF16)
    low = (rest - middle.astype(F32)).astype(BF16)
    return top, middle, low


def stat_rows(stats):
    width = stats.shape[1]
    return jnp.concatenate(
        [piece.astype(F32) for piece in split3(stats)] + [jnp.zeros((8, width), F32)], axis=0
    ).astype(BF16)


def attention_kernel(
    step, info, lens, codes, counts, q_ref, k_own, v_own, k_other, v_other, *rest
):
    if step != 2:
        fresh_own, fresh_other, *rest = rest
    o_ref, acc, stats = rest
    y = info[1]
    x = info[2]
    core = info[3]
    key_row = lax.broadcasted_iota(jnp.int32, (2 * PT, TOK), 0)
    lane = lax.broadcasted_iota(jnp.int32, (2 * PT, TOK), 1)

    def block_loop(block, carry):
        row = lax.bitwise_and(y - jnp.where(core == 0, step, block), 3)
        column = lax.bitwise_and(x - jnp.where(core == 0, block, step), 3)
        request = 2 * row + lax.div(column, 2)

        def absorb(key_of, value_of, mask, guard):
            old = stats[...]
            scores = [
                jnp.where(
                    mask,
                    jnp.dot(key_of(h), q_ref[block, head_rows(h), :], preferred_element_type=F32),
                    NEG,
                )
                for h in range(LH)
            ]
            peaks = [
                jnp.maximum(old[h : h + 1], jnp.max(scores[h], axis=0, keepdims=True))
                for h in range(LH)
            ]
            weights = [jnp.exp2((scores[h] - peaks[h]) * C2) for h in range(LH)]
            if guard:
                weights = [jnp.where(mask, w, 0.0) for w in weights]
            decays = [jnp.exp2((old[h : h + 1] - peaks[h]) * C2) for h in range(LH)]
            totals = [
                old[LH + h : LH + h + 1] * decays[h] + jnp.sum(weights[h], axis=0, keepdims=True)
                for h in range(LH)
            ]
            stats[...] = jnp.concatenate(peaks + totals, axis=0)
            added = [
                lax.dot_general(
                    value_of(h), weights[h].astype(BF16), (((0,), (0,)), ((), ())),
                    preferred_element_type=F32,
                )
                for h in range(LH)
            ]
            for h in range(LH):
                acc[head_rows(h), :] = acc[head_rows(h), :] * decays[h] + added[h]

        acc[...] = jnp.zeros_like(acc)
        stats[...] = jnp.where(lax.broadcasted_iota(jnp.int32, (2 * LH, TOK), 0) < LH, NEG, 0.0)
        count = counts[request]

        def pages_step(i, inner):
            full = 2 * i + 1 < count
            first = codes[request, 2 * i]
            second = codes[request, jnp.where(full, 2 * i + 1, 2 * i)]
            lower = lens[request] - lax.div(first, LIST) * PT
            upper = jnp.where(full, lens[request] - lax.div(second, LIST) * PT, 0) + PT
            mask = key_row < jnp.where(key_row < PT, lower, upper)

            def page_rows(own, other, code, h):
                slot = lax.rem(code, LIST)
                mine = slot < SLOTS
                local = jnp.where(mine, slot, slot - SLOTS)
                return jnp.where(
                    mine, own[local, :, head_rows(h)], other[local, :, head_rows(h)]
                )

            def pair(own, other, h):
                return jnp.concatenate(
                    [page_rows(own, other, first, h), page_rows(own, other, second, h)], axis=0
                )

            absorb(
                lambda h: pair(k_own, k_other, h), lambda h: pair(v_own, v_other, h), mask, False
            )
            return inner

        lax.fori_loop(0, lax.div(count + 1, 2), pages_step, 0)
        if step != 2:

            @pl.when(request == 2 * y + lax.div(x, 2))
            def _():
                pair = lambda cols: jnp.concatenate(
                    [fresh_own[:, cols], fresh_other[:, cols]], axis=0
                )
                token = 2 * lax.bitwise_and(x, 1) * TOK + jnp.where(
                    key_row < PT, key_row + core * TOK, key_row - core * TOK
                )
                query = (2 * lax.bitwise_and(column, 1) + core) * TOK + lane
                absorb(
                    lambda h: pair(head_rows(h)),
                    lambda h: pair(slice(LW + h * HS, LW + (h + 1) * HS)),
                    token <= query,
                    True,
                )

        for h in range(LH):
            o_ref[block, head_rows(h), :] = acc[head_rows(h), :].astype(BF16)
        o_ref[block, LW:PIECES, :] = stat_rows(stats[...])
        return carry

    lax.fori_loop(0, 4, block_loop, 0)


def attend(step, info, lens, lists, queries, caches, fresh):
    operands = [info, lens, *lists, queries, *caches] + ([] if step == 2 else list(fresh))
    specs = [whole(SMEM)] * 4 + [whole()] * (5 if step == 2 else 7)

    def body(*refs):
        attention_kernel(step, *refs)

    return pl.pallas_call(
        body,
        out_shape=jax.ShapeDtypeStruct((4, PIECES, TOK), BF16),
        in_specs=specs,
        out_specs=whole(),
        scratch_shapes=[VMEM((LW, TOK), F32), VMEM((2 * LH, TOK), F32)],
        compiler_params=limit(12),
        cost_estimate=pl.CostEstimate(flops=0, transcendentals=0, bytes_accessed=0),
        name="attend%d" % step,
    )(*operands)


def join(parts):
    read = []
    for part in parts:
        tail = part[LW:PIECES].astype(F32)
        read.append(tail[0:8] + tail[8:16] + tail[16:24])
    peak = read[0][0:LH]
    for value in read[1:]:
        peak = jnp.maximum(peak, value[0:LH])
    factors = [jnp.exp2((value[0:LH] - peak) * C2) for value in read]
    total = sum(value[LH : 2 * LH] * factor for value, factor in zip(read, factors))
    weighted = [
        sum(
            part[head_rows(h)].astype(F32) * factor[h : h + 1]
            for part, factor in zip(parts, factors)
        )
        for h in range(LH)
    ]
    return peak, total, weighted


def join_rows_kernel(a_ref, b_ref, c_ref, d_ref, *outs):
    for block, out in enumerate(outs):
        parts = [ref.at[block] for ref in (a_ref, b_ref, c_ref, d_ref)]
        peak, total, weighted = join(parts)
        for h in range(LH):
            out[head_rows(h), :] = weighted[h].astype(BF16)
        out[LW:PIECES, :] = stat_rows(jnp.concatenate([peak, total], axis=0))


def join_last_kernel(a_ref, b_ref, c_ref, d_ref, out):
    _, total, weighted = join([a_ref, b_ref, c_ref, d_ref])
    inverse = 1.0 / total
    for h in range(LH):
        out[:, head_rows(h)] = (weighted[h] * inverse[h : h + 1]).T.astype(BF16)


def join_rows(parts):
    return pl.pallas_call(
        join_rows_kernel,
        out_shape=tuple(jax.ShapeDtypeStruct((PIECES, TOK), BF16) for _ in range(4)),
        in_specs=[whole()] * 4,
        out_specs=tuple(whole() for _ in range(4)),
        compiler_params=limit(8),
        name="join_rows",
    )(*parts)


def join_last(parts):
    return pl.pallas_call(
        join_last_kernel,
        out_shape=jax.ShapeDtypeStruct((TOK, LW), BF16),
        in_specs=[whole()] * 4,
        out_specs=whole(),
        compiler_params=limit(4),
        name="join_last",
    )(*parts)


def dense_kernel(info, attention, weight, bias, hidden, branch, own, *outs):
    head = info[4]
    base = pl.ds(pl.multiple_of(head * COLS, COLS), COLS)
    for s in range(4):
        target = lax.bitwise_and(head + s, 3)
        cols = pl.ds(pl.multiple_of(target * COLS, COLS), COLS)
        product = jnp.dot(attention[...], weight[:, cols], preferred_element_type=F32)
        if s == 0:
            rest = bias[base].reshape(1, COLS) + hidden[...].astype(F32) + branch[...].astype(F32)
            own[...] = product + rest
        else:
            outs[s - 1][...] = product.astype(BF16)


def dense(info, attention, weight, bias, hidden, branch):
    shape = jax.ShapeDtypeStruct((TOK, COLS), BF16)
    return pl.pallas_call(
        dense_kernel,
        out_shape=(jax.ShapeDtypeStruct((TOK, COLS), F32), shape, shape, shape),
        in_specs=[whole(SMEM)] + [whole()] * 5,
        out_specs=(whole(),) * 4,
        compiler_params=limit(10),
        name="dense",
    )(info, attention, weight, bias, hidden, branch)


def join_shares_kernel(own, a, b, c, out):
    out[...] = (
        own[...] + (a[...].astype(F32) + b[...].astype(F32) + c[...].astype(F32))
    ).astype(BF16)


def join_shares(parts):
    return pl.pallas_call(
        join_shares_kernel,
        out_shape=jax.ShapeDtypeStruct((TOK, COLS), BF16),
        in_specs=[whole()] * 4,
        out_specs=whole(),
        compiler_params=limit(4),
        name="join_shares",
    )(*parts)


def qkv_kernel(info, x0, x1, x2, x3, gain, shift, weight, bias, out):
    head = info[4]
    blocks = (x0, x1, x2, x3)
    total = 0.0
    square = 0.0
    for block in blocks:
        value = block[...].astype(F32)
        total = total + jnp.sum(value, axis=1, keepdims=True)
        square = square + jnp.sum(value * value, axis=1, keepdims=True)
    mean = total / D
    variance = square / D - mean * mean
    scale = lax.rsqrt(variance + 1e-05)
    result = bias[...].reshape(1, QW) + jnp.zeros((TOK, QW), F32)
    for s, block in enumerate(blocks):
        origin = lax.bitwise_and(head - s, 3)
        rows = pl.ds(pl.multiple_of(origin * COLS, COLS), COLS)
        normed = (block[...].astype(F32) - mean) * scale * gain[rows].reshape(1, COLS)
        normed = (normed + shift[rows].reshape(1, COLS)).astype(BF16)
        result = result + jnp.dot(normed, weight[rows, :], preferred_element_type=F32)
    out[...] = result.astype(BF16)


def project_qkv(info, blocks, gain, shift, weight, bias):
    return pl.pallas_call(
        qkv_kernel,
        out_shape=jax.ShapeDtypeStruct((TOK, QW), BF16),
        in_specs=[whole(SMEM)] + [whole()] * 8,
        out_specs=whole(),
        compiler_params=limit(20),
        name="project_qkv",
    )(info, *blocks, gain, shift, weight, bias)


WINDOW = 2 * TOK


def patch_kernel(info, lens, table, *refs):
    news = refs[0:2]
    k_in, v_in, k_out, v_out, src, kbuf, vbuf, sems, bulk, slots, offsets = refs[2:]
    page = info[0]
    core = info[3]
    whole_copies = (
        pltpu.make_async_copy(k_in, k_out, bulk.at[0]),
        pltpu.make_async_copy(v_in, v_out, bulk.at[1]),
    )
    for copy in whole_copies:
        copy.start()

    def source(n, half, ref, block):
        return pltpu.make_async_copy(
            ref.at[block], src.at[n, pl.ds(half * TOK, TOK), :], sems.at[n, half]
        )

    def loads(n, local):
        return (
            pltpu.make_async_copy(k_in.at[local], kbuf.at[n], sems.at[n, 2]),
            pltpu.make_async_copy(v_in.at[local], vbuf.at[n], sems.at[n, 3]),
        )

    def stores(n, local):
        return (
            pltpu.make_async_copy(kbuf.at[n], k_out.at[local], sems.at[n, 4]),
            pltpu.make_async_copy(vbuf.at[n], v_out.at[local], sems.at[n, 5]),
        )

    def scan_request(request, count):
        length = lens[request]
        first = lax.div(length, PT)
        last = lax.div(length + (GROUP - 1), PT)

        def scan(g, n):
            slot = table[request, g]
            here = lax.div(slot, SLOTS) == page

            @pl.when(here)
            def _():
                local = slot - page * SLOTS
                offset = g * PT - length
                lower = lax.div(offset + PT, PT) - 1
                slots[n] = local
                offsets[n] = offset
                for copy in loads(n, local):
                    copy.start()
                for half in range(2):
                    block = jnp.clip(lower + half, 0, 3)
                    chip = 2 * request + lax.div(block, 2)
                    mine = lax.rem(block, 2) == core

                    @pl.when(mine)
                    def _(half=half, chip=chip):
                        source(n, half, news[0], chip).start()

                    @pl.when(jnp.logical_not(mine))
                    def _(half=half, chip=chip):
                        source(n, half, news[1], chip).start()

            return n + here.astype(jnp.int32)

        return lax.fori_loop(first, last + 1, scan, count)

    count = lax.fori_loop(0, REQS, scan_request, jnp.int32(0))
    pick_row = lax.broadcasted_iota(jnp.int32, (PT, WINDOW), 0)
    pick_col = lax.broadcasted_iota(jnp.int32, (PT, WINDOW), 1)
    token = lax.broadcasted_iota(jnp.int32, (PT, LW), 0)

    def update(n, carry):
        for half in range(2):
            source(n, half, news[0], 0).wait()
        for copy in loads(n, 0):
            copy.wait()
        offset = offsets[n]
        base = (lax.div(offset + PT, PT) - 1) * PT
        pick = jnp.where(pick_col == pick_row + (offset - base), 1.0, 0.0).astype(BF16)
        index = token + offset
        fresh = (index >= 0) & (index < GROUP)
        for buf, cols in ((kbuf, slice(0, LW)), (vbuf, slice(LW, 2 * LW))):
            moved = jnp.dot(pick, src[n, :, cols], preferred_element_type=F32)
            buf[n] = jnp.where(fresh, moved, buf[n].astype(F32)).astype(BF16)
        return carry

    def put(n, carry):
        for copy in stores(n, slots[n]):
            copy.start()
        return carry

    def finish(n, carry):
        for copy in stores(n, 0):
            copy.wait()
        return carry

    lax.fori_loop(0, count, update, 0)
    for copy in whole_copies:
        copy.wait()
    lax.fori_loop(0, count, put, 0)
    lax.fori_loop(0, count, finish, 0)


def patch(info, lens, table, news, key_cache, value_cache):
    shape = jax.ShapeDtypeStruct(key_cache.shape, BF16)
    return pl.pallas_call(
        patch_kernel,
        out_shape=(shape, shape),
        in_specs=[whole(SMEM)] * 3 + [whole(HBM)] * 4,
        out_specs=(whole(HBM), whole(HBM)),
        scratch_shapes=[
            VMEM((SLOTS, WINDOW, 2 * LW), BF16),
            VMEM((SLOTS, PT, LW), BF16),
            VMEM((SLOTS, PT, LW), BF16),
            pltpu.SemaphoreType.DMA((SLOTS, 6)),
            pltpu.SemaphoreType.DMA((2,)),
            SMEM((SLOTS,), jnp.int32),
            SMEM((SLOTS,), jnp.int32),
        ],
        compiler_params=pltpu.CompilerParams(vmem_limit_bytes=20 << 20),
        name="patch",
    )(info, lens, table, *news, key_cache, value_cache)


def shift(s):
    return [(i, (i + s) % 4) for i in range(4)]


PLANE = ("y", "x", "core")
CORES = [(0, 1), (1, 0)]


def plane_shift(s, stage):
    pairs = []
    for y in range(4):
        for x in range(4):
            for c in range(2):
                along_x = (c == 0) == (stage == 0)
                to_y, to_x = (y, (x + s) % 4) if along_x else ((y + s) % 4, x)
                pairs.append((y * 8 + x * 2 + c, to_y * 8 + to_x * 2 + c))
    return pairs


def send(array, s, stage):
    return lax.ppermute(array, PLANE, plane_shift(s, stage))


def on_device(
    hidden,
    group_qkv,
    mlp_branch,
    key_cache,
    paged_value_cache,
    cache_lengths,
    page_table,
    dense_weight,
    dense_bias,
    norm_gain,
    norm_bias,
    qkv_weight,
    qkv_bias,
):
    y = lax.axis_index("y").astype(jnp.int32)
    x = lax.axis_index("x").astype(jnp.int32)
    core = lax.axis_index("core").astype(jnp.int32)
    head = lax.axis_index("head").astype(jnp.int32)
    page = 8 * y + 2 * x + core

    info = jnp.stack([page, y, x, core, head])

    inverse = 1.0 / 10000.0 ** (jnp.arange(0, ROT, 2, dtype=F32) / ROT)
    rates = jnp.broadcast_to(inverse[:, None], (ROT // 2, TOK))
    queries, fresh = rotary(info, cache_lengths, group_qkv, rates)

    gathered = lax.all_gather(fresh, ("y", "x"), axis=0)
    other_keys = lax.ppermute(key_cache, "core", CORES)
    other_values = lax.ppermute(paged_value_cache, "core", CORES)
    other_fresh = lax.ppermute(fresh, "core", CORES)
    near = [queries] + [send(queries, s, 0) for s in range(1, 4)]
    near = stack(near)
    all_queries = [near] + [send(near, s, 1) for s in range(1, 4)]

    pool_keys, pool_values, codes, counts = pool(
        info, cache_lengths, page_table, other_keys, other_values
    )
    caches = (key_cache, paged_value_cache, pool_keys, pool_values)

    partials = [None] * 4
    last = None
    for s in (0, 1, 3, 2):
        wanted = all_queries[s]
        if last is not None:
            wanted, last = lax.optimization_barrier((wanted, last))
        part = attend(
            s, info, cache_lengths, (codes, counts), wanted, caches, (fresh, other_fresh)
        )
        if last is not None:
            partials[before] = last if before == 0 else send(last, -before, 1)
        last, before = part, s
    partials[before] = send(last, -before, 1)
    blocks = join_rows(partials)
    blocks, gathered = lax.optimization_barrier((blocks, gathered))
    news = (gathered, lax.ppermute(gathered, "core", CORES))
    blocks = [blocks[0]] + [send(blocks[s], -s, 0) for s in range(1, 4)]
    attention = join_last(blocks)

    shares = dense(info, attention, dense_weight, dense_bias, hidden, mlp_branch)
    shares = [shares[0]] + [lax.ppermute(shares[s], "head", shift(s)) for s in range(1, 4)]
    new_hidden = join_shares(shares)

    streams = [new_hidden] + [lax.ppermute(new_hidden, "head", shift(s)) for s in range(1, 4)]
    late_weight, _ = lax.optimization_barrier((qkv_weight, new_hidden))
    next_qkv = project_qkv(
        info, streams, norm_gain, norm_bias, load(late_weight), qkv_bias
    )

    key_out, value_out = patch(
        info, cache_lengths, page_table, news, key_cache, paged_value_cache
    )
    return (new_hidden, next_qkv, key_out, value_out)


def solution(mesh):
    plane = PLANE
    fine = Mesh(mesh.devices.reshape(4, 4, 4, 2), ("head",) + plane)
    in_specs = (
        P(plane, "head"),
        P(plane, "head"),
        P(plane, "head"),
        P(plane, None, "head"),
        P(plane, None, "head"),
        P(),
        P(),
        P("head", None),
        P(),
        P(),
        P(),
        P(None, "head"),
        P("head"),
    )
    out_specs = (
        P(plane, "head"),
        P(plane, "head"),
        P(plane, None, "head"),
        P(plane, None, "head"),
    )
    return jax.shard_map(
        on_device, mesh=fine, in_specs=in_specs, out_specs=out_specs, check_vma=False
    )
```

time: 186 us -> 153 us (0.82)
  the two profiles are of different devices: /device:TPU:24 before, /device:TPU:1 now
where the time goes in v1:
time: 153 us
  waiting for transfers between devices  62.5 us (41%)
  Pallas kernels  32.2 us (21%)
  starting transfers between devices  29 us (19%)
  local copies, waits for them, and re-layouts  14.5 us (9%)
  between operations  14.3 us (9%)
    ppermute x12, waiting for transfers between devices, send(): return lax.ppermute(array, PLANE, plane_shift(s, stage))  37.6 us
    ppermute x12, starting transfers between devices, send(): return lax.ppermute(array, PLANE, plane_shift(s, stage))  17.2 us
    unnamed x50, local copies, waits for them, and re-layouts  14.4 us
    ppermute x3, waiting for transfers between devices, on_device(): lax.ppermute(shares[s], 'head', shift(s))  12.2 us
    ppermute x3, waiting for transfers between devices, on_device(): lax.ppermute(new_hidden, 'head', shift(s))  8.53 us
    pallas_call x4, Pallas kernels, attend(): pl.pallas_call(body, out_shape=jax.ShapeDtypeStruct((4, PIECES, TOK), BF1...  8.28 us
    pallas_call x1, Pallas kernels, pool(): pl.pallas_call(pool_kernel, out_shape=(shape, shape, jax.ShapeDtypeStruct...  7.99 us
    pallas_call x1, Pallas kernels, load(): pl.pallas_call(load_kernel, out_shape=jax.ShapeDtypeStruct(array.shape, a...  4.85 us
  transfers between devices with their start and end apart: 23, of which 14 were waited for; matrix products, arithmetic and copies ran while one was open for 0% of the time, Pallas kernels for 18%

profile of v1, /device:TPU:1, one launch (start us, length us, event | category | flops | bytes accessed | tf_op | source)
XLA Modules:
  0.0 152.5 jit_solution(3425269961757854612)
XLA Ops:
  7.3 0.1 stack.24.info.refs_0_
  7.3 0.1 broadcast_in_dim.2.rate_ref
  7.4 1.0 copy-done.5
  8.4 0.7 copy-done.14
  9.1 1.5 rotary.1
  10.6 1.5 collective-permute-start.4
  12.1 0.1 collective-permute-start.5
  12.2 2.8 %collective-permute-start.2 = (bf16[512,128]{1,0:T(8,128)(2,1)S(1)}, bf16[512,128]{1,0:T(8,128)(2,1)S(1)}, u32[]{:S(2)}, u32[]{:S(2)}) collective-permute-start(bf16[512,128]{1,0:T(8,128)(2,1)S(1)} %get-tuple-element.32.refs_0_), channel_id=1, source_target_pairs={{0,6},{1,25},{2,0},{3,27},{4,2},{5,29},{6,4},{7,31},{8,14},{9,1},{... | collective-permute-start | bytes 393224 | tf_op jit(solution)/shard_map/ppermute | solution.py:605
  15.0 0.3 collective-permute-start.1
  15.4 0.7 collective-permute-start
  16.1 2.3 %collective-permute-done.2.refs_3_ = bf16[512,128]{1,0:T(8,128)(2,1)S(1)} collective-permute-done((bf16[512,128]{1,0:T(8,128)(2,1)S(1)}, bf16[512,128]{1,0:T(8,128)(2,1)S(1)}, u32[]{:S(2)}, u32[]{:S(2)}) %collective-permute-start.2) | collective-permute-done | bytes 131104 | tf_op jit(solution)/shard_map/ppermute | solution.py:605
  18.3 2.3 %collective-permute-done.1.refs_2_ = bf16[512,128]{1,0:T(8,128)(2,1)S(1)} collective-permute-done((bf16[512,128]{1,0:T(8,128)(2,1)S(1)}, bf16[512,128]{1,0:T(8,128)(2,1)S(1)}, u32[]{:S(2)}, u32[]{:S(2)}) %collective-permute-start.1) | collective-permute-done | bytes 131104 | tf_op jit(solution)/shard_map/ppermute | solution.py:605
  20.6 1.4 collective-permute-done.refs_1_
  22.1 1.0 collective-permute-start.3
  23.1 1.8 %collective-permute-start.7 = (bf16[4,512,128]{2,1,0:T(8,128)(2,1)S(1)}, bf16[4,512,128]{2,1,0:T(8,128)(2,1)S(1)}, u32[]{:S(2)}, u32[]{:S(2)}) collective-permute-start(bf16[4,512,128]{2,1,0:T(8,128)(2,1)S(1)} %stack.25.refs_4_), channel_id=1, source_target_pairs={{0,24},{1,7},{2,26},{3,1},{4,28},{5,3},{6,30},{7,5},{8,0},{9,15},{... | collective-permute-start | bytes 1572872 | tf_op jit(solution)/shard_map/ppermute | solution.py:605
  24.8 1.2 collective-permute-start.9
  26.1 2.6 %collective-permute-start.6 = (bf16[128,1024]{1,0:T(8,128)(2,1)}, bf16[128,1024]{1,0:T(8,128)(2,1)S(1)}, u32[]{:S(2)}, u32[]{:S(2)}) collective-permute-start(bf16[128,1024]{1,0:T(8,128)(2,1)} %get-tuple-element.37.refs_9_), channel_id=1, source_target_pairs={{0,1},{1,0},{2,3},{3,2},{4,5},{5,4},{6,7},{7,6},{8,9},{9,8},{10,11... | collective-permute-start | bytes 786440 | tf_op jit(solution)/shard_map/ppermute | solution.py:638
  28.7 8.0 %pool.1 = (bf16[13,128,512]{2,1,0:T(8,128)(2,1)S(1)}, bf16[13,128,512]{2,1,0:T(8,128)(2,1)S(1)}, s32[8,32]{1,0:T(8,128)S(1)}, s32[8]{0:T(128)S(1)}) custom-call(s32[5]{0:T(128)S(1)} %stack.24.info.refs_0_, s32[8]{0:T(128)S(1)} %copy-done.15, s32[8,36]{1,0:T(8,128)S(1)} %copy-done.17, bf16[13,128,512]{2,1,0:T(8,128)(2,1)S(1)} %collective-permute-done.4.k_other, ...), custom_call_target="tpu_custom_call" | custom-call | tf_op jit(solution)/shard_map/pool/pallas_call | solution.py:140
  36.7 2.2 %attend0.1.a_ref = bf16[4,544,128]{2,1,0:T(8,128)(2,1)S(1)} custom-call(s32[5]{0:T(128)S(1)} %stack.24.info.refs_0_, s32[8]{0:T(128)S(1)} %copy-done.15, s32[8,32]{1,0:T(8,128)S(1)} %get-tuple-element.33.refs_2_, s32[8]{0:T(128)S(1)} %get-tuple-element.34.refs_3_, bf16[4,512,128]{2,1,0:T(8,128)(2,1)S(1)} %stack.25.refs_4_, ...), custom_call_target="tpu_custom_call" | custom-call | tf_op jit(solution)/shard_map/attend0/pallas_call | solution.py:314
  38.9 2.1 %attend1.1 = bf16[4,544,128]{2,1,0:T(8,128)(2,1)S(1)} custom-call(s32[5]{0:T(128)S(1)} %stack.24.info.refs_0_, s32[8]{0:T(128)S(1)} %copy-done.15, s32[8,32]{1,0:T(8,128)S(1)} %get-tuple-element.33.refs_2_, s32[8]{0:T(128)S(1)} %get-tuple-element.34.refs_3_, bf16[4,512,128]{2,1,0:T(8,128)(2,1)S(1)} %collective-permute-done.3.refs_4_, ...), custom_call_target="tpu_custom_call" | custom-call | tf_op jit(solution)/shard_map/attend1/pallas_call | solution.py:314
  41.1 2.2 %attend3.1 = bf16[4,544,128]{2,1,0:T(8,128)(2,1)S(1)} custom-call(s32[5]{0:T(128)S(1)} %stack.24.info.refs_0_, s32[8]{0:T(128)S(1)} %copy-done.15, s32[8,32]{1,0:T(8,128)S(1)} %get-tuple-element.33.refs_2_, s32[8]{0:T(128)S(1)} %get-tuple-element.34.refs_3_, bf16[4,512,128]{2,1,0:T(8,128)(2,1)S(1)} %collective-permute-done.7.refs_4_, ...), custom_call_target="tpu_custom_call" | custom-call | tf_op jit(solution)/shard_map/attend3/pallas_call | solution.py:314
  43.3 1.8 %attend2.1 = bf16[4,544,128]{2,1,0:T(8,128)(2,1)S(1)} custom-call(s32[5]{0:T(128)S(1)} %stack.24.info.refs_0_, s32[8]{0:T(128)S(1)} %copy-done.15, s32[8,32]{1,0:T(8,128)S(1)} %get-tuple-element.33.refs_2_, s32[8]{0:T(128)S(1)} %get-tuple-element.34.refs_3_, bf16[4,512,128]{2,1,0:T(8,128)(2,1)S(1)} %collective-permute-done.9.refs_4_, ...), custom_call_target="tpu_custom_call" | custom-call | tf_op jit(solution)/shard_map/attend2/pallas_call | solution.py:314
  45.1 3.6 %collective-permute-start.10 = (bf16[4,544,128]{2,1,0:T(8,128)(2,1)S(1)}, bf16[4,544,128]{2,1,0:T(8,128)(2,1)S(1)}, u32[]{:S(2)}, u32[]{:S(2)}) collective-permute-start(bf16[4,544,128]{2,1,0:T(8,128)(2,1)S(1)} %attend2.1), channel_id=1, source_target_pairs={{0,16},{1,5},{2,18},{3,7},{4,20},{5,1},{6,22},{7,3},{8,24},{9,13},... | collective-permute-start | bytes 1671176 | tf_op jit(solution)/shard_map/ppermute | solution.py:605
  48.7 2.7 %collective-permute-start.8 = (bf16[4,544,128]{2,1,0:T(8,128)(2,1)S(1)}, bf16[4,544,128]{2,1,0:T(8,128)(2,1)S(1)}, u32[]{:S(2)}, u32[]{:S(2)}) collective-permute-start(bf16[4,544,128]{2,1,0:T(8,128)(2,1)S(1)} %attend1.1), channel_id=1, source_target_pairs={{0,24},{1,7},{2,26},{3,1},{4,28},{5,3},{6,30},{7,5},{8,0},{9,15},{... | collective-permute-start | bytes 1671176 | tf_op jit(solution)/shard_map/ppermute | solution.py:605
  51.3 12.3 %collective-permute-done.10.c_ref = bf16[4,544,128]{2,1,0:T(8,128)(2,1)S(1)} collective-permute-done((bf16[4,544,128]{2,1,0:T(8,128)(2,1)S(1)}, bf16[4,544,128]{2,1,0:T(8,128)(2,1)S(1)}, u32[]{:S(2)}, u32[]{:S(2)}) %collective-permute-start.10) | collective-permute-done | bytes 557088 | tf_op jit(solution)/shard_map/ppermute | solution.py:605
  63.6 13.1 %collective-permute-done.11.d_ref = bf16[4,544,128]{2,1,0:T(8,128)(2,1)S(1)} collective-permute-done((bf16[4,544,128]{2,1,0:T(8,128)(2,1)S(1)}, bf16[4,544,128]{2,1,0:T(8,128)(2,1)S(1)}, u32[]{:S(2)}, u32[]{:S(2)}) %collective-permute-start.11) | collective-permute-done | bytes 557088 | tf_op jit(solution)/shard_map/ppermute | solution.py:605
  76.7 0.5 join_rows.1
  77.1 0.6 copy-done.22
  77.8 0.7 copy-done.23
  78.5 0.7 copy-done.24
  79.1 4.2 %all-gather.3.cloned.1.call-done = bf16[2048,1024]{1,0:T(8,128)(2,1)} async-done(((bf16[128,1024]{1,0:T(8,128)(2,1)}), bf16[2048,1024]{1,0:T(8,128)(2,1)}) %all-gather.3.cloned.1.call-update) | async-done | bytes 4194320 | tf_op jit(solution)/shard_map/all_gather | solution.py:635
  83.3 0.7 collective-permute-start.21
  84.0 2.5 %collective-permute-start.12 = (bf16[544,128]{1,0:T(8,128)(2,1)}, bf16[544,128]{1,0:T(8,128)(2,1)S(1)}, u32[]{:S(2)}, u32[]{:S(2)}) collective-permute-start(bf16[544,128]{1,0:T(8,128)(2,1)} %copy-done.24), channel_id=1, source_target_pairs={{0,6},{1,25},{2,0},{3,27},{4,2},{5,29},{6,4},{7,31},{8,14},{9,1},{... | collective-permute-start | bytes 417800 | tf_op jit(solution)/shard_map/ppermute | solution.py:605
  86.5 0.6 collective-permute-start.14
  87.0 3.3 %collective-permute-done.12.b_ref = bf16[544,128]{1,0:T(8,128)(2,1)S(1)} collective-permute-done((bf16[544,128]{1,0:T(8,128)(2,1)}, bf16[544,128]{1,0:T(8,128)(2,1)S(1)}, u32[]{:S(2)}, u32[]{:S(2)}) %collective-permute-start.12) | collective-permute-done | bytes 139296 | tf_op jit(solution)/shard_map/ppermute | solution.py:605
  90.3 1.9 %collective-permute-done.13.c_ref = bf16[544,128]{1,0:T(8,128)(2,1)S(1)} collective-permute-done((bf16[544,128]{1,0:T(8,128)(2,1)}, bf16[544,128]{1,0:T(8,128)(2,1)S(1)}, u32[]{:S(2)}, u32[]{:S(2)}) %collective-permute-start.13) | collective-permute-done | bytes 139296 | tf_op jit(solution)/shard_map/ppermute | solution.py:605
  92.2 1.1 collective-permute-done.14.d_ref
  93.3 0.2 join_last.1.attention
  93.5 2.2 %copy-done.2 = bf16[512,4096]{1,0:T(8,128)(2,1)S(1)} copy-done((bf16[512,4096]{1,0:T(8,128)(2,1)S(1)}, bf16[512,4096]{1,0:T(8,128)(2,1)}, u32[]{:S(2)}) %copy-start.2) | copy-done | bytes 4194328
  95.7 0.9 copy-done.6
  96.6 0.9 copy-done.7
  97.6 0.7 copy-done.16
  98.3 1.3 dense.1
  99.6 0.3 collective-permute-start.15
  99.9 3.9 %collective-permute-start.16 = (bf16[128,1024]{1,0:T(8,128)(2,1)S(1)}, bf16[128,1024]{1,0:T(8,128)(2,1)S(1)}, u32[]{:S(2)}, u32[]{:S(2)}) collective-permute-start(bf16[128,1024]{1,0:T(8,128)(2,1)S(1)} %get-tuple-element.54), channel_id=1, source_target_pairs={{0,64},{32,96},{64,0},{96,32},{1,65},{33,97},{65,1},{97,33},{2,66}... | collective-permute-start | bytes 786440 | tf_op jit(solution)/shard_map/ppermute | solution.py:668
  103.7 0.1 collective-permute-start.17
  103.9 4.9 %collective-permute-done.15.a = bf16[128,1024]{1,0:T(8,128)(2,1)S(1)} collective-permute-done((bf16[128,1024]{1,0:T(8,128)(2,1)S(1)}, bf16[128,1024]{1,0:T(8,128)(2,1)S(1)}, u32[]{:S(2)}, u32[]{:S(2)}) %collective-permute-start.15) | collective-permute-done | bytes 262176 | tf_op jit(solution)/shard_map/ppermute | solution.py:668
  108.8 7.3 %collective-permute-done.16.b = bf16[128,1024]{1,0:T(8,128)(2,1)S(1)} collective-permute-done((bf16[128,1024]{1,0:T(8,128)(2,1)S(1)}, bf16[128,1024]{1,0:T(8,128)(2,1)S(1)}, u32[]{:S(2)}, u32[]{:S(2)}) %collective-permute-start.16) | collective-permute-done | bytes 262176 | tf_op jit(solution)/shard_map/ppermute | solution.py:668
  116.1 0.8 join_shares.1.x0
  116.9 1.8 %collective-permute-start.20 = (bf16[128,1024]{1,0:T(8,128)(2,1)}, bf16[128,1024]{1,0:T(8,128)(2,1)S(1)}, u32[]{:S(2)}, u32[]{:S(2)}) collective-permute-start(bf16[128,1024]{1,0:T(8,128)(2,1)} %join_shares.1.x0), channel_id=1, source_target_pairs={{0,96},{32,0},{64,32},{96,64},{1,97},{33,1},{65,33},{97,65},{2,98}... | collective-permute-start | bytes 786440 | tf_op jit(solution)/shard_map/ppermute | solution.py:671
  118.8 0.8 collective-permute-start.19
  119.5 4.8 %load.1.weight = bf16[4096,1536]{1,0:T(8,128)(2,1)S(1)} custom-call(bf16[4096,1536]{1,0:T(8,128)(2,1)} %src), custom_call_target="tpu_custom_call" | custom-call | tf_op jit(solution)/shard_map/load/pallas_call | solution.py:174
  124.4 0.2 collective-permute-done.20.x3
  124.7 0.7 copy-done.8
  125.4 2.2 %collective-permute-done.19.x2 = bf16[128,1024]{1,0:T(8,128)(2,1)S(1)} collective-permute-done((bf16[128,1024]{1,0:T(8,128)(2,1)}, bf16[128,1024]{1,0:T(8,128)(2,1)S(1)}, u32[]{:S(2)}, u32[]{:S(2)}) %collective-permute-start.19) | collective-permute-done | bytes 262176 | tf_op jit(solution)/shard_map/ppermute | solution.py:671
  127.6 0.7 copy-done.10
  128.3 6.0 %collective-permute-done.18.x1 = bf16[128,1024]{1,0:T(8,128)(2,1)S(1)} collective-permute-done((bf16[128,1024]{1,0:T(8,128)(2,1)}, bf16[128,1024]{1,0:T(8,128)(2,1)S(1)}, u32[]{:S(2)}, u32[]{:S(2)}) %collective-permute-start.18) | collective-permute-done | bytes 262176 | tf_op jit(solution)/shard_map/ppermute | solution.py:671
  134.3 0.7 copy-done.12
  135.1 0.9 copy-done.4
  136.0 0.9 copy-done.9
  137.0 0.9 copy-done.11
  137.9 0.9 copy-done.13
  138.9 3.7 %project_qkv.1 = bf16[128,1536]{1,0:T(8,128)(2,1)} custom-call(s32[5]{0:T(128)S(1)} %stack.24.info.refs_0_, bf16[128,1024]{1,0:T(8,128)(2,1)S(1)} %copy-done.4, bf16[128,1024]{1,0:T(8,128)(2,1)S(1)} %copy-done.13, bf16[128,1024]{1,0:T(8,128)(2,1)S(1)} %copy-done.11, bf16[128,1024]{1,0:T(8,128)(2,1)S(1)} %copy-done.9, f32[4096]{0:T(1024)S(1)} %copy-done.19, ...), custom_call_target="tpu_custom_call" | custom-call | tf_op jit(solution)/shard_map/project_qkv/pallas_call | solution.py:450
  142.6 3.1 %patch.1 = (bf16[13,128,512]{2,1,0:T(8,128)(2,1)}, bf16[13,128,512]{2,1,0:T(8,128)(2,1)}) custom-call(s32[5]{0:T(128)S(1)} %stack.24.info.refs_0_, s32[8]{0:T(128)S(1)} %copy-done.15, s32[8,36]{1,0:T(8,128)S(1)} %copy-done.18, bf16[16,128,1024]{2,1,0:T(8,128)(2,1)S(1)} %bitcast.7, bf16[16,128,1024]{2,1,0:T(8,128)(2,1)S(1)} %collective-permute-done.21.refs_1_, ...), custom_call_target="tpu_custom_call" | custom-call | tf_op jit(solution)/shard_map/patch/pallas_call | solution.py:566
  (50 shorter events, 0.2 us)
Async XLA Ops:
  7.2 21.5 %copy-start.15 = (s32[8]{0:T(128)S(1)}, s32[8]{0:T(128)}, u32[]{:S(2)}) copy-start(s32[8]{0:T(128)} %lens.5) | copy-start | bytes 100
  7.2 21.5 %copy-start.17 = (s32[8,36]{1,0:T(8,128)S(1)}, s32[8,36]{1,0:T(8,128)}, u32[]{:S(2)}) copy-start(s32[8,36]{1,0:T(8,128)} %table.3) | copy-start | bytes 3460
  7.2 76.1 %all-gather.3.cloned.1.call-start = ((), (), s32[]{:S(2)}) async-start(), calls=%async_computation | async-start | bytes 4456448 | tf_op jit(solution)/shard_map/all_gather | solution.py:635
  7.4 1.0 copy-start.5
  8.4 0.7 copy-start.14
  10.6 15.5 %collective-permute-start.4 = (bf16[13,128,512]{2,1,0:T(8,128)(2,1)}, bf16[13,128,512]{2,1,0:T(8,128)(2,1)S(1)}, u32[]{:S(2)}, u32[]{:S(2)}) collective-permute-start(bf16[13,128,512]{2,1,0:T(8,128)(2,1)} %refs_2_.1), channel_id=1, source_target_pairs={{0,1},{1,0},{2,3},{3,2},{4,5},{5,4},{6,7},{7,6},{8,9},{9,8},{10,11... | collective-permute-start | bytes 5111816 | tf_op jit(solution)/shard_map/ppermute | solution.py:636
  12.1 16.6 %collective-permute-start.5 = (bf16[13,128,512]{2,1,0:T(8,128)(2,1)}, bf16[13,128,512]{2,1,0:T(8,128)(2,1)S(1)}, u32[]{:S(2)}, u32[]{:S(2)}) collective-permute-start(bf16[13,128,512]{2,1,0:T(8,128)(2,1)} %refs_3_.1), channel_id=1, source_target_pairs={{0,1},{1,0},{2,3},{3,2},{4,5},{5,4},{6,7},{7,6},{8,9},{9,8},{10,11... | collective-permute-start | bytes 5111816 | tf_op jit(solution)/shard_map/ppermute | solution.py:637
  12.2 6.1 %collective-permute-start.2 = (bf16[512,128]{1,0:T(8,128)(2,1)S(1)}, bf16[512,128]{1,0:T(8,128)(2,1)S(1)}, u32[]{:S(2)}, u32[]{:S(2)}) collective-permute-start(bf16[512,128]{1,0:T(8,128)(2,1)S(1)} %get-tuple-element.32.refs_0_), channel_id=1, source_target_pairs={{0,6},{1,25},{2,0},{3,27},{4,2},{5,29},{6,4},{7,31},{8,14},{9,1},{... | collective-permute-start | bytes 393224 | tf_op jit(solution)/shard_map/ppermute | solution.py:605
  15.0 5.6 %collective-permute-start.1 = (bf16[512,128]{1,0:T(8,128)(2,1)S(1)}, bf16[512,128]{1,0:T(8,128)(2,1)S(1)}, u32[]{:S(2)}, u32[]{:S(2)}) collective-permute-start(bf16[512,128]{1,0:T(8,128)(2,1)S(1)} %get-tuple-element.32.refs_0_), channel_id=1, source_target_pairs={{0,4},{1,17},{2,6},{3,19},{4,0},{5,21},{6,2},{7,23},{8,12},{9,25},... | collective-permute-start | bytes 393224 | tf_op jit(solution)/shard_map/ppermute | solution.py:605
  15.4 6.7 %collective-permute-start = (bf16[512,128]{1,0:T(8,128)(2,1)S(1)}, bf16[512,128]{1,0:T(8,128)(2,1)S(1)}, u32[]{:S(2)}, u32[]{:S(2)}) collective-permute-start(bf16[512,128]{1,0:T(8,128)(2,1)S(1)} %get-tuple-element.32.refs_0_), channel_id=1, source_target_pairs={{0,2},{1,9},{2,4},{3,11},{4,6},{5,13},{6,0},{7,15},{8,10},{9,17},{... | collective-permute-start | bytes 393224 | tf_op jit(solution)/shard_map/ppermute | solution.py:605
  22.1 14.6 %copy-start = (bf16[13,128,512]{2,1,0:T(8,128)(2,1)S(1)}, bf16[13,128,512]{2,1,0:T(8,128)(2,1)}, u32[]{:S(2)}) copy-start(bf16[13,128,512]{2,1,0:T(8,128)(2,1)} %refs_2_.1) | copy-start | bytes 5111812
  22.1 14.6 %copy-start.1 = (bf16[13,128,512]{2,1,0:T(8,128)(2,1)S(1)}, bf16[13,128,512]{2,1,0:T(8,128)(2,1)}, u32[]{:S(2)}) copy-start(bf16[13,128,512]{2,1,0:T(8,128)(2,1)} %refs_3_.1) | copy-start | bytes 5111812
  22.1 16.8 %collective-permute-start.3 = (bf16[4,512,128]{2,1,0:T(8,128)(2,1)S(1)}, bf16[4,512,128]{2,1,0:T(8,128)(2,1)S(1)}, u32[]{:S(2)}, u32[]{:S(2)}) collective-permute-start(bf16[4,512,128]{2,1,0:T(8,128)(2,1)S(1)} %stack.25.refs_4_), channel_id=1, source_target_pairs={{0,8},{1,3},{2,10},{3,5},{4,12},{5,7},{6,14},{7,1},{8,16},{9,11},{... | collective-permute-start | bytes 1572872 | tf_op jit(solution)/shard_map/ppermute | solution.py:605
  23.1 18.0 %collective-permute-start.7 = (bf16[4,512,128]{2,1,0:T(8,128)(2,1)S(1)}, bf16[4,512,128]{2,1,0:T(8,128)(2,1)S(1)}, u32[]{:S(2)}, u32[]{:S(2)}) collective-permute-start(bf16[4,512,128]{2,1,0:T(8,128)(2,1)S(1)} %stack.25.refs_4_), channel_id=1, source_target_pairs={{0,24},{1,7},{2,26},{3,1},{4,28},{5,3},{6,30},{7,5},{8,0},{9,15},{... | collective-permute-start | bytes 1572872 | tf_op jit(solution)/shard_map/ppermute | solution.py:605
  24.8 18.4 %collective-permute-start.9 = (bf16[4,512,128]{2,1,0:T(8,128)(2,1)S(1)}, bf16[4,512,128]{2,1,0:T(8,128)(2,1)S(1)}, u32[]{:S(2)}, u32[]{:S(2)}) collective-permute-start(bf16[4,512,128]{2,1,0:T(8,128)(2,1)S(1)} %stack.25.refs_4_), channel_id=1, source_target_pairs={{0,16},{1,5},{2,18},{3,7},{4,20},{5,1},{6,22},{7,3},{8,24},{9,13},... | collective-permute-start | bytes 1572872 | tf_op jit(solution)/shard_map/ppermute | solution.py:605
  26.1 10.6 %collective-permute-start.6 = (bf16[128,1024]{1,0:T(8,128)(2,1)}, bf16[128,1024]{1,0:T(8,128)(2,1)S(1)}, u32[]{:S(2)}, u32[]{:S(2)}) collective-permute-start(bf16[128,1024]{1,0:T(8,128)(2,1)} %get-tuple-element.37.refs_9_), channel_id=1, source_target_pairs={{0,1},{1,0},{2,3},{3,2},{4,5},{5,4},{6,7},{7,6},{8,9},{9,8},{10,11... | collective-permute-start | bytes 786440 | tf_op jit(solution)/shard_map/ppermute | solution.py:638
  45.1 18.5 %collective-permute-start.10 = (bf16[4,544,128]{2,1,0:T(8,128)(2,1)S(1)}, bf16[4,544,128]{2,1,0:T(8,128)(2,1)S(1)}, u32[]{:S(2)}, u32[]{:S(2)}) collective-permute-start(bf16[4,544,128]{2,1,0:T(8,128)(2,1)S(1)} %attend2.1), channel_id=1, source_target_pairs={{0,16},{1,5},{2,18},{3,7},{4,20},{5,1},{6,22},{7,3},{8,24},{9,13},... | collective-permute-start | bytes 1671176 | tf_op jit(solution)/shard_map/ppermute | solution.py:605
  48.6 28.0 %collective-permute-start.11 = (bf16[4,544,128]{2,1,0:T(8,128)(2,1)S(1)}, bf16[4,544,128]{2,1,0:T(8,128)(2,1)S(1)}, u32[]{:S(2)}, u32[]{:S(2)}) collective-permute-start(bf16[4,544,128]{2,1,0:T(8,128)(2,1)S(1)} %attend3.1), channel_id=1, source_target_pairs={{0,8},{1,3},{2,10},{3,5},{4,12},{5,7},{6,14},{7,1},{8,16},{9,11},{... | collective-permute-start | bytes 1671176 | tf_op jit(solution)/shard_map/ppermute | solution.py:605
  48.7 28.0 %collective-permute-start.8 = (bf16[4,544,128]{2,1,0:T(8,128)(2,1)S(1)}, bf16[4,544,128]{2,1,0:T(8,128)(2,1)S(1)}, u32[]{:S(2)}, u32[]{:S(2)}) collective-permute-start(bf16[4,544,128]{2,1,0:T(8,128)(2,1)S(1)} %attend1.1), channel_id=1, source_target_pairs={{0,24},{1,7},{2,26},{3,1},{4,28},{5,3},{6,30},{7,5},{8,0},{9,15},{... | collective-permute-start | bytes 1671176 | tf_op jit(solution)/shard_map/ppermute | solution.py:605
  77.1 0.7 copy-start.22
  77.8 0.7 copy-start.23
  78.5 0.7 copy-start.24
  83.3 59.3 %collective-permute-start.21 = (bf16[16,128,1024]{2,1,0:T(8,128)(2,1)}, bf16[16,128,1024]{2,1,0:T(8,128)(2,1)S(1)}, u32[]{:S(2)}, u32[]{:S(2)}) collective-permute-start(bf16[16,128,1024]{2,1,0:T(8,128)(2,1)} %bitcast.6), channel_id=1, source_target_pairs={{0,1},{1,0},{2,3},{3,2},{4,5},{5,4},{6,7},{7,6},{8,9},{9,8},{10,11... | collective-permute-start | bytes 12582920 | tf_op jit(solution)/shard_map/ppermute | solution.py:663
  84.0 6.3 %collective-permute-start.12 = (bf16[544,128]{1,0:T(8,128)(2,1)}, bf16[544,128]{1,0:T(8,128)(2,1)S(1)}, u32[]{:S(2)}, u32[]{:S(2)}) collective-permute-start(bf16[544,128]{1,0:T(8,128)(2,1)} %copy-done.24), channel_id=1, source_target_pairs={{0,6},{1,25},{2,0},{3,27},{4,2},{5,29},{6,4},{7,31},{8,14},{9,1},{... | collective-permute-start | bytes 417800 | tf_op jit(solution)/shard_map/ppermute | solution.py:605
  86.5 5.7 %collective-permute-start.13 = (bf16[544,128]{1,0:T(8,128)(2,1)}, bf16[544,128]{1,0:T(8,128)(2,1)S(1)}, u32[]{:S(2)}, u32[]{:S(2)}) collective-permute-start(bf16[544,128]{1,0:T(8,128)(2,1)} %copy-done.23), channel_id=1, source_target_pairs={{0,4},{1,17},{2,6},{3,19},{4,0},{5,21},{6,2},{7,23},{8,12},{9,25},... | collective-permute-start | bytes 417800 | tf_op jit(solution)/shard_map/ppermute | solution.py:605
  86.5 6.8 %collective-permute-start.14 = (bf16[544,128]{1,0:T(8,128)(2,1)}, bf16[544,128]{1,0:T(8,128)(2,1)S(1)}, u32[]{:S(2)}, u32[]{:S(2)}) collective-permute-start(bf16[544,128]{1,0:T(8,128)(2,1)} %copy-done.22), channel_id=1, source_target_pairs={{0,2},{1,9},{2,4},{3,11},{4,6},{5,13},{6,0},{7,15},{8,10},{9,17},{... | collective-permute-start | bytes 417800 | tf_op jit(solution)/shard_map/ppermute | solution.py:605
  93.5 2.2 %copy-start.2 = (bf16[512,4096]{1,0:T(8,128)(2,1)S(1)}, bf16[512,4096]{1,0:T(8,128)(2,1)}, u32[]{:S(2)}) copy-start(bf16[512,4096]{1,0:T(8,128)(2,1)} %weight.1) | copy-start | bytes 12582916
  95.7 0.9 copy-start.6
  96.6 0.9 copy-start.7
  97.6 0.7 copy-start.16
  99.6 9.2 %collective-permute-start.15 = (bf16[128,1024]{1,0:T(8,128)(2,1)S(1)}, bf16[128,1024]{1,0:T(8,128)(2,1)S(1)}, u32[]{:S(2)}, u32[]{:S(2)}) collective-permute-start(bf16[128,1024]{1,0:T(8,128)(2,1)S(1)} %get-tuple-element.53), channel_id=1, source_target_pairs={{0,32},{32,64},{64,96},{96,0},{1,33},{33,65},{65,97},{97,1},{2,34}... | collective-permute-start | bytes 786440 | tf_op jit(solution)/shard_map/ppermute | solution.py:668
  99.9 16.3 %collective-permute-start.16 = (bf16[128,1024]{1,0:T(8,128)(2,1)S(1)}, bf16[128,1024]{1,0:T(8,128)(2,1)S(1)}, u32[]{:S(2)}, u32[]{:S(2)}) collective-permute-start(bf16[128,1024]{1,0:T(8,128)(2,1)S(1)} %get-tuple-element.54), channel_id=1, source_target_pairs={{0,64},{32,96},{64,0},{96,32},{1,65},{33,97},{65,1},{97,33},{2,66}... | collective-permute-start | bytes 786440 | tf_op jit(solution)/shard_map/ppermute | solution.py:668
  103.7 12.4 %collective-permute-start.17 = (bf16[128,1024]{1,0:T(8,128)(2,1)S(1)}, bf16[128,1024]{1,0:T(8,128)(2,1)S(1)}, u32[]{:S(2)}, u32[]{:S(2)}) collective-permute-start(bf16[128,1024]{1,0:T(8,128)(2,1)S(1)} %get-tuple-element.55), channel_id=1, source_target_pairs={{0,96},{32,0},{64,32},{96,64},{1,97},{33,1},{65,33},{97,65},{2,98}... | collective-permute-start | bytes 786440 | tf_op jit(solution)/shard_map/ppermute | solution.py:668
  116.9 18.1 %copy-start.19 = (f32[4096]{0:T(1024)S(1)}, f32[4096]{0:T(1024)}, u32[]{:S(2)}) copy-start(f32[4096]{0:T(1024)} %gain.1) | copy-start | bytes 49156
  116.9 18.1 %copy-start.20 = (f32[4096]{0:T(1024)S(1)}, f32[4096]{0:T(1024)}, u32[]{:S(2)}) copy-start(f32[4096]{0:T(1024)} %shift.1) | copy-start | bytes 49156
  116.9 18.1 %copy-start.21 = (f32[1536]{0:T(1024)S(1)}, f32[1536]{0:T(1024)}, u32[]{:S(2)}) copy-start(f32[1536]{0:T(1024)} %bias.3) | copy-start | bytes 18436
  116.9 7.7 %collective-permute-start.20 = (bf16[128,1024]{1,0:T(8,128)(2,1)}, bf16[128,1024]{1,0:T(8,128)(2,1)S(1)}, u32[]{:S(2)}, u32[]{:S(2)}) collective-permute-start(bf16[128,1024]{1,0:T(8,128)(2,1)} %join_shares.1.x0), channel_id=1, source_target_pairs={{0,96},{32,0},{64,32},{96,64},{1,97},{33,1},{65,33},{97,65},{2,98}... | collective-permute-start | bytes 786440 | tf_op jit(solution)/shard_map/ppermute | solution.py:671
  118.8 8.8 %collective-permute-start.19 = (bf16[128,1024]{1,0:T(8,128)(2,1)}, bf16[128,1024]{1,0:T(8,128)(2,1)S(1)}, u32[]{:S(2)}, u32[]{:S(2)}) collective-permute-start(bf16[128,1024]{1,0:T(8,128)(2,1)} %join_shares.1.x0), channel_id=1, source_target_pairs={{0,64},{32,96},{64,0},{96,32},{1,65},{33,97},{65,1},{97,33},{2,66}... | collective-permute-start | bytes 786440 | tf_op jit(solution)/shard_map/ppermute | solution.py:671
  119.5 14.8 %collective-permute-start.18 = (bf16[128,1024]{1,0:T(8,128)(2,1)}, bf16[128,1024]{1,0:T(8,128)(2,1)S(1)}, u32[]{:S(2)}, u32[]{:S(2)}) collective-permute-start(bf16[128,1024]{1,0:T(8,128)(2,1)} %join_shares.1.x0), channel_id=1, source_target_pairs={{0,32},{32,64},{64,96},{96,0},{1,33},{33,65},{65,97},{97,1},{2,34}... | collective-permute-start | bytes 786440 | tf_op jit(solution)/shard_map/ppermute | solution.py:671
  119.5 23.0 %copy-start.18 = (s32[8,36]{1,0:T(8,128)S(1)}, s32[8,36]{1,0:T(8,128)}, u32[]{:S(2)}) copy-start(s32[8,36]{1,0:T(8,128)} %table.3) | copy-start | bytes 3460
  124.6 0.7 copy-start.8
  127.6 0.7 copy-start.10
  134.3 0.7 copy-start.12
  135.1 1.0 copy-start.4
  136.0 0.9 copy-start.9
  137.0 0.9 copy-start.11
  137.9 0.9 copy-start.13
  138.9 3.7 %copy-start.3 = (bf16[2048,1024]{1,0:T(8,128)(2,1)S(1)}, bf16[2048,1024]{1,0:T(8,128)(2,1)}, u32[]{:S(2)}) copy-start(bf16[2048,1024]{1,0:T(8,128)(2,1)} %all-gather.3.cloned.1.call-done) | copy-start | bytes 12582916
Sparse Core Ops, SparseCore 0:
  10.7 72.5 all-gather.2

commit v2 on v1

--- a/solution.py
+++ b/solution.py
@@ -93,7 +93,7 @@
         out_shape=jax.ShapeDtypeStruct((len(parts),) + parts[0].shape, parts[0].dtype),
         in_specs=[whole()] * len(parts),
         out_specs=whole(),
-        compiler_params=limit(6),
+        compiler_params=limit(12),
         name="stack",
     )(*parts)
 
@@ -101,9 +101,41 @@
 LIST = 32
 
 
-def pool_kernel(info, lens, table, k_other, v_other, keys, values, codes, counts, sems):
-    page = info[0]
-    chip = lax.div(page, 2)
+def list_kernel(info, lens, table, codes, counts):
+    core = info[3]
+    first_slot = 2 * SLOTS * lax.div(info[0], 2)
+    own_first = SLOTS * core
+
+    def scan_request(request, carry):
+        length = lens[request]
+        found = jnp.int32(0)
+        for g in range(LIST):
+            slot = table[request, g] - first_slot
+            here = (slot >= 0) & (slot < 2 * SLOTS) & (g * PT < length)
+            local = slot - own_first
+            codes[request, found] = g * LIST + jnp.where(local < 0, local + 2 * SLOTS, local)
+            found = found + here.astype(jnp.int32)
+        counts[request] = found
+        return carry
+
+    lax.fori_loop(0, REQS, scan_request, 0)
+
+
+def page_lists(info, lens, table):
+    return pl.pallas_call(
+        list_kernel,
+        out_shape=(
+            jax.ShapeDtypeStruct((REQS, LIST + 1), jnp.int32),
+            jax.ShapeDtypeStruct((REQS,), jnp.int32),
+        ),
+        in_specs=[whole(SMEM)] * 3,
+        out_specs=(whole(SMEM), whole(SMEM)),
+        compiler_params=limit(1),
+        name="page_lists",
+    )(info, lens, table)
+
+
+def pool_kernel(k_other, v_other, keys, values, sems):
     copies = [
         pltpu.make_async_copy(src.at[i], dst.at[i], sems.at[n, i])
         for n, (src, dst) in enumerate(((k_other, keys), (v_other, values)))
@@ -111,46 +143,21 @@
     ]
     for copy in copies:
         copy.start()
-
-    def scan_request(request, carry):
-        def scan(g, n):
-            slot = table[request, g]
-            device = lax.div(slot, SLOTS)
-            here = lax.div(device, 2) == chip
-
-            @pl.when(here)
-            def _():
-                local = slot - device * SLOTS
-                local = jnp.where(device == page, local, local + SLOTS)
-                codes[request, n] = g * LIST + local
-
-            return n + here.astype(jnp.int32)
-
-        used = lax.div(lens[request] + (PT - 1), PT)
-        counts[request] = lax.fori_loop(0, used, scan, jnp.int32(0))
-        return carry
-
-    lax.fori_loop(0, REQS, scan_request, 0)
     for copy in copies:
         copy.wait()
 
 
-def pool(info, lens, table, k_other, v_other):
+def pool(k_other, v_other):
     shape = jax.ShapeDtypeStruct(k_other.shape, BF16)
     return pl.pallas_call(
         pool_kernel,
-        out_shape=(
-            shape,
-            shape,
-            jax.ShapeDtypeStruct((REQS, LIST), jnp.int32),
-            jax.ShapeDtypeStruct((REQS,), jnp.int32),
-        ),
-        in_specs=[whole(SMEM)] * 3 + [whole(HBM)] * 2,
-        out_specs=(whole(), whole(), whole(SMEM), whole(SMEM)),
+        out_shape=(shape, shape),
+        in_specs=[whole(HBM)] * 2,
+        out_specs=(whole(), whole()),
         scratch_shapes=[pltpu.SemaphoreType.DMA((2, SLOTS))],
         compiler_params=limit(8),
         name="pool",
-    )(info, lens, table, k_other, v_other)
+    )(k_other, v_other)
 
 
 PARTS = 32
@@ -464,6 +471,8 @@
     news = refs[0:2]
     k_in, v_in, k_out, v_out, src, kbuf, vbuf, sems, bulk, slots, offsets = refs[2:]
     page = info[0]
+    y = info[1]
+    x = info[2]
     core = info[3]
     whole_copies = (
         pltpu.make_async_copy(k_in, k_out, bulk.at[0]),
@@ -472,9 +481,9 @@
     for copy in whole_copies:
         copy.start()
 
-    def source(n, half, ref, block):
+    def source(n, half, ref, outer, inner):
         return pltpu.make_async_copy(
-            ref.at[block], src.at[n, pl.ds(half * TOK, TOK), :], sems.at[n, half]
+            ref.at[outer, inner], src.at[n, pl.ds(half * TOK, TOK), :], sems.at[n, half]
         )
 
     def loads(n, local):
@@ -507,18 +516,22 @@
                 offsets[n] = offset
                 for copy in loads(n, local):
                     copy.start()
+                row_shift = lax.bitwise_and(y - lax.div(request, 2), 3)
                 for half in range(2):
                     block = jnp.clip(lower + half, 0, 3)
-                    chip = 2 * request + lax.div(block, 2)
-                    mine = lax.rem(block, 2) == core
-
-                    @pl.when(mine)
-                    def _(half=half, chip=chip):
-                        source(n, half, news[0], chip).start()
-
-                    @pl.when(jnp.logical_not(mine))
-                    def _(half=half, chip=chip):
-                        source(n, half, news[1], chip).start()
+                    column = 2 * lax.rem(request, 2) + lax.div(block, 2)
+                    column_shift = lax.bitwise_and(x - column, 3)
+                    origin = lax.rem(block, 2)
+                    inner = jnp.where(origin == 0, column_shift, row_shift)
+                    outer = jnp.where(origin == 0, row_shift, column_shift)
+
+                    @pl.when(origin == core)
+                    def _(half=half, outer=outer, inner=inner):
+                        source(n, half, news[0], outer, inner).start()
+
+                    @pl.when(origin != core)
+                    def _(half=half, outer=outer, inner=inner):
+                        source(n, half, news[1], outer, inner).start()
 
             return n + here.astype(jnp.int32)
 
@@ -531,7 +544,7 @@
 
     def update(n, carry):
         for half in range(2):
-            source(n, half, news[0], 0).wait()
+            source(n, half, news[0], 0, 0).wait()
         for copy in loads(n, 0):
             copy.wait()
         offset = offsets[n]
@@ -632,17 +645,18 @@
     rates = jnp.broadcast_to(inverse[:, None], (ROT // 2, TOK))
     queries, fresh = rotary(info, cache_lengths, group_qkv, rates)
 
-    gathered = lax.all_gather(fresh, ("y", "x"), axis=0)
     other_keys = lax.ppermute(key_cache, "core", CORES)
     other_values = lax.ppermute(paged_value_cache, "core", CORES)
     other_fresh = lax.ppermute(fresh, "core", CORES)
     near = [queries] + [send(queries, s, 0) for s in range(1, 4)]
+    codes, counts = page_lists(info, cache_lengths, page_table)
+    pool_keys, pool_values = pool(other_keys, other_values)
+    near, codes, pool_keys = lax.optimization_barrier((near, codes, pool_keys))
     near = stack(near)
     all_queries = [near] + [send(near, s, 1) for s in range(1, 4)]
 
-    pool_keys, pool_values, codes, counts = pool(
-        info, cache_lengths, page_table, other_keys, other_values
-    )
+    late_fresh, _ = lax.optimization_barrier((fresh, near))
+    new_rows = [fresh] + [send(late_fresh, s, 0) for s in range(1, 4)]
     caches = (key_cache, paged_value_cache, pool_keys, pool_values)
 
     partials = [None] * 4
@@ -659,14 +673,23 @@
         last, before = part, s
     partials[before] = send(last, -before, 1)
     blocks = join_rows(partials)
-    blocks, gathered = lax.optimization_barrier((blocks, gathered))
-    news = (gathered, lax.ppermute(gathered, "core", CORES))
+    new_rows = stack(new_rows)
+    blocks, new_rows = lax.optimization_barrier((blocks, new_rows))
+    from_left = send(new_rows, 1, 1)
+    from_right = send(new_rows, 3, 1)
     blocks = [blocks[0]] + [send(blocks[s], -s, 0) for s in range(1, 4)]
     attention = join_last(blocks)
 
     shares = dense(info, attention, dense_weight, dense_bias, hidden, mlp_branch)
     shares = [shares[0]] + [lax.ppermute(shares[s], "head", shift(s)) for s in range(1, 4)]
+    (from_left, from_right, new_rows), _ = lax.optimization_barrier(
+        ((from_left, from_right, new_rows), shares[0])
+    )
+    opposite = send(from_left, 1, 1)
     new_hidden = join_shares(shares)
+    (opposite, new_rows), _ = lax.optimization_barrier(((opposite, new_rows), new_hidden))
+    gathered = stack([new_rows, from_left, opposite, from_right])
+    news = (gathered, lax.ppermute(gathered, "core", CORES))
 
     streams = [new_hidden] + [lax.ppermute(new_hidden, "head", shift(s)) for s in range(1, 4)]
     late_weight, _ = lax.optimization_barrier((qkv_weight, new_hidden))

time: 153 us -> 129 us (0.84); the launches traced: 153 us -> 126 us
  waiting for transfers between devices: 62.5 us -> 47.7 us
  between operations: 14.3 us -> 1.12 us
  local copies, waits for them, and re-layouts: 14.5 us -> 2.57 us
  starting transfers between devices: 29 us -> 40.7 us
  Pallas kernels: 32.2 us -> 34.2 us
    unnamed x50 -> x30, local copies, waits for them, and re-layouts: 14.4 us -> 2.41 us
    ppermute x12 -> x18, starting transfers between devices: 17.2 us -> 24.5 us  [send(): return lax.ppermute(array, PLANE, plane_shift(s, stage))]
    ppermute x12 -> x18, waiting for transfers between devices: 37.6 us -> 31.4 us  [send(): return lax.ppermute(array, PLANE, plane_shift(s, stage))]
    all_gather x1 -> x0, waiting for transfers between devices: 4.19 us -> none  [on_device(): gathered = lax.all_gather(fresh, ('y', 'x'), axis=0)]
    ppermute x3, waiting for transfers between devices: 12.2 us -> 9.4 us  [on_device(): lax.ppermute(shares[s], 'head', shift(s))]
    ppermute x3, waiting for transfers between devices: 8.53 us -> 5.73 us  [on_device(): lax.ppermute(new_hidden, 'head', shift(s))]
    ppermute x1, starting transfers between devices: 0.68 us -> 2.83 us  [on_device(): news = (gathered, lax.ppermute(gathered, 'core', CORES))]
    pallas_call x1 -> x2, Pallas kernels: 7.99 us -> 7.59 us  [the longest x1 4.67 us: pool(): pl.pallas_call(pool_kernel, out_shape=(shape, shape), in_specs=[whole(HBM...]
  transfers between devices with their start and end apart: 23 -> 28, of which waited for: 14 -> 15; matrix products, arithmetic and copies ran while one was open for 0% -> 0% of each run, Pallas kernels for 18% -> 23%
where the time goes in v2:
time: 129 us; the launch traced here: 126 us
  waiting for transfers between devices  47.7 us (37%)
  starting transfers between devices  40.7 us (32%)
  Pallas kernels  34.2 us (27%)
  local copies, waits for them, and re-layouts  2.57 us (2%)
    ppermute x18, waiting for transfers between devices, send(): return lax.ppermute(array, PLANE, plane_shift(s, stage))  31.4 us
    ppermute x18, starting transfers between devices, send(): return lax.ppermute(array, PLANE, plane_shift(s, stage))  24.5 us
    ppermute x3, waiting for transfers between devices, on_device(): lax.ppermute(shares[s], 'head', shift(s))  9.4 us
    pallas_call x4, Pallas kernels, attend(): pl.pallas_call(body, out_shape=jax.ShapeDtypeStruct((4, PIECES, TOK), BF1...  9.21 us
    ppermute x3, waiting for transfers between devices, on_device(): lax.ppermute(new_hidden, 'head', shift(s))  5.73 us
    ppermute x3, starting transfers between devices, on_device(): lax.ppermute(shares[s], 'head', shift(s))  5.72 us
    pallas_call x1, Pallas kernels, load(): pl.pallas_call(load_kernel, out_shape=jax.ShapeDtypeStruct(array.shape, a...  4.84 us
    pallas_call x1, Pallas kernels, pool(): pl.pallas_call(pool_kernel, out_shape=(shape, shape), in_specs=[whole(HBM...  4.67 us
  transfers between devices with their start and end apart: 28, of which 15 were waited for; matrix products, arithmetic and copies ran while one was open for 0% of the time, Pallas kernels for 23%

profile of v2, /device:TPU:1, one launch (start us, length us, event | category | flops | bytes accessed | tf_op | source)
XLA Modules:
  0.0 126.4 jit_solution(14098470686536001006)
XLA Ops:
  0.6 1.5 %collective-permute-start.3 = (bf16[13,128,512]{2,1,0:T(8,128)(2,1)}, bf16[13,128,512]{2,1,0:T(8,128)(2,1)S(1)}, u32[]{:S(2)}, u32[]{:S(2)}) collective-permute-start(bf16[13,128,512]{2,1,0:T(8,128)(2,1)} %refs_2_.1), channel_id=1, source_target_pairs={{0,1},{1,0},{2,3},{3,2},{4,5},{5,4},{6,7},{7,6},{8,9},{9,8},{10,11... | collective-permute-start | bytes 5111816 | tf_op jit(solution)/shard_map/ppermute | solution.py:648
  2.1 0.1 collective-permute-start.4
  2.2 0.1 stack.26.info.refs_0_
  2.3 0.1 broadcast_in_dim.2.rate_ref
  2.4 1.0 copy-done.4
  3.4 0.7 copy-done.7
  4.1 0.8 rotary.1
  4.9 1.4 %collective-permute-start = (bf16[512,128]{1,0:T(8,128)(2,1)S(1)}, bf16[512,128]{1,0:T(8,128)(2,1)S(1)}, u32[]{:S(2)}, u32[]{:S(2)}) collective-permute-start(bf16[512,128]{1,0:T(8,128)(2,1)S(1)} %get-tuple-element.47.refs_0_), channel_id=1, source_target_pairs={{0,2},{1,9},{2,4},{3,11},{4,6},{5,13},{6,0},{7,15},{8,10},{9,17},{... | collective-permute-start | bytes 393224 | tf_op jit(solution)/shard_map/ppermute | solution.py:618
  6.3 2.6 %collective-permute-start.1 = (bf16[512,128]{1,0:T(8,128)(2,1)S(1)}, bf16[512,128]{1,0:T(8,128)(2,1)S(1)}, u32[]{:S(2)}, u32[]{:S(2)}) collective-permute-start(bf16[512,128]{1,0:T(8,128)(2,1)S(1)} %get-tuple-element.47.refs_0_), channel_id=1, source_target_pairs={{0,4},{1,17},{2,6},{3,19},{4,0},{5,21},{6,2},{7,23},{8,12},{9,25},... | collective-permute-start | bytes 393224 | tf_op jit(solution)/shard_map/ppermute | solution.py:618
  8.9 1.1 collective-permute-start.2
  10.0 0.7 copy-done.10
  10.7 2.9 %page_lists.1 = (s32[8,33]{1,0:T(8,128)S(1)}, s32[8]{0:T(128)S(1)}) custom-call(s32[5]{0:T(128)S(1)} %stack.26.info.refs_0_, s32[8]{0:T(128)S(1)} %copy-done.7, s32[8,36]{1,0:T(8,128)S(1)} %copy-done.10), custom_call_target="tpu_custom_call" | custom-call | tf_op jit(solution)/shard_map/page_lists/pallas_call | solution.py:125
  13.6 0.0 copy-start
  13.7 4.7 %pool.1 = (bf16[13,128,512]{2,1,0:T(8,128)(2,1)S(1)}, bf16[13,128,512]{2,1,0:T(8,128)(2,1)S(1)}) custom-call(bf16[13,128,512]{2,1,0:T(8,128)(2,1)S(1)} %collective-permute-done.3.k_other, bf16[13,128,512]{2,1,0:T(8,128)(2,1)S(1)} %collective-permute-done.4.v_other), custom_call_target="tpu_custom_call" | custom-call | tf_op jit(solution)/shard_map/pool/pallas_call | solution.py:152
  18.4 1.3 %collective-permute-start.5 = (bf16[4,512,128]{2,1,0:T(8,128)(2,1)S(1)}, bf16[4,512,128]{2,1,0:T(8,128)(2,1)S(1)}, u32[]{:S(2)}, u32[]{:S(2)}) collective-permute-start(bf16[4,512,128]{2,1,0:T(8,128)(2,1)S(1)} %stack.27.refs_4_), channel_id=1, source_target_pairs={{0,8},{1,3},{2,10},{3,5},{4,12},{5,7},{6,14},{7,1},{8,16},{9,11},{... | collective-permute-start | bytes 1572872 | tf_op jit(solution)/shard_map/ppermute | solution.py:618
  19.7 1.5 %collective-permute-start.7 = (bf16[4,512,128]{2,1,0:T(8,128)(2,1)S(1)}, bf16[4,512,128]{2,1,0:T(8,128)(2,1)S(1)}, u32[]{:S(2)}, u32[]{:S(2)}) collective-permute-start(bf16[4,512,128]{2,1,0:T(8,128)(2,1)S(1)} %stack.27.refs_4_), channel_id=1, source_target_pairs={{0,24},{1,7},{2,26},{3,1},{4,28},{5,3},{6,30},{7,5},{8,0},{9,15},{... | collective-permute-start | bytes 1572872 | tf_op jit(solution)/shard_map/ppermute | solution.py:618
  21.2 1.5 %collective-permute-start.9 = (bf16[4,512,128]{2,1,0:T(8,128)(2,1)S(1)}, bf16[4,512,128]{2,1,0:T(8,128)(2,1)S(1)}, u32[]{:S(2)}, u32[]{:S(2)}) collective-permute-start(bf16[4,512,128]{2,1,0:T(8,128)(2,1)S(1)} %stack.27.refs_4_), channel_id=1, source_target_pairs={{0,16},{1,5},{2,18},{3,7},{4,20},{5,1},{6,22},{7,3},{8,24},{9,13},... | collective-permute-start | bytes 1572872 | tf_op jit(solution)/shard_map/ppermute | solution.py:618
  22.7 2.1 %collective-permute-start.6 = (bf16[128,1024]{1,0:T(8,128)(2,1)S(1)}, bf16[128,1024]{1,0:T(8,128)(2,1)S(1)}, u32[]{:S(2)}, u32[]{:S(2)}) collective-permute-start(bf16[128,1024]{1,0:T(8,128)(2,1)S(1)} %get-tuple-element.66.refs_9_.refs_0_), channel_id=1, source_target_pairs={{0,1},{1,0},{2,3},{3,2},{4,5},{5,4},{6,7},{7,6},{8,9},{9,8},{10,11... | collective-permute-start | bytes 786440 | tf_op jit(solution)/shard_map/ppermute | solution.py:650
  24.8 1.2 collective-permute-done.6.refs_10_
  26.0 2.3 %attend0.1.a_ref = bf16[4,544,128]{2,1,0:T(8,128)(2,1)S(1)} custom-call(s32[5]{0:T(128)S(1)} %stack.26.info.refs_0_, s32[8]{0:T(128)S(1)} %copy-done.8, s32[8,33]{1,0:T(8,128)S(1)} %get-tuple-element.51.refs_2_, s32[8]{0:T(128)S(1)} %get-tuple-element.52.refs_3_, bf16[4,512,128]{2,1,0:T(8,128)(2,1)S(1)} %stack.27.refs_4_, bf16[13,128,512]{2,1,0:T(8,128)(2,1)S(1)} %copy-done, ...), custom_call_target="tpu_custom_call" | custom-call | tf_op jit(solution)/shard_map/attend0/pallas_call | solution.py:321
  28.3 2.3 %attend1.1 = bf16[4,544,128]{2,1,0:T(8,128)(2,1)S(1)} custom-call(s32[5]{0:T(128)S(1)} %stack.26.info.refs_0_, s32[8]{0:T(128)S(1)} %copy-done.8, s32[8,33]{1,0:T(8,128)S(1)} %get-tuple-element.51.refs_2_, s32[8]{0:T(128)S(1)} %get-tuple-element.52.refs_3_, bf16[4,512,128]{2,1,0:T(8,128)(2,1)S(1)} %collective-permute-done.5.refs_4_, ...), custom_call_target="tpu_custom_call" | custom-call | tf_op jit(solution)/shard_map/attend1/pallas_call | solution.py:321
  30.6 5.5 %collective-permute-start.8 = (bf16[4,544,128]{2,1,0:T(8,128)(2,1)S(1)}, bf16[4,544,128]{2,1,0:T(8,128)(2,1)S(1)}, u32[]{:S(2)}, u32[]{:S(2)}) collective-permute-start(bf16[4,544,128]{2,1,0:T(8,128)(2,1)S(1)} %attend1.1), channel_id=1, source_target_pairs={{0,24},{1,7},{2,26},{3,1},{4,28},{5,3},{6,30},{7,5},{8,0},{9,15},{... | collective-permute-start | bytes 1671176 | tf_op jit(solution)/shard_map/ppermute | solution.py:618
  36.1 2.3 %attend3.1 = bf16[4,544,128]{2,1,0:T(8,128)(2,1)S(1)} custom-call(s32[5]{0:T(128)S(1)} %stack.26.info.refs_0_, s32[8]{0:T(128)S(1)} %copy-done.8, s32[8,33]{1,0:T(8,128)S(1)} %get-tuple-element.51.refs_2_, s32[8]{0:T(128)S(1)} %get-tuple-element.52.refs_3_, bf16[4,512,128]{2,1,0:T(8,128)(2,1)S(1)} %collective-permute-done.7.refs_4_, ...), custom_call_target="tpu_custom_call" | custom-call | tf_op jit(solution)/shard_map/attend3/pallas_call | solution.py:321
  38.5 2.3 %attend2.1 = bf16[4,544,128]{2,1,0:T(8,128)(2,1)S(1)} custom-call(s32[5]{0:T(128)S(1)} %stack.26.info.refs_0_, s32[8]{0:T(128)S(1)} %copy-done.8, s32[8,33]{1,0:T(8,128)S(1)} %get-tuple-element.51.refs_2_, s32[8]{0:T(128)S(1)} %get-tuple-element.52.refs_3_, bf16[4,512,128]{2,1,0:T(8,128)(2,1)S(1)} %collective-permute-done.9.refs_4_, ...), custom_call_target="tpu_custom_call" | custom-call | tf_op jit(solution)/shard_map/attend2/pallas_call | solution.py:321
  40.8 0.1 collective-permute-start.10
  40.8 0.1 collective-permute-start.11
  40.9 1.0 collective-permute-start.12
  41.9 1.9 %collective-permute-start.13 = (bf16[128,1024]{1,0:T(8,128)(2,1)S(1)}, bf16[128,1024]{1,0:T(8,128)(2,1)S(1)}, u32[]{:S(2)}, u32[]{:S(2)}) collective-permute-start(bf16[128,1024]{1,0:T(8,128)(2,1)S(1)} %get-tuple-element.66.refs_9_.refs_0_), channel_id=1, source_target_pairs={{0,4},{1,17},{2,6},{3,19},{4,0},{5,21},{6,2},{7,23},{8,12},{9,25},... | collective-permute-start | bytes 786440 | tf_op jit(solution)/shard_map/ppermute | solution.py:618
  43.8 3.7 %collective-permute-done.12.refs_1_ = bf16[128,1024]{1,0:T(8,128)(2,1)S(1)} collective-permute-done((bf16[128,1024]{1,0:T(8,128)(2,1)S(1)}, bf16[128,1024]{1,0:T(8,128)(2,1)S(1)}, u32[]{:S(2)}, u32[]{:S(2)}) %collective-permute-start.12) | collective-permute-done | bytes 262176 | tf_op jit(solution)/shard_map/ppermute | solution.py:618
  47.4 0.6 collective-permute-start.14
  48.1 5.0 %collective-permute-done.13.refs_2_ = bf16[128,1024]{1,0:T(8,128)(2,1)S(1)} collective-permute-done((bf16[128,1024]{1,0:T(8,128)(2,1)S(1)}, bf16[128,1024]{1,0:T(8,128)(2,1)S(1)}, u32[]{:S(2)}, u32[]{:S(2)}) %collective-permute-start.13) | collective-permute-done | bytes 262176 | tf_op jit(solution)/shard_map/ppermute | solution.py:618
  53.0 4.0 %collective-permute-done.14.refs_3_ = bf16[128,1024]{1,0:T(8,128)(2,1)S(1)} collective-permute-done((bf16[128,1024]{1,0:T(8,128)(2,1)S(1)}, bf16[128,1024]{1,0:T(8,128)(2,1)S(1)}, u32[]{:S(2)}, u32[]{:S(2)}) %collective-permute-start.14) | collective-permute-done | bytes 262176 | tf_op jit(solution)/shard_map/ppermute | solution.py:618
  57.1 0.1 stack.28.refs_0_
  57.2 5.2 %collective-permute-done.11.d_ref = bf16[4,544,128]{2,1,0:T(8,128)(2,1)S(1)} collective-permute-done((bf16[4,544,128]{2,1,0:T(8,128)(2,1)S(1)}, bf16[4,544,128]{2,1,0:T(8,128)(2,1)S(1)}, u32[]{:S(2)}, u32[]{:S(2)}) %collective-permute-start.11) | collective-permute-done | bytes 557088 | tf_op jit(solution)/shard_map/ppermute | solution.py:618
  62.4 0.5 join_rows.1
  62.9 4.0 %collective-permute-start.24 = (bf16[4,128,1024]{2,1,0:T(8,128)(2,1)S(1)}, bf16[4,128,1024]{2,1,0:T(8,128)(2,1)S(1)}, u32[]{:S(2)}, u32[]{:S(2)}) collective-permute-start(bf16[4,128,1024]{2,1,0:T(8,128)(2,1)S(1)} %stack.28.refs_0_), channel_id=1, source_target_pairs={{0,8},{1,3},{2,10},{3,5},{4,12},{5,7},{6,14},{7,1},{8,16},{9,11},{... | collective-permute-start | bytes 3145736 | tf_op jit(solution)/shard_map/ppermute | solution.py:618
  66.9 1.2 collective-permute-start.15
  68.1 0.1 collective-permute-start.16
  68.2 0.4 collective-permute-start.17
  68.7 3.3 %collective-permute-done.15.b_ref = bf16[544,128]{1,0:T(8,128)(2,1)S(1)} collective-permute-done((bf16[544,128]{1,0:T(8,128)(2,1)S(1)}, bf16[544,128]{1,0:T(8,128)(2,1)S(1)}, u32[]{:S(2)}, u32[]{:S(2)}) %collective-permute-start.15) | collective-permute-done | bytes 139296 | tf_op jit(solution)/shard_map/ppermute | solution.py:618
  72.0 3.3 %collective-permute-done.16.c_ref = bf16[544,128]{1,0:T(8,128)(2,1)S(1)} collective-permute-done((bf16[544,128]{1,0:T(8,128)(2,1)S(1)}, bf16[544,128]{1,0:T(8,128)(2,1)S(1)}, u32[]{:S(2)}, u32[]{:S(2)}) %collective-permute-start.16) | collective-permute-done | bytes 139296 | tf_op jit(solution)/shard_map/ppermute | solution.py:618
  75.4 1.3 %collective-permute-done.17.d_ref = bf16[544,128]{1,0:T(8,128)(2,1)S(1)} collective-permute-done((bf16[544,128]{1,0:T(8,128)(2,1)S(1)}, bf16[544,128]{1,0:T(8,128)(2,1)S(1)}, u32[]{:S(2)}, u32[]{:S(2)}) %collective-permute-start.17) | collective-permute-done | bytes 139296 | tf_op jit(solution)/shard_map/ppermute | solution.py:618
  76.7 0.2 join_last.1.attention
  76.9 1.3 %dense.1 = (f32[128,1024]{1,0:T(8,128)S(1)}, bf16[128,1024]{1,0:T(8,128)(2,1)S(1)}, bf16[128,1024]{1,0:T(8,128)(2,1)S(1)}, bf16[128,1024]{1,0:T(8,128)(2,1)S(1)}) custom-call(s32[5]{0:T(128)S(1)} %stack.26.info.refs_0_, bf16[128,512]{1,0:T(8,128)(2,1)S(1)} %join_last.1.attention, bf16[512,4096]{1,0:T(8,128)(2,1)S(1)} %copy-done.2, f32[4096]{0:T(1024)S(1)} %copy-done.9, ...), custom_call_target="tpu_custom_call" | custom-call | tf_op jit(solution)/shard_map/dense/pallas_call | solution.py:407
  78.3 3.4 %collective-permute-done.24.refs_1_ = bf16[4,128,1024]{2,1,0:T(8,128)(2,1)S(1)} collective-permute-done((bf16[4,128,1024]{2,1,0:T(8,128)(2,1)S(1)}, bf16[4,128,1024]{2,1,0:T(8,128)(2,1)S(1)}, u32[]{:S(2)}, u32[]{:S(2)}) %collective-permute-start.24) | collective-permute-done | bytes 1048608 | tf_op jit(solution)/shard_map/ppermute | solution.py:618
  81.6 2.2 %collective-permute-done.25.refs_3_ = bf16[4,128,1024]{2,1,0:T(8,128)(2,1)S(1)} collective-permute-done((bf16[4,128,1024]{2,1,0:T(8,128)(2,1)S(1)}, bf16[4,128,1024]{2,1,0:T(8,128)(2,1)S(1)}, u32[]{:S(2)}, u32[]{:S(2)}) %collective-permute-start.25) | collective-permute-done | bytes 1048608 | tf_op jit(solution)/shard_map/ppermute | solution.py:618
  83.8 0.1 collective-permute-start.26
  83.9 1.7 %collective-permute-start.18 = (bf16[128,1024]{1,0:T(8,128)(2,1)S(1)}, bf16[128,1024]{1,0:T(8,128)(2,1)S(1)}, u32[]{:S(2)}, u32[]{:S(2)}) collective-permute-start(bf16[128,1024]{1,0:T(8,128)(2,1)S(1)} %get-tuple-element.72), channel_id=1, source_target_pairs={{0,32},{32,64},{64,96},{96,0},{1,33},{33,65},{65,97},{97,1},{2,34}... | collective-permute-start | bytes 786440 | tf_op jit(solution)/shard_map/ppermute | solution.py:684
  85.6 3.3 %collective-permute-start.19 = (bf16[128,1024]{1,0:T(8,128)(2,1)S(1)}, bf16[128,1024]{1,0:T(8,128)(2,1)S(1)}, u32[]{:S(2)}, u32[]{:S(2)}) collective-permute-start(bf16[128,1024]{1,0:T(8,128)(2,1)S(1)} %get-tuple-element.73), channel_id=1, source_target_pairs={{0,64},{32,96},{64,0},{96,32},{1,65},{33,97},{65,1},{97,33},{2,66}... | collective-permute-start | bytes 786440 | tf_op jit(solution)/shard_map/ppermute | solution.py:684
  88.9 0.7 collective-permute-start.20
  89.6 2.8 %collective-permute-done.18.a = bf16[128,1024]{1,0:T(8,128)(2,1)S(1)} collective-permute-done((bf16[128,1024]{1,0:T(8,128)(2,1)S(1)}, bf16[128,1024]{1,0:T(8,128)(2,1)S(1)}, u32[]{:S(2)}, u32[]{:S(2)}) %collective-permute-start.18) | collective-permute-done | bytes 262176 | tf_op jit(solution)/shard_map/ppermute | solution.py:684
  92.4 6.5 %collective-permute-done.19.b = bf16[128,1024]{1,0:T(8,128)(2,1)S(1)} collective-permute-done((bf16[128,1024]{1,0:T(8,128)(2,1)S(1)}, bf16[128,1024]{1,0:T(8,128)(2,1)S(1)}, u32[]{:S(2)}, u32[]{:S(2)}) %collective-permute-start.19) | collective-permute-done | bytes 262176 | tf_op jit(solution)/shard_map/ppermute | solution.py:684
  99.0 0.1 collective-permute-done.20.c
  99.0 0.8 join_shares.1.x0
  99.9 0.3 stack.29.refs_0_
  100.2 2.8 %collective-permute-start.27 = (bf16[4,4,128,1024]{3,2,1,0:T(8,128)(2,1)S(1)}, bf16[4,4,128,1024]{3,2,1,0:T(8,128)(2,1)S(1)}, u32[]{:S(2)}, u32[]{:S(2)}) collective-permute-start(bf16[4,4,128,1024]{3,2,1,0:T(8,128)(2,1)S(1)} %stack.29.refs_0_), channel_id=1, source_target_pairs={{0,1},{1,0},{2,3},{3,2},{4,5},{5,4},{6,7},{7,6},{8,9},{9,8},{10,11... | collective-permute-start | bytes 12582920 | tf_op jit(solution)/shard_map/ppermute | solution.py:692
  103.0 0.9 collective-permute-start.21
  103.9 2.1 %collective-permute-start.22 = (bf16[128,1024]{1,0:T(8,128)(2,1)S(1)}, bf16[128,1024]{1,0:T(8,128)(2,1)}, u32[]{:S(2)}, u32[]{:S(2)}) collective-permute-start(bf16[128,1024]{1,0:T(8,128)(2,1)S(1)} %copy-done.3), channel_id=1, source_target_pairs={{0,64},{32,96},{64,0},{96,32},{1,65},{33,97},{65,1},{97,33},{2,66}... | collective-permute-start | bytes 786440 | tf_op jit(solution)/shard_map/ppermute | solution.py:694
  106.0 1.1 collective-permute-start.23
  107.0 4.8 %load.1.weight = bf16[4096,1536]{1,0:T(8,128)(2,1)S(1)} custom-call(bf16[4096,1536]{1,0:T(8,128)(2,1)} %src), custom_call_target="tpu_custom_call" | custom-call | tf_op jit(solution)/shard_map/load/pallas_call | solution.py:181
  111.9 5.6 %collective-permute-done.22.x2 = bf16[128,1024]{1,0:T(8,128)(2,1)} collective-permute-done((bf16[128,1024]{1,0:T(8,128)(2,1)S(1)}, bf16[128,1024]{1,0:T(8,128)(2,1)}, u32[]{:S(2)}, u32[]{:S(2)}) %collective-permute-start.22) | collective-permute-done | bytes 262176 | tf_op jit(solution)/shard_map/ppermute | solution.py:694
  117.5 0.1 collective-permute-done.23.x3
  117.6 4.1 %project_qkv.1 = bf16[128,1536]{1,0:T(8,128)(2,1)} custom-call(s32[5]{0:T(128)S(1)} %stack.26.info.refs_0_, bf16[128,1024]{1,0:T(8,128)(2,1)S(1)} %copy-done.3, bf16[128,1024]{1,0:T(8,128)(2,1)S(1)} %collective-permute-done.21.x1, bf16[128,1024]{1,0:T(8,128)(2,1)} %collective-permute-done.22.x2, bf16[128,1024]{1,0:T(8,128)(2,1)} %collective-permute-done.23.x3, ...), custom_call_target="tpu_custom_call" | custom-call | tf_op jit(solution)/shard_map/project_qkv/pallas_call | solution.py:457
  121.8 4.4 %patch.1 = (bf16[13,128,512]{2,1,0:T(8,128)(2,1)}, bf16[13,128,512]{2,1,0:T(8,128)(2,1)}) custom-call(s32[5]{0:T(128)S(1)} %stack.26.info.refs_0_, s32[8]{0:T(128)S(1)} %copy-done.8, s32[8,36]{1,0:T(8,128)S(1)} %copy-done.11, bf16[4,4,128,1024]{3,2,1,0:T(8,128)(2,1)S(1)} %stack.29.refs_0_, bf16[4,4,128,1024]{3,2,1,0:T(8,128)(2,1)S(1)} %collective-permute-done.27.refs_1_, ...), custom_call_target="tpu_custom_call" | custom-call | tf_op jit(solution)/shard_map/patch/pallas_call | solution.py:579
  (42 shorter events, 0.2 us)
Async XLA Ops:
  0.6 13.0 %collective-permute-start.3 = (bf16[13,128,512]{2,1,0:T(8,128)(2,1)}, bf16[13,128,512]{2,1,0:T(8,128)(2,1)S(1)}, u32[]{:S(2)}, u32[]{:S(2)}) collective-permute-start(bf16[13,128,512]{2,1,0:T(8,128)(2,1)} %refs_2_.1), channel_id=1, source_target_pairs={{0,1},{1,0},{2,3},{3,2},{4,5},{5,4},{6,7},{7,6},{8,9},{9,8},{10,11... | collective-permute-start | bytes 5111816 | tf_op jit(solution)/shard_map/ppermute | solution.py:648
  2.1 11.5 %collective-permute-start.4 = (bf16[13,128,512]{2,1,0:T(8,128)(2,1)}, bf16[13,128,512]{2,1,0:T(8,128)(2,1)S(1)}, u32[]{:S(2)}, u32[]{:S(2)}) collective-permute-start(bf16[13,128,512]{2,1,0:T(8,128)(2,1)} %refs_3_.1), channel_id=1, source_target_pairs={{0,1},{1,0},{2,3},{3,2},{4,5},{5,4},{6,7},{7,6},{8,9},{9,8},{10,11... | collective-permute-start | bytes 5111816 | tf_op jit(solution)/shard_map/ppermute | solution.py:649
  2.4 1.0 copy-start.4
  3.4 0.7 copy-start.7
  4.9 13.5 %collective-permute-start = (bf16[512,128]{1,0:T(8,128)(2,1)S(1)}, bf16[512,128]{1,0:T(8,128)(2,1)S(1)}, u32[]{:S(2)}, u32[]{:S(2)}) collective-permute-start(bf16[512,128]{1,0:T(8,128)(2,1)S(1)} %get-tuple-element.47.refs_0_), channel_id=1, source_target_pairs={{0,2},{1,9},{2,4},{3,11},{4,6},{5,13},{6,0},{7,15},{8,10},{9,17},{... | collective-permute-start | bytes 393224 | tf_op jit(solution)/shard_map/ppermute | solution.py:618
  6.3 12.1 %collective-permute-start.1 = (bf16[512,128]{1,0:T(8,128)(2,1)S(1)}, bf16[512,128]{1,0:T(8,128)(2,1)S(1)}, u32[]{:S(2)}, u32[]{:S(2)}) collective-permute-start(bf16[512,128]{1,0:T(8,128)(2,1)S(1)} %get-tuple-element.47.refs_0_), channel_id=1, source_target_pairs={{0,4},{1,17},{2,6},{3,19},{4,0},{5,21},{6,2},{7,23},{8,12},{9,25},... | collective-permute-start | bytes 393224 | tf_op jit(solution)/shard_map/ppermute | solution.py:618
  8.9 9.4 %collective-permute-start.2 = (bf16[512,128]{1,0:T(8,128)(2,1)S(1)}, bf16[512,128]{1,0:T(8,128)(2,1)S(1)}, u32[]{:S(2)}, u32[]{:S(2)}) collective-permute-start(bf16[512,128]{1,0:T(8,128)(2,1)S(1)} %get-tuple-element.47.refs_0_), channel_id=1, source_target_pairs={{0,6},{1,25},{2,0},{3,27},{4,2},{5,29},{6,4},{7,31},{8,14},{9,1},{... | collective-permute-start | bytes 393224 | tf_op jit(solution)/shard_map/ppermute | solution.py:618
  10.0 0.7 copy-start.10
  13.6 12.3 %copy-start = (bf16[13,128,512]{2,1,0:T(8,128)(2,1)S(1)}, bf16[13,128,512]{2,1,0:T(8,128)(2,1)}, u32[]{:S(2)}) copy-start(bf16[13,128,512]{2,1,0:T(8,128)(2,1)} %refs_2_.1) | copy-start | bytes 5111812
  13.6 12.3 %copy-start.1 = (bf16[13,128,512]{2,1,0:T(8,128)(2,1)S(1)}, bf16[13,128,512]{2,1,0:T(8,128)(2,1)}, u32[]{:S(2)}) copy-start(bf16[13,128,512]{2,1,0:T(8,128)(2,1)} %refs_3_.1) | copy-start | bytes 5111812
  13.6 12.3 %copy-start.8 = (s32[8]{0:T(128)S(1)}, s32[8]{0:T(128)}, u32[]{:S(2)}) copy-start(s32[8]{0:T(128)} %lens.5) | copy-start | bytes 100
  18.4 9.9 %collective-permute-start.5 = (bf16[4,512,128]{2,1,0:T(8,128)(2,1)S(1)}, bf16[4,512,128]{2,1,0:T(8,128)(2,1)S(1)}, u32[]{:S(2)}, u32[]{:S(2)}) collective-permute-start(bf16[4,512,128]{2,1,0:T(8,128)(2,1)S(1)} %stack.27.refs_4_), channel_id=1, source_target_pairs={{0,8},{1,3},{2,10},{3,5},{4,12},{5,7},{6,14},{7,1},{8,16},{9,11},{... | collective-permute-start | bytes 1572872 | tf_op jit(solution)/shard_map/ppermute | solution.py:618
  19.7 10.9 %collective-permute-start.7 = (bf16[4,512,128]{2,1,0:T(8,128)(2,1)S(1)}, bf16[4,512,128]{2,1,0:T(8,128)(2,1)S(1)}, u32[]{:S(2)}, u32[]{:S(2)}) collective-permute-start(bf16[4,512,128]{2,1,0:T(8,128)(2,1)S(1)} %stack.27.refs_4_), channel_id=1, source_target_pairs={{0,24},{1,7},{2,26},{3,1},{4,28},{5,3},{6,30},{7,5},{8,0},{9,15},{... | collective-permute-start | bytes 1572872 | tf_op jit(solution)/shard_map/ppermute | solution.py:618
  21.2 17.3 %collective-permute-start.9 = (bf16[4,512,128]{2,1,0:T(8,128)(2,1)S(1)}, bf16[4,512,128]{2,1,0:T(8,128)(2,1)S(1)}, u32[]{:S(2)}, u32[]{:S(2)}) collective-permute-start(bf16[4,512,128]{2,1,0:T(8,128)(2,1)S(1)} %stack.27.refs_4_), channel_id=1, source_target_pairs={{0,16},{1,5},{2,18},{3,7},{4,20},{5,1},{6,22},{7,3},{8,24},{9,13},... | collective-permute-start | bytes 1572872 | tf_op jit(solution)/shard_map/ppermute | solution.py:618
  22.7 3.3 %collective-permute-start.6 = (bf16[128,1024]{1,0:T(8,128)(2,1)S(1)}, bf16[128,1024]{1,0:T(8,128)(2,1)S(1)}, u32[]{:S(2)}, u32[]{:S(2)}) collective-permute-start(bf16[128,1024]{1,0:T(8,128)(2,1)S(1)} %get-tuple-element.66.refs_9_.refs_0_), channel_id=1, source_target_pairs={{0,1},{1,0},{2,3},{3,2},{4,5},{5,4},{6,7},{7,6},{8,9},{9,8},{10,11... | collective-permute-start | bytes 786440 | tf_op jit(solution)/shard_map/ppermute | solution.py:650
  30.6 26.6 %collective-permute-start.8 = (bf16[4,544,128]{2,1,0:T(8,128)(2,1)S(1)}, bf16[4,544,128]{2,1,0:T(8,128)(2,1)S(1)}, u32[]{:S(2)}, u32[]{:S(2)}) collective-permute-start(bf16[4,544,128]{2,1,0:T(8,128)(2,1)S(1)} %attend1.1), channel_id=1, source_target_pairs={{0,24},{1,7},{2,26},{3,1},{4,28},{5,3},{6,30},{7,5},{8,0},{9,15},{... | collective-permute-start | bytes 1671176 | tf_op jit(solution)/shard_map/ppermute | solution.py:618
  40.8 16.4 %collective-permute-start.10 = (bf16[4,544,128]{2,1,0:T(8,128)(2,1)S(1)}, bf16[4,544,128]{2,1,0:T(8,128)(2,1)S(1)}, u32[]{:S(2)}, u32[]{:S(2)}) collective-permute-start(bf16[4,544,128]{2,1,0:T(8,128)(2,1)S(1)} %attend2.1), channel_id=1, source_target_pairs={{0,16},{1,5},{2,18},{3,7},{4,20},{5,1},{6,22},{7,3},{8,24},{9,13},... | collective-permute-start | bytes 1671176 | tf_op jit(solution)/shard_map/ppermute | solution.py:618
  40.8 21.5 %collective-permute-start.11 = (bf16[4,544,128]{2,1,0:T(8,128)(2,1)S(1)}, bf16[4,544,128]{2,1,0:T(8,128)(2,1)S(1)}, u32[]{:S(2)}, u32[]{:S(2)}) collective-permute-start(bf16[4,544,128]{2,1,0:T(8,128)(2,1)S(1)} %attend3.1), channel_id=1, source_target_pairs={{0,8},{1,3},{2,10},{3,5},{4,12},{5,7},{6,14},{7,1},{8,16},{9,11},{... | collective-permute-start | bytes 1671176 | tf_op jit(solution)/shard_map/ppermute | solution.py:618
  40.9 6.5 %collective-permute-start.12 = (bf16[128,1024]{1,0:T(8,128)(2,1)S(1)}, bf16[128,1024]{1,0:T(8,128)(2,1)S(1)}, u32[]{:S(2)}, u32[]{:S(2)}) collective-permute-start(bf16[128,1024]{1,0:T(8,128)(2,1)S(1)} %get-tuple-element.66.refs_9_.refs_0_), channel_id=1, source_target_pairs={{0,2},{1,9},{2,4},{3,11},{4,6},{5,13},{6,0},{7,15},{8,10},{9,17},{... | collective-permute-start | bytes 786440 | tf_op jit(solution)/shard_map/ppermute | solution.py:618
  41.9 11.1 %collective-permute-start.13 = (bf16[128,1024]{1,0:T(8,128)(2,1)S(1)}, bf16[128,1024]{1,0:T(8,128)(2,1)S(1)}, u32[]{:S(2)}, u32[]{:S(2)}) collective-permute-start(bf16[128,1024]{1,0:T(8,128)(2,1)S(1)} %get-tuple-element.66.refs_9_.refs_0_), channel_id=1, source_target_pairs={{0,4},{1,17},{2,6},{3,19},{4,0},{5,21},{6,2},{7,23},{8,12},{9,25},... | collective-permute-start | bytes 786440 | tf_op jit(solution)/shard_map/ppermute | solution.py:618
  47.4 9.6 %collective-permute-start.14 = (bf16[128,1024]{1,0:T(8,128)(2,1)S(1)}, bf16[128,1024]{1,0:T(8,128)(2,1)S(1)}, u32[]{:S(2)}, u32[]{:S(2)}) collective-permute-start(bf16[128,1024]{1,0:T(8,128)(2,1)S(1)} %get-tuple-element.66.refs_9_.refs_0_), channel_id=1, source_target_pairs={{0,6},{1,25},{2,0},{3,27},{4,2},{5,29},{6,4},{7,31},{8,14},{9,1},{... | collective-permute-start | bytes 786440 | tf_op jit(solution)/shard_map/ppermute | solution.py:618
  57.1 19.8 %copy-start.2 = (bf16[512,4096]{1,0:T(8,128)(2,1)S(1)}, bf16[512,4096]{1,0:T(8,128)(2,1)}, u32[]{:S(2)}) copy-start(bf16[512,4096]{1,0:T(8,128)(2,1)} %weight.1) | copy-start | bytes 12582916
  57.1 19.8 %copy-start.5 = (bf16[128,1024]{1,0:T(8,128)(2,1)S(1)}, bf16[128,1024]{1,0:T(8,128)(2,1)}, u32[]{:S(2)}) copy-start(bf16[128,1024]{1,0:T(8,128)(2,1)} %hidden.1) | copy-start | bytes 786436
  57.1 19.8 %copy-start.6 = (bf16[128,1024]{1,0:T(8,128)(2,1)S(1)}, bf16[128,1024]{1,0:T(8,128)(2,1)}, u32[]{:S(2)}) copy-start(bf16[128,1024]{1,0:T(8,128)(2,1)} %branch.1) | copy-start | bytes 786436
  57.2 19.8 %copy-start.9 = (f32[4096]{0:T(1024)S(1)}, f32[4096]{0:T(1024)}, u32[]{:S(2)}) copy-start(f32[4096]{0:T(1024)} %bias.2) | copy-start | bytes 49156
  62.9 18.7 %collective-permute-start.24 = (bf16[4,128,1024]{2,1,0:T(8,128)(2,1)S(1)}, bf16[4,128,1024]{2,1,0:T(8,128)(2,1)S(1)}, u32[]{:S(2)}, u32[]{:S(2)}) collective-permute-start(bf16[4,128,1024]{2,1,0:T(8,128)(2,1)S(1)} %stack.28.refs_0_), channel_id=1, source_target_pairs={{0,8},{1,3},{2,10},{3,5},{4,12},{5,7},{6,14},{7,1},{8,16},{9,11},{... | collective-permute-start | bytes 3145736 | tf_op jit(solution)/shard_map/ppermute | solution.py:618
  66.9 16.9 %collective-permute-start.25 = (bf16[4,128,1024]{2,1,0:T(8,128)(2,1)S(1)}, bf16[4,128,1024]{2,1,0:T(8,128)(2,1)S(1)}, u32[]{:S(2)}, u32[]{:S(2)}) collective-permute-start(bf16[4,128,1024]{2,1,0:T(8,128)(2,1)S(1)} %stack.28.refs_0_), channel_id=1, source_target_pairs={{0,24},{1,7},{2,26},{3,1},{4,28},{5,3},{6,30},{7,5},{8,0},{9,15},{... | collective-permute-start | bytes 3145736 | tf_op jit(solution)/shard_map/ppermute | solution.py:618
  66.9 5.1 %collective-permute-start.15 = (bf16[544,128]{1,0:T(8,128)(2,1)S(1)}, bf16[544,128]{1,0:T(8,128)(2,1)S(1)}, u32[]{:S(2)}, u32[]{:S(2)}) collective-permute-start(bf16[544,128]{1,0:T(8,128)(2,1)S(1)} %get-tuple-element.68), channel_id=1, source_target_pairs={{0,6},{1,25},{2,0},{3,27},{4,2},{5,29},{6,4},{7,31},{8,14},{9,1},{... | collective-permute-start | bytes 417800 | tf_op jit(solution)/shard_map/ppermute | solution.py:618
  68.1 7.3 %collective-permute-start.16 = (bf16[544,128]{1,0:T(8,128)(2,1)S(1)}, bf16[544,128]{1,0:T(8,128)(2,1)S(1)}, u32[]{:S(2)}, u32[]{:S(2)}) collective-permute-start(bf16[544,128]{1,0:T(8,128)(2,1)S(1)} %get-tuple-element.69), channel_id=1, source_target_pairs={{0,4},{1,17},{2,6},{3,19},{4,0},{5,21},{6,2},{7,23},{8,12},{9,25},... | collective-permute-start | bytes 417800 | tf_op jit(solution)/shard_map/ppermute | solution.py:618
  68.2 8.5 %collective-permute-start.17 = (bf16[544,128]{1,0:T(8,128)(2,1)S(1)}, bf16[544,128]{1,0:T(8,128)(2,1)S(1)}, u32[]{:S(2)}, u32[]{:S(2)}) collective-permute-start(bf16[544,128]{1,0:T(8,128)(2,1)S(1)} %get-tuple-element.70), channel_id=1, source_target_pairs={{0,2},{1,9},{2,4},{3,11},{4,6},{5,13},{6,0},{7,15},{8,10},{9,17},{... | collective-permute-start | bytes 417800 | tf_op jit(solution)/shard_map/ppermute | solution.py:618
  83.8 16.0 %collective-permute-start.26 = (bf16[4,128,1024]{2,1,0:T(8,128)(2,1)S(1)}, bf16[4,128,1024]{2,1,0:T(8,128)(2,1)S(1)}, u32[]{:S(2)}, u32[]{:S(2)}) collective-permute-start(bf16[4,128,1024]{2,1,0:T(8,128)(2,1)S(1)} %collective-permute-done.24.refs_1_), channel_id=1, source_target_pairs={{0,8},{1,3},{2,10},{3,5},{4,12},{5,7},{6,14},{7,1},{8,16},{9,11},{... | collective-permute-start | bytes 3145736 | tf_op jit(solution)/shard_map/ppermute | solution.py:618
  83.9 8.5 %collective-permute-start.18 = (bf16[128,1024]{1,0:T(8,128)(2,1)S(1)}, bf16[128,1024]{1,0:T(8,128)(2,1)S(1)}, u32[]{:S(2)}, u32[]{:S(2)}) collective-permute-start(bf16[128,1024]{1,0:T(8,128)(2,1)S(1)} %get-tuple-element.72), channel_id=1, source_target_pairs={{0,32},{32,64},{64,96},{96,0},{1,33},{33,65},{65,97},{97,1},{2,34}... | collective-permute-start | bytes 786440 | tf_op jit(solution)/shard_map/ppermute | solution.py:684
  85.6 13.4 %collective-permute-start.19 = (bf16[128,1024]{1,0:T(8,128)(2,1)S(1)}, bf16[128,1024]{1,0:T(8,128)(2,1)S(1)}, u32[]{:S(2)}, u32[]{:S(2)}) collective-permute-start(bf16[128,1024]{1,0:T(8,128)(2,1)S(1)} %get-tuple-element.73), channel_id=1, source_target_pairs={{0,64},{32,96},{64,0},{96,32},{1,65},{33,97},{65,1},{97,33},{2,66}... | collective-permute-start | bytes 786440 | tf_op jit(solution)/shard_map/ppermute | solution.py:684
  88.9 10.1 %collective-permute-start.20 = (bf16[128,1024]{1,0:T(8,128)(2,1)S(1)}, bf16[128,1024]{1,0:T(8,128)(2,1)S(1)}, u32[]{:S(2)}, u32[]{:S(2)}) collective-permute-start(bf16[128,1024]{1,0:T(8,128)(2,1)S(1)} %get-tuple-element.74), channel_id=1, source_target_pairs={{0,96},{32,0},{64,32},{96,64},{1,97},{33,1},{65,33},{97,65},{2,98}... | collective-permute-start | bytes 786440 | tf_op jit(solution)/shard_map/ppermute | solution.py:684
  99.9 3.2 %copy-start.3 = (bf16[128,1024]{1,0:T(8,128)(2,1)S(1)}, bf16[128,1024]{1,0:T(8,128)(2,1)}, u32[]{:S(2)}) copy-start(bf16[128,1024]{1,0:T(8,128)(2,1)} %join_shares.1.x0) | copy-start | bytes 786436
  100.1 17.5 %copy-start.12 = (f32[4096]{0:T(1024)S(1)}, f32[4096]{0:T(1024)}, u32[]{:S(2)}) copy-start(f32[4096]{0:T(1024)} %gain.1) | copy-start | bytes 49156
  100.1 17.5 %copy-start.13 = (f32[4096]{0:T(1024)S(1)}, f32[4096]{0:T(1024)}, u32[]{:S(2)}) copy-start(f32[4096]{0:T(1024)} %shift.1) | copy-start | bytes 49156
  100.2 17.5 %copy-start.14 = (f32[1536]{0:T(1024)S(1)}, f32[1536]{0:T(1024)}, u32[]{:S(2)}) copy-start(f32[1536]{0:T(1024)} %bias.3) | copy-start | bytes 18436
  100.2 21.6 %collective-permute-start.27 = (bf16[4,4,128,1024]{3,2,1,0:T(8,128)(2,1)S(1)}, bf16[4,4,128,1024]{3,2,1,0:T(8,128)(2,1)S(1)}, u32[]{:S(2)}, u32[]{:S(2)}) collective-permute-start(bf16[4,4,128,1024]{3,2,1,0:T(8,128)(2,1)S(1)} %stack.29.refs_0_), channel_id=1, source_target_pairs={{0,1},{1,0},{2,3},{3,2},{4,5},{5,4},{6,7},{7,6},{8,9},{9,8},{10,11... | collective-permute-start | bytes 12582920 | tf_op jit(solution)/shard_map/ppermute | solution.py:692
  103.0 8.9 %collective-permute-start.21 = (bf16[128,1024]{1,0:T(8,128)(2,1)S(1)}, bf16[128,1024]{1,0:T(8,128)(2,1)S(1)}, u32[]{:S(2)}, u32[]{:S(2)}) collective-permute-start(bf16[128,1024]{1,0:T(8,128)(2,1)S(1)} %copy-done.3), channel_id=1, source_target_pairs={{0,32},{32,64},{64,96},{96,0},{1,33},{33,65},{65,97},{97,1},{2,34}... | collective-permute-start | bytes 786440 | tf_op jit(solution)/shard_map/ppermute | solution.py:694
  103.9 13.7 %collective-permute-start.22 = (bf16[128,1024]{1,0:T(8,128)(2,1)S(1)}, bf16[128,1024]{1,0:T(8,128)(2,1)}, u32[]{:S(2)}, u32[]{:S(2)}) collective-permute-start(bf16[128,1024]{1,0:T(8,128)(2,1)S(1)} %copy-done.3), channel_id=1, source_target_pairs={{0,64},{32,96},{64,0},{96,32},{1,65},{33,97},{65,1},{97,33},{2,66}... | collective-permute-start | bytes 786440 | tf_op jit(solution)/shard_map/ppermute | solution.py:694
  106.0 11.6 %collective-permute-start.23 = (bf16[128,1024]{1,0:T(8,128)(2,1)S(1)}, bf16[128,1024]{1,0:T(8,128)(2,1)}, u32[]{:S(2)}, u32[]{:S(2)}) collective-permute-start(bf16[128,1024]{1,0:T(8,128)(2,1)S(1)} %copy-done.3), channel_id=1, source_target_pairs={{0,96},{32,0},{64,32},{96,64},{1,97},{33,1},{65,33},{97,65},{2,98}... | collective-permute-start | bytes 786440 | tf_op jit(solution)/shard_map/ppermute | solution.py:694
  111.9 9.9 %copy-start.11 = (s32[8,36]{1,0:T(8,128)S(1)}, s32[8,36]{1,0:T(8,128)}, u32[]{:S(2)}) copy-start(s32[8,36]{1,0:T(8,128)} %table.3) | copy-start | bytes 3460

commit v3 on v2

--- a/solution.py
+++ b/solution.py
@@ -431,7 +431,7 @@
     )(*parts)
 
 
-def qkv_kernel(info, x0, x1, x2, x3, gain, shift, weight, bias, out):
+def qkv_kernel(info, token, x0, x1, x2, x3, gain, shift, weight, bias, out):
     head = info[4]
     blocks = (x0, x1, x2, x3)
     total = 0.0
@@ -453,15 +453,15 @@
     out[...] = result.astype(BF16)
 
 
-def project_qkv(info, blocks, gain, shift, weight, bias):
+def project_qkv(info, token, blocks, gain, shift, weight, bias):
     return pl.pallas_call(
         qkv_kernel,
         out_shape=jax.ShapeDtypeStruct((TOK, QW), BF16),
-        in_specs=[whole(SMEM)] + [whole()] * 8,
+        in_specs=[whole(SMEM)] * 2 + [whole()] * 8,
         out_specs=whole(),
         compiler_params=limit(20),
         name="project_qkv",
-    )(info, *blocks, gain, shift, weight, bias)
+    )(info, token, *blocks, gain, shift, weight, bias)
 
 
 WINDOW = 2 * TOK
@@ -469,7 +469,7 @@
 
 def patch_kernel(info, lens, table, *refs):
     news = refs[0:2]
-    k_in, v_in, k_out, v_out, src, kbuf, vbuf, sems, bulk, slots, offsets = refs[2:]
+    k_in, v_in, k_out, v_out, token_out, src, kbuf, vbuf, sems, bulk, slots, offsets = refs[2:]
     page = info[0]
     y = info[1]
     x = info[2]
@@ -516,14 +516,14 @@
                 offsets[n] = offset
                 for copy in loads(n, local):
                     copy.start()
-                row_shift = lax.bitwise_and(y - lax.div(request, 2), 3)
+                row = lax.div(request, 2)
                 for half in range(2):
                     block = jnp.clip(lower + half, 0, 3)
                     column = 2 * lax.rem(request, 2) + lax.div(block, 2)
-                    column_shift = lax.bitwise_and(x - column, 3)
                     origin = lax.rem(block, 2)
-                    inner = jnp.where(origin == 0, column_shift, row_shift)
-                    outer = jnp.where(origin == 0, row_shift, column_shift)
+                    inner = jnp.where(origin == 0, column ^ x, row ^ y)
+                    inner = inner ^ lax.div(inner, 2)
+                    outer = lax.bitwise_and(jnp.where(origin == 0, y - row, x - column), 3)
 
                     @pl.when(origin == core)
                     def _(half=half, outer=outer, inner=inner):
@@ -538,6 +538,7 @@
         return lax.fori_loop(first, last + 1, scan, count)
 
     count = lax.fori_loop(0, REQS, scan_request, jnp.int32(0))
+    token_out[0] = count
     pick_row = lax.broadcasted_iota(jnp.int32, (PT, WINDOW), 0)
     pick_col = lax.broadcasted_iota(jnp.int32, (PT, WINDOW), 1)
     token = lax.broadcasted_iota(jnp.int32, (PT, LW), 0)
@@ -578,9 +579,9 @@
     shape = jax.ShapeDtypeStruct(key_cache.shape, BF16)
     return pl.pallas_call(
         patch_kernel,
-        out_shape=(shape, shape),
+        out_shape=(shape, shape, jax.ShapeDtypeStruct((1,), jnp.int32)),
         in_specs=[whole(SMEM)] * 3 + [whole(HBM)] * 4,
-        out_specs=(whole(HBM), whole(HBM)),
+        out_specs=(whole(HBM), whole(HBM), whole(SMEM)),
         scratch_shapes=[
             VMEM((SLOTS, WINDOW, 2 * LW), BF16),
             VMEM((SLOTS, PT, LW), BF16),
@@ -603,19 +604,23 @@
 CORES = [(0, 1), (1, 0)]
 
 
-def plane_shift(s, stage):
+def plane_pairs(target, stage):
     pairs = []
     for y in range(4):
         for x in range(4):
             for c in range(2):
                 along_x = (c == 0) == (stage == 0)
-                to_y, to_x = (y, (x + s) % 4) if along_x else ((y + s) % 4, x)
+                to_y, to_x = (y, target(x)) if along_x else (target(y), x)
                 pairs.append((y * 8 + x * 2 + c, to_y * 8 + to_x * 2 + c))
     return pairs
 
 
 def send(array, s, stage):
-    return lax.ppermute(array, PLANE, plane_shift(s, stage))
+    return lax.ppermute(array, PLANE, plane_pairs(lambda u: (u + s) % 4, stage))
+
+
+def exchange(array, bits, stage):
+    return lax.ppermute(array, PLANE, plane_pairs(lambda u: u ^ bits, stage))
 
 
 def on_device(
@@ -651,13 +656,17 @@
     near = [queries] + [send(queries, s, 0) for s in range(1, 4)]
     codes, counts = page_lists(info, cache_lengths, page_table)
     pool_keys, pool_values = pool(other_keys, other_values)
-    near, codes, pool_keys = lax.optimization_barrier((near, codes, pool_keys))
+    neighbour = exchange(fresh, 1, 0)
+    near, codes, pool_keys, other_fresh, neighbour = lax.optimization_barrier(
+        (near, codes, pool_keys, other_fresh, neighbour)
+    )
     near = stack(near)
     all_queries = [near] + [send(near, s, 1) for s in range(1, 4)]
 
-    late_fresh, _ = lax.optimization_barrier((fresh, near))
-    new_rows = [fresh] + [send(late_fresh, s, 0) for s in range(1, 4)]
     caches = (key_cache, paged_value_cache, pool_keys, pool_values)
+
+    pair = stack([fresh, neighbour])
+    new_rows = stack([pair, exchange(pair, 3, 0)]).reshape(4, TOK, 2 * LW)
 
     partials = [None] * 4
     last = None
@@ -665,6 +674,8 @@
         wanted = all_queries[s]
         if last is not None:
             wanted, last = lax.optimization_barrier((wanted, last))
+        if s == 1:
+            wanted, new_rows = lax.optimization_barrier((wanted, new_rows))
         part = attend(
             s, info, cache_lengths, (codes, counts), wanted, caches, (fresh, other_fresh)
         )
@@ -672,34 +683,32 @@
             partials[before] = last if before == 0 else send(last, -before, 1)
         last, before = part, s
     partials[before] = send(last, -before, 1)
-    blocks = join_rows(partials)
-    new_rows = stack(new_rows)
-    blocks, new_rows = lax.optimization_barrier((blocks, new_rows))
     from_left = send(new_rows, 1, 1)
     from_right = send(new_rows, 3, 1)
+    partials, from_left, from_right = lax.optimization_barrier((partials, from_left, from_right))
+    blocks = join_rows(partials)
+    blocks, from_left = lax.optimization_barrier((blocks, from_left))
+    opposite = send(from_left, 1, 1)
     blocks = [blocks[0]] + [send(blocks[s], -s, 0) for s in range(1, 4)]
     attention = join_last(blocks)
 
     shares = dense(info, attention, dense_weight, dense_bias, hidden, mlp_branch)
     shares = [shares[0]] + [lax.ppermute(shares[s], "head", shift(s)) for s in range(1, 4)]
-    (from_left, from_right, new_rows), _ = lax.optimization_barrier(
-        ((from_left, from_right, new_rows), shares[0])
+    news = [new_rows, from_left, opposite, from_right]
+    new_hidden = join_shares(shares)
+    news, _ = lax.optimization_barrier((news, new_hidden))
+    gathered = stack(news)
+    news = (gathered, lax.ppermute(gathered, "core", CORES))
+
+    streams = [new_hidden] + [lax.ppermute(new_hidden, "head", shift(s)) for s in range(1, 4)]
+    key_out, value_out, token = patch(
+        info, cache_lengths, page_table, news, key_cache, paged_value_cache
     )
-    opposite = send(from_left, 1, 1)
-    new_hidden = join_shares(shares)
-    (opposite, new_rows), _ = lax.optimization_barrier(((opposite, new_rows), new_hidden))
-    gathered = stack([new_rows, from_left, opposite, from_right])
-    news = (gathered, lax.ppermute(gathered, "core", CORES))
-
-    streams = [new_hidden] + [lax.ppermute(new_hidden, "head", shift(s)) for s in range(1, 4)]
     late_weight, _ = lax.optimization_barrier((qkv_weight, new_hidden))
     next_qkv = project_qkv(
-        info, streams, norm_gain, norm_bias, load(late_weight), qkv_bias
+        info, token, streams, norm_gain, norm_bias, load(late_weight), qkv_bias
     )
 
-    key_out, value_out = patch(
-        info, cache_lengths, page_table, news, key_cache, paged_value_cache
-    )
     return (new_hidden, next_qkv, key_out, value_out)
 
 

time: 129 us -> 123 us (0.953); the launches traced: 126 us -> 122 us
  starting transfers between devices: 40.7 us -> 36 us
  Pallas kernels: 34.2 us -> 36 us
    ppermute x18 -> x17, starting transfers between devices: 24.5 us -> 18.4 us  [the longest x15 14.9 us: send(): return lax.ppermute(array, PLANE, plane_pairs(lambda u: (u + s) % 4, stage))]
    ppermute x1, starting transfers between devices: 2.83 us -> 6.54 us  [on_device(): news = (gathered, lax.ppermute(gathered, 'core', CORES))]
    ppermute x18 -> x17, waiting for transfers between devices: 31.4 us -> 35.1 us  [the longest x15 32.6 us: send(): return lax.ppermute(array, PLANE, plane_pairs(lambda u: (u + s) % 4, stage))]
    ppermute x3, waiting for transfers between devices: 9.4 us -> 5.93 us  [on_device(): lax.ppermute(shares[s], 'head', shift(s))]
    pallas_call x4, Pallas kernels: 9.21 us -> 11.2 us  [attend(): pl.pallas_call(body, out_shape=jax.ShapeDtypeStruct((4, PIECES, TOK), BF1...]
    ppermute x1, starting transfers between devices: 2.1 us -> 0.61 us  [on_device(): other_fresh = lax.ppermute(fresh, 'core', CORES)]
  transfers between devices with their start and end apart: 28 -> 27, of which waited for: 15 -> 10; matrix products, arithmetic and copies ran while one was open for 0% -> 0% of each run, Pallas kernels for 23% -> 25%
where the time goes in v3:
time: 123 us; the launch traced here: 122 us
  waiting for transfers between devices  46.8 us (38%)
  starting transfers between devices  36 us (29%)
  Pallas kernels  36 us (29%)
  local copies, waits for them, and re-layouts  2.57 us (2%)
    ppermute x15, waiting for transfers between devices, send(): return lax.ppermute(array, PLANE, plane_pairs(lambda u: (u + s) % 4, stage))  32.6 us
    ppermute x15, starting transfers between devices, send(): return lax.ppermute(array, PLANE, plane_pairs(lambda u: (u + s) % 4, stage))  14.9 us
    pallas_call x4, Pallas kernels, attend(): pl.pallas_call(body, out_shape=jax.ShapeDtypeStruct((4, PIECES, TOK), BF1...  11.2 us
    ppermute x1, starting transfers between devices, on_device(): news = (gathered, lax.ppermute(gathered, 'core', CORES))  6.54 us
    ppermute x3, waiting for transfers between devices, on_device(): lax.ppermute(shares[s], 'head', shift(s))  5.93 us
    ppermute x3, starting transfers between devices, on_device(): lax.ppermute(shares[s], 'head', shift(s))  5.75 us
    ppermute x3, waiting for transfers between devices, on_device(): lax.ppermute(new_hidden, 'head', shift(s))  5.71 us
    pallas_call x1, Pallas kernels, load(): pl.pallas_call(load_kernel, out_shape=jax.ShapeDtypeStruct(array.shape, a...  4.84 us
  transfers between devices with their start and end apart: 27, of which 10 were waited for; matrix products, arithmetic and copies ran while one was open for 0% of the time, Pallas kernels for 25%

profile of v3, /device:TPU:1, one launch (start us, length us, event | category | flops | bytes accessed | tf_op | source)
XLA Modules:
  0.0 122.3 jit_solution(13577100095321912028)
XLA Ops:
  0.6 1.5 %collective-permute-start.3 = (bf16[13,128,512]{2,1,0:T(8,128)(2,1)}, bf16[13,128,512]{2,1,0:T(8,128)(2,1)S(1)}, u32[]{:S(2)}, u32[]{:S(2)}) collective-permute-start(bf16[13,128,512]{2,1,0:T(8,128)(2,1)} %refs_2_.1), channel_id=1, source_target_pairs={{0,1},{1,0},{2,3},{3,2},{4,5},{5,4},{6,7},{7,6},{8,9},{9,8},{10,11... | collective-permute-start | bytes 5111816 | tf_op jit(solution)/shard_map/ppermute | solution.py:653
  2.1 0.1 collective-permute-start.4
  2.2 0.1 stack.27.info.refs_0_
  2.3 0.1 broadcast_in_dim.2.rate_ref
  2.4 1.0 copy-done.4
  3.4 0.7 copy-done.7
  4.1 0.8 rotary.1
  4.9 1.5 %collective-permute-start.6 = (bf16[128,1024]{1,0:T(8,128)(2,1)S(1)}, bf16[128,1024]{1,0:T(8,128)(2,1)S(1)}, u32[]{:S(2)}, u32[]{:S(2)}) collective-permute-start(bf16[128,1024]{1,0:T(8,128)(2,1)S(1)} %get-tuple-element.56.refs_9_.refs_0_), channel_id=1, source_target_pairs={{0,2},{1,9},{2,0},{3,11},{4,6},{5,13},{6,4},{7,15},{8,10},{9,1},{1... | collective-permute-start | bytes 786440 | tf_op jit(solution)/shard_map/ppermute | solution.py:623
  6.3 0.6 collective-permute-start.5
  6.9 2.7 %collective-permute-start.2 = (bf16[512,128]{1,0:T(8,128)(2,1)S(1)}, bf16[512,128]{1,0:T(8,128)(2,1)S(1)}, u32[]{:S(2)}, u32[]{:S(2)}) collective-permute-start(bf16[512,128]{1,0:T(8,128)(2,1)S(1)} %get-tuple-element.57.refs_0_), channel_id=1, source_target_pairs={{0,6},{1,25},{2,0},{3,27},{4,2},{5,29},{6,4},{7,31},{8,14},{9,1},{... | collective-permute-start | bytes 393224 | tf_op jit(solution)/shard_map/ppermute | solution.py:619
  9.7 0.3 collective-permute-start.1
  10.0 0.7 collective-permute-start
  10.7 0.7 copy-done.12
  11.4 2.9 %page_lists.1 = (s32[8,33]{1,0:T(8,128)S(1)}, s32[8]{0:T(128)S(1)}) custom-call(s32[5]{0:T(128)S(1)} %stack.27.info.refs_0_, s32[8]{0:T(128)S(1)} %copy-done.7, s32[8,36]{1,0:T(8,128)S(1)} %copy-done.12), custom_call_target="tpu_custom_call" | custom-call | tf_op jit(solution)/shard_map/page_lists/pallas_call | solution.py:125
  14.3 0.0 copy-start.1
  14.3 4.7 %pool.1 = (bf16[13,128,512]{2,1,0:T(8,128)(2,1)S(1)}, bf16[13,128,512]{2,1,0:T(8,128)(2,1)S(1)}) custom-call(bf16[13,128,512]{2,1,0:T(8,128)(2,1)S(1)} %collective-permute-done.3.k_other, bf16[13,128,512]{2,1,0:T(8,128)(2,1)S(1)} %collective-permute-done.4.v_other), custom_call_target="tpu_custom_call" | custom-call | tf_op jit(solution)/shard_map/pool/pallas_call | solution.py:152
  19.0 0.0 copy-start.8
  19.1 0.4 collective-permute-start.7
  19.5 2.0 %collective-permute-start.9 = (bf16[2,128,1024]{2,1,0:T(8,128)(2,1)S(1)}, bf16[2,128,1024]{2,1,0:T(8,128)(2,1)S(1)}, u32[]{:S(2)}, u32[]{:S(2)}) collective-permute-start(bf16[2,128,1024]{2,1,0:T(8,128)(2,1)S(1)} %stack.29.refs_0_), channel_id=1, source_target_pairs={{0,6},{1,25},{2,4},{3,27},{4,2},{5,29},{6,0},{7,31},{8,14},{9,17},... | collective-permute-start | bytes 1572872 | tf_op jit(solution)/shard_map/ppermute | solution.py:623
  21.6 2.4 %collective-permute-start.8 = (bf16[4,512,128]{2,1,0:T(8,128)(2,1)S(1)}, bf16[4,512,128]{2,1,0:T(8,128)(2,1)S(1)}, u32[]{:S(2)}, u32[]{:S(2)}) collective-permute-start(bf16[4,512,128]{2,1,0:T(8,128)(2,1)S(1)} %stack.28.refs_4_), channel_id=1, source_target_pairs={{0,24},{1,7},{2,26},{3,1},{4,28},{5,3},{6,30},{7,5},{8,0},{9,15},{... | collective-permute-start | bytes 1572872 | tf_op jit(solution)/shard_map/ppermute | solution.py:619
  24.0 1.2 %collective-permute-start.11 = (bf16[4,512,128]{2,1,0:T(8,128)(2,1)S(1)}, bf16[4,512,128]{2,1,0:T(8,128)(2,1)S(1)}, u32[]{:S(2)}, u32[]{:S(2)}) collective-permute-start(bf16[4,512,128]{2,1,0:T(8,128)(2,1)S(1)} %stack.28.refs_4_), channel_id=1, source_target_pairs={{0,16},{1,5},{2,18},{3,7},{4,20},{5,1},{6,22},{7,3},{8,24},{9,13},... | collective-permute-start | bytes 1572872 | tf_op jit(solution)/shard_map/ppermute | solution.py:619
  25.2 3.3 %attend0.1.a_ref = bf16[4,544,128]{2,1,0:T(8,128)(2,1)S(1)} custom-call(s32[5]{0:T(128)S(1)} %stack.27.info.refs_0_, s32[8]{0:T(128)S(1)} %copy-done.8, s32[8,33]{1,0:T(8,128)S(1)} %get-tuple-element.61.refs_2_, s32[8]{0:T(128)S(1)} %get-tuple-element.62.refs_3_, bf16[4,512,128]{2,1,0:T(8,128)(2,1)S(1)} %stack.28.refs_4_, bf16[13,128,512]{2,1,0:T(8,128)(2,1)S(1)} %copy-done, ...), custom_call_target="tpu_custom_call" | custom-call | tf_op jit(solution)/shard_map/attend0/pallas_call | solution.py:321
  28.6 8.8 %collective-permute-done.7.refs_4_ = bf16[4,512,128]{2,1,0:T(8,128)(2,1)S(1)} collective-permute-done((bf16[4,512,128]{2,1,0:T(8,128)(2,1)S(1)}, bf16[4,512,128]{2,1,0:T(8,128)(2,1)S(1)}, u32[]{:S(2)}, u32[]{:S(2)}) %collective-permute-start.7) | collective-permute-done | bytes 524320 | tf_op jit(solution)/shard_map/ppermute | solution.py:619
  37.4 2.5 %collective-permute-done.9.refs_1_ = bf16[2,128,1024]{2,1,0:T(8,128)(2,1)S(1)} collective-permute-done((bf16[2,128,1024]{2,1,0:T(8,128)(2,1)S(1)}, bf16[2,128,1024]{2,1,0:T(8,128)(2,1)S(1)}, u32[]{:S(2)}, u32[]{:S(2)}) %collective-permute-start.9) | collective-permute-done | bytes 524320 | tf_op jit(solution)/shard_map/ppermute | solution.py:623
  39.8 0.1 stack.30
  39.9 2.7 %collective-permute-start.15 = (bf16[4,128,1024]{2,1,0:T(8,128)(2,1)S(1)}, bf16[4,128,1024]{2,1,0:T(8,128)(2,1)S(1)}, u32[]{:S(2)}, u32[]{:S(2)}) collective-permute-start(bf16[4,128,1024]{2,1,0:T(8,128)(2,1)S(1)} %bitcast.6), channel_id=1, source_target_pairs={{0,24},{1,7},{2,26},{3,1},{4,28},{5,3},{6,30},{7,5},{8,0},{9,15},{... | collective-permute-start | bytes 3145736 | tf_op jit(solution)/shard_map/ppermute | solution.py:619
  42.6 2.3 %attend1.1 = bf16[4,544,128]{2,1,0:T(8,128)(2,1)S(1)} custom-call(s32[5]{0:T(128)S(1)} %stack.27.info.refs_0_, s32[8]{0:T(128)S(1)} %copy-done.8, s32[8,33]{1,0:T(8,128)S(1)} %get-tuple-element.61.refs_2_, s32[8]{0:T(128)S(1)} %get-tuple-element.62.refs_3_, bf16[4,512,128]{2,1,0:T(8,128)(2,1)S(1)} %collective-permute-done.7.refs_4_, ...), custom_call_target="tpu_custom_call" | custom-call | tf_op jit(solution)/shard_map/attend1/pallas_call | solution.py:321
  44.9 3.3 %attend3.1 = bf16[4,544,128]{2,1,0:T(8,128)(2,1)S(1)} custom-call(s32[5]{0:T(128)S(1)} %stack.27.info.refs_0_, s32[8]{0:T(128)S(1)} %copy-done.8, s32[8,33]{1,0:T(8,128)S(1)} %get-tuple-element.61.refs_2_, s32[8]{0:T(128)S(1)} %get-tuple-element.62.refs_3_, bf16[4,512,128]{2,1,0:T(8,128)(2,1)S(1)} %collective-permute-done.8.refs_4_, ...), custom_call_target="tpu_custom_call" | custom-call | tf_op jit(solution)/shard_map/attend3/pallas_call | solution.py:321
  48.3 2.3 %attend2.1 = bf16[4,544,128]{2,1,0:T(8,128)(2,1)S(1)} custom-call(s32[5]{0:T(128)S(1)} %stack.27.info.refs_0_, s32[8]{0:T(128)S(1)} %copy-done.8, s32[8,33]{1,0:T(8,128)S(1)} %get-tuple-element.61.refs_2_, s32[8]{0:T(128)S(1)} %get-tuple-element.62.refs_3_, bf16[4,512,128]{2,1,0:T(8,128)(2,1)S(1)} %collective-permute-done.11.refs_4_, ...), custom_call_target="tpu_custom_call" | custom-call | tf_op jit(solution)/shard_map/attend2/pallas_call | solution.py:321
  50.6 0.0 copy-start.6
  50.6 0.0 copy-start.9
  50.6 0.1 collective-permute-start.12
  50.7 1.2 %collective-permute-start.13 = (bf16[4,544,128]{2,1,0:T(8,128)(2,1)S(1)}, bf16[4,544,128]{2,1,0:T(8,128)(2,1)S(1)}, u32[]{:S(2)}, u32[]{:S(2)}) collective-permute-start(bf16[4,544,128]{2,1,0:T(8,128)(2,1)S(1)} %attend3.1), channel_id=1, source_target_pairs={{0,8},{1,3},{2,10},{3,5},{4,12},{5,7},{6,14},{7,1},{8,16},{9,11},{... | collective-permute-start | bytes 1671176 | tf_op jit(solution)/shard_map/ppermute | solution.py:619
  51.9 1.5 %collective-permute-start.10 = (bf16[4,544,128]{2,1,0:T(8,128)(2,1)S(1)}, bf16[4,544,128]{2,1,0:T(8,128)(2,1)S(1)}, u32[]{:S(2)}, u32[]{:S(2)}) collective-permute-start(bf16[4,544,128]{2,1,0:T(8,128)(2,1)S(1)} %attend1.1), channel_id=1, source_target_pairs={{0,24},{1,7},{2,26},{3,1},{4,28},{5,3},{6,30},{7,5},{8,0},{9,15},{... | collective-permute-start | bytes 1671176 | tf_op jit(solution)/shard_map/ppermute | solution.py:619
  53.4 9.0 %collective-permute-done.12.c_ref = bf16[4,544,128]{2,1,0:T(8,128)(2,1)S(1)} collective-permute-done((bf16[4,544,128]{2,1,0:T(8,128)(2,1)S(1)}, bf16[4,544,128]{2,1,0:T(8,128)(2,1)S(1)}, u32[]{:S(2)}, u32[]{:S(2)}) %collective-permute-start.12) | collective-permute-done | bytes 557088 | tf_op jit(solution)/shard_map/ppermute | solution.py:619
  62.4 7.3 %collective-permute-done.13.d_ref = bf16[4,544,128]{2,1,0:T(8,128)(2,1)S(1)} collective-permute-done((bf16[4,544,128]{2,1,0:T(8,128)(2,1)S(1)}, bf16[4,544,128]{2,1,0:T(8,128)(2,1)S(1)}, u32[]{:S(2)}, u32[]{:S(2)}) %collective-permute-start.13) | collective-permute-done | bytes 557088 | tf_op jit(solution)/shard_map/ppermute | solution.py:619
  69.7 0.5 join_rows.1
  70.2 0.1 collective-permute-start.22
  70.3 0.1 collective-permute-start.16
  70.3 0.1 collective-permute-start.17
  70.4 1.4 %collective-permute-start.18 = (bf16[544,128]{1,0:T(8,128)(2,1)S(1)}, bf16[544,128]{1,0:T(8,128)(2,1)S(1)}, u32[]{:S(2)}, u32[]{:S(2)}) collective-permute-start(bf16[544,128]{1,0:T(8,128)(2,1)S(1)} %get-tuple-element.87), channel_id=1, source_target_pairs={{0,2},{1,9},{2,4},{3,11},{4,6},{5,13},{6,0},{7,15},{8,10},{9,17},{... | collective-permute-start | bytes 417800 | tf_op jit(solution)/shard_map/ppermute | solution.py:619
  71.8 2.4 %collective-permute-done.16.b_ref = bf16[544,128]{1,0:T(8,128)(2,1)S(1)} collective-permute-done((bf16[544,128]{1,0:T(8,128)(2,1)S(1)}, bf16[544,128]{1,0:T(8,128)(2,1)S(1)}, u32[]{:S(2)}, u32[]{:S(2)}) %collective-permute-start.16) | collective-permute-done | bytes 139296 | tf_op jit(solution)/shard_map/ppermute | solution.py:619
  74.2 3.0 %collective-permute-done.17.c_ref = bf16[544,128]{1,0:T(8,128)(2,1)S(1)} collective-permute-done((bf16[544,128]{1,0:T(8,128)(2,1)S(1)}, bf16[544,128]{1,0:T(8,128)(2,1)S(1)}, u32[]{:S(2)}, u32[]{:S(2)}) %collective-permute-start.17) | collective-permute-done | bytes 139296 | tf_op jit(solution)/shard_map/ppermute | solution.py:619
  77.3 2.1 %collective-permute-done.18.d_ref = bf16[544,128]{1,0:T(8,128)(2,1)S(1)} collective-permute-done((bf16[544,128]{1,0:T(8,128)(2,1)S(1)}, bf16[544,128]{1,0:T(8,128)(2,1)S(1)}, u32[]{:S(2)}, u32[]{:S(2)}) %collective-permute-start.18) | collective-permute-done | bytes 139296 | tf_op jit(solution)/shard_map/ppermute | solution.py:619
  79.3 0.2 join_last.1.attention
  79.6 1.3 %dense.1 = (f32[128,1024]{1,0:T(8,128)S(1)}, bf16[128,1024]{1,0:T(8,128)(2,1)S(1)}, bf16[128,1024]{1,0:T(8,128)(2,1)S(1)}, bf16[128,1024]{1,0:T(8,128)(2,1)S(1)}) custom-call(s32[5]{0:T(128)S(1)} %stack.27.info.refs_0_, bf16[128,512]{1,0:T(8,128)(2,1)S(1)} %join_last.1.attention, bf16[512,4096]{1,0:T(8,128)(2,1)S(1)} %copy-done.2, f32[4096]{0:T(1024)S(1)} %copy-done.9, ...), custom_call_target="tpu_custom_call" | custom-call | tf_op jit(solution)/shard_map/dense/pallas_call | solution.py:407
  80.9 1.7 %collective-permute-start.19 = (bf16[128,1024]{1,0:T(8,128)(2,1)S(1)}, bf16[128,1024]{1,0:T(8,128)(2,1)S(1)}, u32[]{:S(2)}, u32[]{:S(2)}) collective-permute-start(bf16[128,1024]{1,0:T(8,128)(2,1)S(1)} %get-tuple-element.89), channel_id=1, source_target_pairs={{0,32},{32,64},{64,96},{96,0},{1,33},{33,65},{65,97},{97,1},{2,34}... | collective-permute-start | bytes 786440 | tf_op jit(solution)/shard_map/ppermute | solution.py:696
  82.6 3.3 %collective-permute-start.20 = (bf16[128,1024]{1,0:T(8,128)(2,1)S(1)}, bf16[128,1024]{1,0:T(8,128)(2,1)S(1)}, u32[]{:S(2)}, u32[]{:S(2)}) collective-permute-start(bf16[128,1024]{1,0:T(8,128)(2,1)S(1)} %get-tuple-element.90), channel_id=1, source_target_pairs={{0,64},{32,96},{64,0},{96,32},{1,65},{33,97},{65,1},{97,33},{2,66}... | collective-permute-start | bytes 786440 | tf_op jit(solution)/shard_map/ppermute | solution.py:696
  85.9 0.7 collective-permute-start.21
  86.6 2.1 %collective-permute-done.19.a = bf16[128,1024]{1,0:T(8,128)(2,1)S(1)} collective-permute-done((bf16[128,1024]{1,0:T(8,128)(2,1)S(1)}, bf16[128,1024]{1,0:T(8,128)(2,1)S(1)}, u32[]{:S(2)}, u32[]{:S(2)}) %collective-permute-start.19) | collective-permute-done | bytes 262176 | tf_op jit(solution)/shard_map/ppermute | solution.py:696
  88.8 3.8 %collective-permute-done.20.b = bf16[128,1024]{1,0:T(8,128)(2,1)S(1)} collective-permute-done((bf16[128,1024]{1,0:T(8,128)(2,1)S(1)}, bf16[128,1024]{1,0:T(8,128)(2,1)S(1)}, u32[]{:S(2)}, u32[]{:S(2)}) %collective-permute-start.20) | collective-permute-done | bytes 262176 | tf_op jit(solution)/shard_map/ppermute | solution.py:696
  92.6 0.8 join_shares.1.x0
  93.4 0.3 stack.31.refs_0_
  93.7 0.0 copy-start.13
  93.7 6.5 %collective-permute-start.23 = (bf16[4,4,128,1024]{3,2,1,0:T(8,128)(2,1)S(1)}, bf16[4,4,128,1024]{3,2,1,0:T(8,128)(2,1)S(1)}, u32[]{:S(2)}, u32[]{:S(2)}) collective-permute-start(bf16[4,4,128,1024]{3,2,1,0:T(8,128)(2,1)S(1)} %stack.31.refs_0_), channel_id=1, source_target_pairs={{0,1},{1,0},{2,3},{3,2},{4,5},{5,4},{6,7},{7,6},{8,9},{9,8},{10,11... | collective-permute-start | bytes 12582920 | tf_op jit(solution)/shard_map/ppermute | solution.py:701
  100.2 1.9 %collective-permute-start.26 = (bf16[128,1024]{1,0:T(8,128)(2,1)S(1)}, bf16[128,1024]{1,0:T(8,128)(2,1)S(1)}, u32[]{:S(2)}, u32[]{:S(2)}) collective-permute-start(bf16[128,1024]{1,0:T(8,128)(2,1)S(1)} %copy-done.3), channel_id=1, source_target_pairs={{0,96},{32,0},{64,32},{96,64},{1,97},{33,1},{65,33},{97,65},{2,98}... | collective-permute-start | bytes 786440 | tf_op jit(solution)/shard_map/ppermute | solution.py:703
  102.1 1.1 collective-permute-start.25
  103.3 0.1 collective-permute-start.24
  103.3 4.8 %load.1.weight = bf16[4096,1536]{1,0:T(8,128)(2,1)S(1)} custom-call(bf16[4096,1536]{1,0:T(8,128)(2,1)} %src), custom_call_target="tpu_custom_call" | custom-call | tf_op jit(solution)/shard_map/load/pallas_call | solution.py:181
  108.2 0.0 copy-start.10
  108.2 0.0 copy-start.11
  108.2 3.6 %patch.1 = (bf16[13,128,512]{2,1,0:T(8,128)(2,1)}, bf16[13,128,512]{2,1,0:T(8,128)(2,1)}, s32[1]{0:T(128)}) custom-call(s32[5]{0:T(128)S(1)} %stack.27.info.refs_0_, s32[8]{0:T(128)S(1)} %copy-done.8, s32[8,36]{1,0:T(8,128)S(1)} %copy-done.13, bf16[4,4,128,1024]{3,2,1,0:T(8,128)(2,1)S(1)} %stack.31.refs_0_, ...), custom_call_target="tpu_custom_call" | custom-call | tf_op jit(solution)/shard_map/patch/pallas_call | solution.py:580
  111.9 5.7 %collective-permute-done.24.x1 = bf16[128,1024]{1,0:T(8,128)(2,1)} collective-permute-done((bf16[128,1024]{1,0:T(8,128)(2,1)S(1)}, bf16[128,1024]{1,0:T(8,128)(2,1)}, u32[]{:S(2)}, u32[]{:S(2)}) %collective-permute-start.24) | collective-permute-done | bytes 262176 | tf_op jit(solution)/shard_map/ppermute | solution.py:703
  117.6 4.8 %project_qkv.1 = bf16[128,1536]{1,0:T(8,128)(2,1)} custom-call(s32[5]{0:T(128)S(1)} %stack.27.info.refs_0_, s32[1]{0:T(128)} %get-tuple-element.98.token, bf16[128,1024]{1,0:T(8,128)(2,1)S(1)} %copy-done.3, bf16[128,1024]{1,0:T(8,128)(2,1)} %collective-permute-done.24.x1, bf16[128,1024]{1,0:T(8,128)(2,1)} %collective-permute-done.25.x2, ...), custom_call_target="tpu_custom_call" | custom-call | tf_op jit(solution)/shard_map/project_qkv/pallas_call | solution.py:457
  (41 shorter events, 0.2 us)
Async XLA Ops:
  0.6 9.0 %collective-permute-start.3 = (bf16[13,128,512]{2,1,0:T(8,128)(2,1)}, bf16[13,128,512]{2,1,0:T(8,128)(2,1)S(1)}, u32[]{:S(2)}, u32[]{:S(2)}) collective-permute-start(bf16[13,128,512]{2,1,0:T(8,128)(2,1)} %refs_2_.1), channel_id=1, source_target_pairs={{0,1},{1,0},{2,3},{3,2},{4,5},{5,4},{6,7},{7,6},{8,9},{9,8},{10,11... | collective-permute-start | bytes 5111816 | tf_op jit(solution)/shard_map/ppermute | solution.py:653
  2.1 7.9 %collective-permute-start.4 = (bf16[13,128,512]{2,1,0:T(8,128)(2,1)}, bf16[13,128,512]{2,1,0:T(8,128)(2,1)S(1)}, u32[]{:S(2)}, u32[]{:S(2)}) collective-permute-start(bf16[13,128,512]{2,1,0:T(8,128)(2,1)} %refs_3_.1), channel_id=1, source_target_pairs={{0,1},{1,0},{2,3},{3,2},{4,5},{5,4},{6,7},{7,6},{8,9},{9,8},{10,11... | collective-permute-start | bytes 5111816 | tf_op jit(solution)/shard_map/ppermute | solution.py:654
  2.4 1.0 copy-start.4
  3.4 0.7 copy-start.7
  4.9 14.2 %collective-permute-start.6 = (bf16[128,1024]{1,0:T(8,128)(2,1)S(1)}, bf16[128,1024]{1,0:T(8,128)(2,1)S(1)}, u32[]{:S(2)}, u32[]{:S(2)}) collective-permute-start(bf16[128,1024]{1,0:T(8,128)(2,1)S(1)} %get-tuple-element.56.refs_9_.refs_0_), channel_id=1, source_target_pairs={{0,2},{1,9},{2,0},{3,11},{4,6},{5,13},{6,4},{7,15},{8,10},{9,1},{1... | collective-permute-start | bytes 786440 | tf_op jit(solution)/shard_map/ppermute | solution.py:623
  6.3 12.8 %collective-permute-start.5 = (bf16[128,1024]{1,0:T(8,128)(2,1)S(1)}, bf16[128,1024]{1,0:T(8,128)(2,1)S(1)}, u32[]{:S(2)}, u32[]{:S(2)}) collective-permute-start(bf16[128,1024]{1,0:T(8,128)(2,1)S(1)} %get-tuple-element.56.refs_9_.refs_0_), channel_id=1, source_target_pairs={{0,1},{1,0},{2,3},{3,2},{4,5},{5,4},{6,7},{7,6},{8,9},{9,8},{10,11... | collective-permute-start | bytes 786440 | tf_op jit(solution)/shard_map/ppermute | solution.py:655
  6.9 12.1 %collective-permute-start.2 = (bf16[512,128]{1,0:T(8,128)(2,1)S(1)}, bf16[512,128]{1,0:T(8,128)(2,1)S(1)}, u32[]{:S(2)}, u32[]{:S(2)}) collective-permute-start(bf16[512,128]{1,0:T(8,128)(2,1)S(1)} %get-tuple-element.57.refs_0_), channel_id=1, source_target_pairs={{0,6},{1,25},{2,0},{3,27},{4,2},{5,29},{6,4},{7,31},{8,14},{9,1},{... | collective-permute-start | bytes 393224 | tf_op jit(solution)/shard_map/ppermute | solution.py:619
  9.7 9.4 %collective-permute-start.1 = (bf16[512,128]{1,0:T(8,128)(2,1)S(1)}, bf16[512,128]{1,0:T(8,128)(2,1)S(1)}, u32[]{:S(2)}, u32[]{:S(2)}) collective-permute-start(bf16[512,128]{1,0:T(8,128)(2,1)S(1)} %get-tuple-element.57.refs_0_), channel_id=1, source_target_pairs={{0,4},{1,17},{2,6},{3,19},{4,0},{5,21},{6,2},{7,23},{8,12},{9,25},... | collective-permute-start | bytes 393224 | tf_op jit(solution)/shard_map/ppermute | solution.py:619
  10.0 9.0 %collective-permute-start = (bf16[512,128]{1,0:T(8,128)(2,1)S(1)}, bf16[512,128]{1,0:T(8,128)(2,1)S(1)}, u32[]{:S(2)}, u32[]{:S(2)}) collective-permute-start(bf16[512,128]{1,0:T(8,128)(2,1)S(1)} %get-tuple-element.57.refs_0_), channel_id=1, source_target_pairs={{0,2},{1,9},{2,4},{3,11},{4,6},{5,13},{6,0},{7,15},{8,10},{9,17},{... | collective-permute-start | bytes 393224 | tf_op jit(solution)/shard_map/ppermute | solution.py:619
  10.7 0.7 copy-start.12
  14.3 10.9 %copy-start.1 = (bf16[13,128,512]{2,1,0:T(8,128)(2,1)S(1)}, bf16[13,128,512]{2,1,0:T(8,128)(2,1)}, u32[]{:S(2)}) copy-start(bf16[13,128,512]{2,1,0:T(8,128)(2,1)} %refs_3_.1) | copy-start | bytes 5111812
  19.0 6.2 %copy-start = (bf16[13,128,512]{2,1,0:T(8,128)(2,1)S(1)}, bf16[13,128,512]{2,1,0:T(8,128)(2,1)}, u32[]{:S(2)}) copy-start(bf16[13,128,512]{2,1,0:T(8,128)(2,1)} %refs_2_.1) | copy-start | bytes 5111812
  19.0 6.2 %copy-start.8 = (s32[8]{0:T(128)S(1)}, s32[8]{0:T(128)}, u32[]{:S(2)}) copy-start(s32[8]{0:T(128)} %lens.5) | copy-start | bytes 100
  19.1 18.2 %collective-permute-start.7 = (bf16[4,512,128]{2,1,0:T(8,128)(2,1)S(1)}, bf16[4,512,128]{2,1,0:T(8,128)(2,1)S(1)}, u32[]{:S(2)}, u32[]{:S(2)}) collective-permute-start(bf16[4,512,128]{2,1,0:T(8,128)(2,1)S(1)} %stack.28.refs_4_), channel_id=1, source_target_pairs={{0,8},{1,3},{2,10},{3,5},{4,12},{5,7},{6,14},{7,1},{8,16},{9,11},{... | collective-permute-start | bytes 1572872 | tf_op jit(solution)/shard_map/ppermute | solution.py:619
  19.5 20.3 %collective-permute-start.9 = (bf16[2,128,1024]{2,1,0:T(8,128)(2,1)S(1)}, bf16[2,128,1024]{2,1,0:T(8,128)(2,1)S(1)}, u32[]{:S(2)}, u32[]{:S(2)}) collective-permute-start(bf16[2,128,1024]{2,1,0:T(8,128)(2,1)S(1)} %stack.29.refs_0_), channel_id=1, source_target_pairs={{0,6},{1,25},{2,4},{3,27},{4,2},{5,29},{6,0},{7,31},{8,14},{9,17},... | collective-permute-start | bytes 1572872 | tf_op jit(solution)/shard_map/ppermute | solution.py:623
  21.6 23.3 %collective-permute-start.8 = (bf16[4,512,128]{2,1,0:T(8,128)(2,1)S(1)}, bf16[4,512,128]{2,1,0:T(8,128)(2,1)S(1)}, u32[]{:S(2)}, u32[]{:S(2)}) collective-permute-start(bf16[4,512,128]{2,1,0:T(8,128)(2,1)S(1)} %stack.28.refs_4_), channel_id=1, source_target_pairs={{0,24},{1,7},{2,26},{3,1},{4,28},{5,3},{6,30},{7,5},{8,0},{9,15},{... | collective-permute-start | bytes 1572872 | tf_op jit(solution)/shard_map/ppermute | solution.py:619
  24.0 24.3 %collective-permute-start.11 = (bf16[4,512,128]{2,1,0:T(8,128)(2,1)S(1)}, bf16[4,512,128]{2,1,0:T(8,128)(2,1)S(1)}, u32[]{:S(2)}, u32[]{:S(2)}) collective-permute-start(bf16[4,512,128]{2,1,0:T(8,128)(2,1)S(1)} %stack.28.refs_4_), channel_id=1, source_target_pairs={{0,16},{1,5},{2,18},{3,7},{4,20},{5,1},{6,22},{7,3},{8,24},{9,13},... | collective-permute-start | bytes 1572872 | tf_op jit(solution)/shard_map/ppermute | solution.py:619
  39.9 29.8 %collective-permute-start.15 = (bf16[4,128,1024]{2,1,0:T(8,128)(2,1)S(1)}, bf16[4,128,1024]{2,1,0:T(8,128)(2,1)S(1)}, u32[]{:S(2)}, u32[]{:S(2)}) collective-permute-start(bf16[4,128,1024]{2,1,0:T(8,128)(2,1)S(1)} %bitcast.6), channel_id=1, source_target_pairs={{0,24},{1,7},{2,26},{3,1},{4,28},{5,3},{6,30},{7,5},{8,0},{9,15},{... | collective-permute-start | bytes 3145736 | tf_op jit(solution)/shard_map/ppermute | solution.py:619
  42.6 27.1 %collective-permute-start.14 = (bf16[4,128,1024]{2,1,0:T(8,128)(2,1)S(1)}, bf16[4,128,1024]{2,1,0:T(8,128)(2,1)S(1)}, u32[]{:S(2)}, u32[]{:S(2)}) collective-permute-start(bf16[4,128,1024]{2,1,0:T(8,128)(2,1)S(1)} %bitcast.7), channel_id=1, source_target_pairs={{0,8},{1,3},{2,10},{3,5},{4,12},{5,7},{6,14},{7,1},{8,16},{9,11},{... | collective-permute-start | bytes 3145736 | tf_op jit(solution)/shard_map/ppermute | solution.py:619
  48.3 31.3 %copy-start.2 = (bf16[512,4096]{1,0:T(8,128)(2,1)S(1)}, bf16[512,4096]{1,0:T(8,128)(2,1)}, u32[]{:S(2)}) copy-start(bf16[512,4096]{1,0:T(8,128)(2,1)} %weight.1) | copy-start | bytes 12582916
  50.5 29.0 %copy-start.5 = (bf16[128,1024]{1,0:T(8,128)(2,1)S(1)}, bf16[128,1024]{1,0:T(8,128)(2,1)}, u32[]{:S(2)}) copy-start(bf16[128,1024]{1,0:T(8,128)(2,1)} %hidden.1) | copy-start | bytes 786436
  50.6 29.0 %copy-start.6 = (bf16[128,1024]{1,0:T(8,128)(2,1)S(1)}, bf16[128,1024]{1,0:T(8,128)(2,1)}, u32[]{:S(2)}) copy-start(bf16[128,1024]{1,0:T(8,128)(2,1)} %branch.1) | copy-start | bytes 786436
  50.6 29.0 %copy-start.9 = (f32[4096]{0:T(1024)S(1)}, f32[4096]{0:T(1024)}, u32[]{:S(2)}) copy-start(f32[4096]{0:T(1024)} %bias.2) | copy-start | bytes 49156
  50.6 11.8 %collective-permute-start.12 = (bf16[4,544,128]{2,1,0:T(8,128)(2,1)S(1)}, bf16[4,544,128]{2,1,0:T(8,128)(2,1)S(1)}, u32[]{:S(2)}, u32[]{:S(2)}) collective-permute-start(bf16[4,544,128]{2,1,0:T(8,128)(2,1)S(1)} %attend2.1), channel_id=1, source_target_pairs={{0,16},{1,5},{2,18},{3,7},{4,20},{5,1},{6,22},{7,3},{8,24},{9,13},... | collective-permute-start | bytes 1671176 | tf_op jit(solution)/shard_map/ppermute | solution.py:619
  50.7 19.0 %collective-permute-start.13 = (bf16[4,544,128]{2,1,0:T(8,128)(2,1)S(1)}, bf16[4,544,128]{2,1,0:T(8,128)(2,1)S(1)}, u32[]{:S(2)}, u32[]{:S(2)}) collective-permute-start(bf16[4,544,128]{2,1,0:T(8,128)(2,1)S(1)} %attend3.1), channel_id=1, source_target_pairs={{0,8},{1,3},{2,10},{3,5},{4,12},{5,7},{6,14},{7,1},{8,16},{9,11},{... | collective-permute-start | bytes 1671176 | tf_op jit(solution)/shard_map/ppermute | solution.py:619
  51.9 17.8 %collective-permute-start.10 = (bf16[4,544,128]{2,1,0:T(8,128)(2,1)S(1)}, bf16[4,544,128]{2,1,0:T(8,128)(2,1)S(1)}, u32[]{:S(2)}, u32[]{:S(2)}) collective-permute-start(bf16[4,544,128]{2,1,0:T(8,128)(2,1)S(1)} %attend1.1), channel_id=1, source_target_pairs={{0,24},{1,7},{2,26},{3,1},{4,28},{5,3},{6,30},{7,5},{8,0},{9,15},{... | collective-permute-start | bytes 1671176 | tf_op jit(solution)/shard_map/ppermute | solution.py:619
  70.2 23.2 %collective-permute-start.22 = (bf16[4,128,1024]{2,1,0:T(8,128)(2,1)S(1)}, bf16[4,128,1024]{2,1,0:T(8,128)(2,1)S(1)}, u32[]{:S(2)}, u32[]{:S(2)}) collective-permute-start(bf16[4,128,1024]{2,1,0:T(8,128)(2,1)S(1)} %collective-permute-done.14.refs_1_), channel_id=1, source_target_pairs={{0,8},{1,3},{2,10},{3,5},{4,12},{5,7},{6,14},{7,1},{8,16},{9,11},{... | collective-permute-start | bytes 3145736 | tf_op jit(solution)/shard_map/ppermute | solution.py:619
  70.3 4.0 %collective-permute-start.16 = (bf16[544,128]{1,0:T(8,128)(2,1)S(1)}, bf16[544,128]{1,0:T(8,128)(2,1)S(1)}, u32[]{:S(2)}, u32[]{:S(2)}) collective-permute-start(bf16[544,128]{1,0:T(8,128)(2,1)S(1)} %get-tuple-element.85), channel_id=1, source_target_pairs={{0,6},{1,25},{2,0},{3,27},{4,2},{5,29},{6,4},{7,31},{8,14},{9,1},{... | collective-permute-start | bytes 417800 | tf_op jit(solution)/shard_map/ppermute | solution.py:619
  70.3 6.9 %collective-permute-start.17 = (bf16[544,128]{1,0:T(8,128)(2,1)S(1)}, bf16[544,128]{1,0:T(8,128)(2,1)S(1)}, u32[]{:S(2)}, u32[]{:S(2)}) collective-permute-start(bf16[544,128]{1,0:T(8,128)(2,1)S(1)} %get-tuple-element.86), channel_id=1, source_target_pairs={{0,4},{1,17},{2,6},{3,19},{4,0},{5,21},{6,2},{7,23},{8,12},{9,25},... | collective-permute-start | bytes 417800 | tf_op jit(solution)/shard_map/ppermute | solution.py:619
  70.4 8.9 %collective-permute-start.18 = (bf16[544,128]{1,0:T(8,128)(2,1)S(1)}, bf16[544,128]{1,0:T(8,128)(2,1)S(1)}, u32[]{:S(2)}, u32[]{:S(2)}) collective-permute-start(bf16[544,128]{1,0:T(8,128)(2,1)S(1)} %get-tuple-element.87), channel_id=1, source_target_pairs={{0,2},{1,9},{2,4},{3,11},{4,6},{5,13},{6,0},{7,15},{8,10},{9,17},{... | collective-permute-start | bytes 417800 | tf_op jit(solution)/shard_map/ppermute | solution.py:619
  80.9 7.9 %collective-permute-start.19 = (bf16[128,1024]{1,0:T(8,128)(2,1)S(1)}, bf16[128,1024]{1,0:T(8,128)(2,1)S(1)}, u32[]{:S(2)}, u32[]{:S(2)}) collective-permute-start(bf16[128,1024]{1,0:T(8,128)(2,1)S(1)} %get-tuple-element.89), channel_id=1, source_target_pairs={{0,32},{32,64},{64,96},{96,0},{1,33},{33,65},{65,97},{97,1},{2,34}... | collective-permute-start | bytes 786440 | tf_op jit(solution)/shard_map/ppermute | solution.py:696
  82.6 10.0 %collective-permute-start.20 = (bf16[128,1024]{1,0:T(8,128)(2,1)S(1)}, bf16[128,1024]{1,0:T(8,128)(2,1)S(1)}, u32[]{:S(2)}, u32[]{:S(2)}) collective-permute-start(bf16[128,1024]{1,0:T(8,128)(2,1)S(1)} %get-tuple-element.90), channel_id=1, source_target_pairs={{0,64},{32,96},{64,0},{96,32},{1,65},{33,97},{65,1},{97,33},{2,66}... | collective-permute-start | bytes 786440 | tf_op jit(solution)/shard_map/ppermute | solution.py:696
  85.9 6.7 %collective-permute-start.21 = (bf16[128,1024]{1,0:T(8,128)(2,1)S(1)}, bf16[128,1024]{1,0:T(8,128)(2,1)S(1)}, u32[]{:S(2)}, u32[]{:S(2)}) collective-permute-start(bf16[128,1024]{1,0:T(8,128)(2,1)S(1)} %get-tuple-element.91), channel_id=1, source_target_pairs={{0,96},{32,0},{64,32},{96,64},{1,97},{33,1},{65,33},{97,65},{2,98}... | collective-permute-start | bytes 786440 | tf_op jit(solution)/shard_map/ppermute | solution.py:696
  93.4 6.8 %copy-start.3 = (bf16[128,1024]{1,0:T(8,128)(2,1)S(1)}, bf16[128,1024]{1,0:T(8,128)(2,1)}, u32[]{:S(2)}) copy-start(bf16[128,1024]{1,0:T(8,128)(2,1)} %join_shares.1.x0) | copy-start | bytes 786436
  93.7 14.6 %copy-start.13 = (s32[8,36]{1,0:T(8,128)S(1)}, s32[8,36]{1,0:T(8,128)}, u32[]{:S(2)}) copy-start(s32[8,36]{1,0:T(8,128)} %table.3) | copy-start | bytes 3460
  93.7 14.5 %collective-permute-start.23 = (bf16[4,4,128,1024]{3,2,1,0:T(8,128)(2,1)S(1)}, bf16[4,4,128,1024]{3,2,1,0:T(8,128)(2,1)S(1)}, u32[]{:S(2)}, u32[]{:S(2)}) collective-permute-start(bf16[4,4,128,1024]{3,2,1,0:T(8,128)(2,1)S(1)} %stack.31.refs_0_), channel_id=1, source_target_pairs={{0,1},{1,0},{2,3},{3,2},{4,5},{5,4},{6,7},{7,6},{8,9},{9,8},{10,11... | collective-permute-start | bytes 12582920 | tf_op jit(solution)/shard_map/ppermute | solution.py:701
  100.2 11.6 %collective-permute-start.26 = (bf16[128,1024]{1,0:T(8,128)(2,1)S(1)}, bf16[128,1024]{1,0:T(8,128)(2,1)S(1)}, u32[]{:S(2)}, u32[]{:S(2)}) collective-permute-start(bf16[128,1024]{1,0:T(8,128)(2,1)S(1)} %copy-done.3), channel_id=1, source_target_pairs={{0,96},{32,0},{64,32},{96,64},{1,97},{33,1},{65,33},{97,65},{2,98}... | collective-permute-start | bytes 786440 | tf_op jit(solution)/shard_map/ppermute | solution.py:703
  102.1 9.7 %collective-permute-start.25 = (bf16[128,1024]{1,0:T(8,128)(2,1)S(1)}, bf16[128,1024]{1,0:T(8,128)(2,1)}, u32[]{:S(2)}, u32[]{:S(2)}) collective-permute-start(bf16[128,1024]{1,0:T(8,128)(2,1)S(1)} %copy-done.3), channel_id=1, source_target_pairs={{0,64},{32,96},{64,0},{96,32},{1,65},{33,97},{65,1},{97,33},{2,66}... | collective-permute-start | bytes 786440 | tf_op jit(solution)/shard_map/ppermute | solution.py:703
  103.3 14.3 %collective-permute-start.24 = (bf16[128,1024]{1,0:T(8,128)(2,1)S(1)}, bf16[128,1024]{1,0:T(8,128)(2,1)}, u32[]{:S(2)}, u32[]{:S(2)}) collective-permute-start(bf16[128,1024]{1,0:T(8,128)(2,1)S(1)} %copy-done.3), channel_id=1, source_target_pairs={{0,32},{32,64},{64,96},{96,0},{1,33},{33,65},{65,97},{97,1},{2,34}... | collective-permute-start | bytes 786440 | tf_op jit(solution)/shard_map/ppermute | solution.py:703
  108.2 9.4 %copy-start.10 = (f32[4096]{0:T(1024)S(1)}, f32[4096]{0:T(1024)}, u32[]{:S(2)}) copy-start(f32[4096]{0:T(1024)} %gain.1) | copy-start | bytes 49156
  108.2 9.4 %copy-start.11 = (f32[4096]{0:T(1024)S(1)}, f32[4096]{0:T(1024)}, u32[]{:S(2)}) copy-start(f32[4096]{0:T(1024)} %shift.1) | copy-start | bytes 49156
  108.2 9.4 %copy-start.14 = (f32[1536]{0:T(1024)S(1)}, f32[1536]{0:T(1024)}, u32[]{:S(2)}) copy-start(f32[1536]{0:T(1024)} %bias.3) | copy-start | bytes 18436

commit v4 on v3

--- a/solution.py
+++ b/solution.py
@@ -666,7 +666,6 @@
     caches = (key_cache, paged_value_cache, pool_keys, pool_values)
 
     pair = stack([fresh, neighbour])
-    new_rows = stack([pair, exchange(pair, 3, 0)]).reshape(4, TOK, 2 * LW)
 
     partials = [None] * 4
     last = None
@@ -675,6 +674,9 @@
         if last is not None:
             wanted, last = lax.optimization_barrier((wanted, last))
         if s == 1:
+            wanted, pair = lax.optimization_barrier((wanted, pair))
+            new_rows = stack([pair, exchange(pair, 3, 0)]).reshape(4, TOK, 2 * LW)
+        if s == 2:
             wanted, new_rows = lax.optimization_barrier((wanted, new_rows))
         part = attend(
             s, info, cache_lengths, (codes, counts), wanted, caches, (fresh, other_fresh)
@@ -683,17 +685,17 @@
             partials[before] = last if before == 0 else send(last, -before, 1)
         last, before = part, s
     partials[before] = send(last, -before, 1)
+    blocks = join_rows(partials)
+    blocks, new_rows = lax.optimization_barrier((blocks, new_rows))
     from_left = send(new_rows, 1, 1)
     from_right = send(new_rows, 3, 1)
-    partials, from_left, from_right = lax.optimization_barrier((partials, from_left, from_right))
-    blocks = join_rows(partials)
-    blocks, from_left = lax.optimization_barrier((blocks, from_left))
-    opposite = send(from_left, 1, 1)
     blocks = [blocks[0]] + [send(blocks[s], -s, 0) for s in range(1, 4)]
     attention = join_last(blocks)
 
     shares = dense(info, attention, dense_weight, dense_bias, hidden, mlp_branch)
     shares = [shares[0]] + [lax.ppermute(shares[s], "head", shift(s)) for s in range(1, 4)]
+    from_left, from_right, _ = lax.optimization_barrier((from_left, from_right, shares[0]))
+    opposite = send(from_left, 1, 1)
     news = [new_rows, from_left, opposite, from_right]
     new_hidden = join_shares(shares)
     news, _ = lax.optimization_barrier((news, new_hidden))

time: 123 us -> 120 us (0.976)
  waiting for transfers between devices: 46.8 us -> 44.4 us
  starting transfers between devices: 36 us -> 37.8 us
  Pallas kernels: 36 us -> 34.4 us
    ppermute x15, starting transfers between devices: 14.9 us -> 20.4 us  [send(): return lax.ppermute(array, PLANE, plane_pairs(lambda u: (u + s) % 4, stage))]
    ppermute x1, starting transfers between devices: 6.54 us -> 2.61 us  [on_device(): news = (gathered, lax.ppermute(gathered, 'core', CORES))]
    ppermute x15, waiting for transfers between devices: 32.6 us -> 28.9 us  [send(): return lax.ppermute(array, PLANE, plane_pairs(lambda u: (u + s) % 4, stage))]
    ppermute x3, waiting for transfers between devices: 5.93 us -> 9.61 us  [on_device(): lax.ppermute(shares[s], 'head', shift(s))]
    pallas_call x4, Pallas kernels: 11.2 us -> 8.23 us  [attend(): pl.pallas_call(body, out_shape=jax.ShapeDtypeStruct((4, PIECES, TOK), BF1...]
    ppermute x3, waiting for transfers between devices: 5.71 us -> 4.2 us  [on_device(): lax.ppermute(new_hidden, 'head', shift(s))]
    pallas_call x1, Pallas kernels: 3.59 us -> 5 us  [patch(): pl.pallas_call(patch_kernel, out_shape=(shape, shape, jax.ShapeDtypeStruc...]
  transfers between devices with their start and end apart: 27 -> 27, of which waited for: 10 -> 14; matrix products, arithmetic and copies ran while one was open for 0% -> 0% of each run, Pallas kernels for 25% -> 24%
where the time goes in v4:
time: 120 us
  waiting for transfers between devices  44.4 us (37%)
  starting transfers between devices  37.8 us (31%)
  Pallas kernels  34.4 us (29%)
  local copies, waits for them, and re-layouts  2.57 us (2%)
    ppermute x15, waiting for transfers between devices, send(): return lax.ppermute(array, PLANE, plane_pairs(lambda u: (u + s) % 4, stage))  28.9 us
    ppermute x15, starting transfers between devices, send(): return lax.ppermute(array, PLANE, plane_pairs(lambda u: (u + s) % 4, stage))  20.4 us
    ppermute x3, waiting for transfers between devices, on_device(): lax.ppermute(shares[s], 'head', shift(s))  9.61 us
    pallas_call x4, Pallas kernels, attend(): pl.pallas_call(body, out_shape=jax.ShapeDtypeStruct((4, PIECES, TOK), BF1...  8.23 us
    ppermute x3, starting transfers between devices, on_device(): lax.ppermute(shares[s], 'head', shift(s))  5.67 us
    pallas_call x1, Pallas kernels, patch(): pl.pallas_call(patch_kernel, out_shape=(shape, shape, jax.ShapeDtypeStruc...  5 us
    pallas_call x1, Pallas kernels, load(): pl.pallas_call(load_kernel, out_shape=jax.ShapeDtypeStruct(array.shape, a...  4.84 us
    pallas_call x1, Pallas kernels, project_qkv(): pl.pallas_call(qkv_kernel, out_shape=jax.ShapeDtypeStruct((TOK, QW), BF16...  4.75 us
  transfers between devices with their start and end apart: 27, of which 14 were waited for; matrix products, arithmetic and copies ran while one was open for 0% of the time, Pallas kernels for 24%

profile of v4, /device:TPU:1, one launch (start us, length us, event | category | flops | bytes accessed | tf_op | source)
XLA Modules:
  0.0 120.1 jit_solution(10845120138566413305)
XLA Ops:
  0.6 1.5 %collective-permute-start.3 = (bf16[13,128,512]{2,1,0:T(8,128)(2,1)}, bf16[13,128,512]{2,1,0:T(8,128)(2,1)S(1)}, u32[]{:S(2)}, u32[]{:S(2)}) collective-permute-start(bf16[13,128,512]{2,1,0:T(8,128)(2,1)} %refs_2_.1), channel_id=1, source_target_pairs={{0,1},{1,0},{2,3},{3,2},{4,5},{5,4},{6,7},{7,6},{8,9},{9,8},{10,11... | collective-permute-start | bytes 5111816 | tf_op jit(solution)/shard_map/ppermute | solution.py:653
  2.1 0.1 collective-permute-start.4
  2.2 0.1 stack.27.info.refs_0_
  2.3 0.1 broadcast_in_dim.2.rate_ref
  2.4 1.0 copy-done.4
  3.4 0.7 copy-done.7
  4.1 0.8 rotary.1
  4.9 1.5 %collective-permute-start.6 = (bf16[128,1024]{1,0:T(8,128)(2,1)S(1)}, bf16[128,1024]{1,0:T(8,128)(2,1)S(1)}, u32[]{:S(2)}, u32[]{:S(2)}) collective-permute-start(bf16[128,1024]{1,0:T(8,128)(2,1)S(1)} %get-tuple-element.54.refs_9_.refs_0_), channel_id=1, source_target_pairs={{0,2},{1,9},{2,0},{3,11},{4,6},{5,13},{6,4},{7,15},{8,10},{9,1},{1... | collective-permute-start | bytes 786440 | tf_op jit(solution)/shard_map/ppermute | solution.py:623
  6.3 0.6 collective-permute-start.5
  6.9 2.7 %collective-permute-start.2 = (bf16[512,128]{1,0:T(8,128)(2,1)S(1)}, bf16[512,128]{1,0:T(8,128)(2,1)S(1)}, u32[]{:S(2)}, u32[]{:S(2)}) collective-permute-start(bf16[512,128]{1,0:T(8,128)(2,1)S(1)} %get-tuple-element.55.refs_0_), channel_id=1, source_target_pairs={{0,6},{1,25},{2,0},{3,27},{4,2},{5,29},{6,4},{7,31},{8,14},{9,1},{... | collective-permute-start | bytes 393224 | tf_op jit(solution)/shard_map/ppermute | solution.py:619
  9.7 0.3 collective-permute-start.1
  10.0 0.7 collective-permute-start
  10.7 0.7 copy-done.12
  11.4 2.9 %page_lists.1 = (s32[8,33]{1,0:T(8,128)S(1)}, s32[8]{0:T(128)S(1)}) custom-call(s32[5]{0:T(128)S(1)} %stack.27.info.refs_0_, s32[8]{0:T(128)S(1)} %copy-done.7, s32[8,36]{1,0:T(8,128)S(1)} %copy-done.12), custom_call_target="tpu_custom_call" | custom-call | tf_op jit(solution)/shard_map/page_lists/pallas_call | solution.py:125
  14.3 0.0 copy-start.1
  14.3 4.7 %pool.1 = (bf16[13,128,512]{2,1,0:T(8,128)(2,1)S(1)}, bf16[13,128,512]{2,1,0:T(8,128)(2,1)S(1)}) custom-call(bf16[13,128,512]{2,1,0:T(8,128)(2,1)S(1)} %collective-permute-done.3.k_other, bf16[13,128,512]{2,1,0:T(8,128)(2,1)S(1)} %collective-permute-done.4.v_other), custom_call_target="tpu_custom_call" | custom-call | tf_op jit(solution)/shard_map/pool/pallas_call | solution.py:152
  19.0 0.0 copy-start
  19.0 0.0 copy-start.8
  19.1 0.4 collective-permute-start.7
  19.5 2.7 %collective-permute-start.10 = (bf16[4,512,128]{2,1,0:T(8,128)(2,1)S(1)}, bf16[4,512,128]{2,1,0:T(8,128)(2,1)S(1)}, u32[]{:S(2)}, u32[]{:S(2)}) collective-permute-start(bf16[4,512,128]{2,1,0:T(8,128)(2,1)S(1)} %stack.28.refs_4_), channel_id=1, source_target_pairs={{0,16},{1,5},{2,18},{3,7},{4,20},{5,1},{6,22},{7,3},{8,24},{9,13},... | collective-permute-start | bytes 1572872 | tf_op jit(solution)/shard_map/ppermute | solution.py:619
  22.2 1.5 %collective-permute-start.8 = (bf16[4,512,128]{2,1,0:T(8,128)(2,1)S(1)}, bf16[4,512,128]{2,1,0:T(8,128)(2,1)S(1)}, u32[]{:S(2)}, u32[]{:S(2)}) collective-permute-start(bf16[4,512,128]{2,1,0:T(8,128)(2,1)S(1)} %stack.28.refs_4_), channel_id=1, source_target_pairs={{0,24},{1,7},{2,26},{3,1},{4,28},{5,3},{6,30},{7,5},{8,0},{9,15},{... | collective-permute-start | bytes 1572872 | tf_op jit(solution)/shard_map/ppermute | solution.py:619
  23.8 2.3 %attend0.1.a_ref = bf16[4,544,128]{2,1,0:T(8,128)(2,1)S(1)} custom-call(s32[5]{0:T(128)S(1)} %stack.27.info.refs_0_, s32[8]{0:T(128)S(1)} %copy-done.8, s32[8,33]{1,0:T(8,128)S(1)} %get-tuple-element.59.refs_2_, s32[8]{0:T(128)S(1)} %get-tuple-element.60.refs_3_, bf16[4,512,128]{2,1,0:T(8,128)(2,1)S(1)} %stack.28.refs_4_, bf16[13,128,512]{2,1,0:T(8,128)(2,1)S(1)} %copy-done, ...), custom_call_target="tpu_custom_call" | custom-call | tf_op jit(solution)/shard_map/attend0/pallas_call | solution.py:321
  26.1 2.6 %collective-permute-done.7.refs_4_ = bf16[4,512,128]{2,1,0:T(8,128)(2,1)S(1)} collective-permute-done((bf16[4,512,128]{2,1,0:T(8,128)(2,1)S(1)}, bf16[4,512,128]{2,1,0:T(8,128)(2,1)S(1)}, u32[]{:S(2)}, u32[]{:S(2)}) %collective-permute-start.7) | collective-permute-done | bytes 524320 | tf_op jit(solution)/shard_map/ppermute | solution.py:619
  28.7 2.0 %collective-permute-start.11 = (bf16[2,128,1024]{2,1,0:T(8,128)(2,1)S(1)}, bf16[2,128,1024]{2,1,0:T(8,128)(2,1)S(1)}, u32[]{:S(2)}, u32[]{:S(2)}) collective-permute-start(bf16[2,128,1024]{2,1,0:T(8,128)(2,1)S(1)} %stack.29.refs_0_), channel_id=1, source_target_pairs={{0,6},{1,25},{2,4},{3,27},{4,2},{5,29},{6,0},{7,31},{8,14},{9,17},... | collective-permute-start | bytes 1572872 | tf_op jit(solution)/shard_map/ppermute | solution.py:623
  30.7 1.8 %attend1.1 = bf16[4,544,128]{2,1,0:T(8,128)(2,1)S(1)} custom-call(s32[5]{0:T(128)S(1)} %stack.27.info.refs_0_, s32[8]{0:T(128)S(1)} %copy-done.8, s32[8,33]{1,0:T(8,128)S(1)} %get-tuple-element.59.refs_2_, s32[8]{0:T(128)S(1)} %get-tuple-element.60.refs_3_, bf16[4,512,128]{2,1,0:T(8,128)(2,1)S(1)} %collective-permute-done.7.refs_4_, ...), custom_call_target="tpu_custom_call" | custom-call | tf_op jit(solution)/shard_map/attend1/pallas_call | solution.py:321
  32.5 2.4 %collective-permute-done.8.refs_4_ = bf16[4,512,128]{2,1,0:T(8,128)(2,1)S(1)} collective-permute-done((bf16[4,512,128]{2,1,0:T(8,128)(2,1)S(1)}, bf16[4,512,128]{2,1,0:T(8,128)(2,1)S(1)}, u32[]{:S(2)}, u32[]{:S(2)}) %collective-permute-start.8) | collective-permute-done | bytes 524320 | tf_op jit(solution)/shard_map/ppermute | solution.py:619
  35.0 2.3 %attend3.1 = bf16[4,544,128]{2,1,0:T(8,128)(2,1)S(1)} custom-call(s32[5]{0:T(128)S(1)} %stack.27.info.refs_0_, s32[8]{0:T(128)S(1)} %copy-done.8, s32[8,33]{1,0:T(8,128)S(1)} %get-tuple-element.59.refs_2_, s32[8]{0:T(128)S(1)} %get-tuple-element.60.refs_3_, bf16[4,512,128]{2,1,0:T(8,128)(2,1)S(1)} %collective-permute-done.8.refs_4_, ...), custom_call_target="tpu_custom_call" | custom-call | tf_op jit(solution)/shard_map/attend3/pallas_call | solution.py:321
  37.3 2.5 %collective-permute-start.13 = (bf16[4,544,128]{2,1,0:T(8,128)(2,1)S(1)}, bf16[4,544,128]{2,1,0:T(8,128)(2,1)S(1)}, u32[]{:S(2)}, u32[]{:S(2)}) collective-permute-start(bf16[4,544,128]{2,1,0:T(8,128)(2,1)S(1)} %attend3.1), channel_id=1, source_target_pairs={{0,8},{1,3},{2,10},{3,5},{4,12},{5,7},{6,14},{7,1},{8,16},{9,11},{... | collective-permute-start | bytes 1671176 | tf_op jit(solution)/shard_map/ppermute | solution.py:619
  39.8 0.3 collective-permute-start.9
  40.1 1.7 %collective-permute-done.11.refs_1_ = bf16[2,128,1024]{2,1,0:T(8,128)(2,1)S(1)} collective-permute-done((bf16[2,128,1024]{2,1,0:T(8,128)(2,1)S(1)}, bf16[2,128,1024]{2,1,0:T(8,128)(2,1)S(1)}, u32[]{:S(2)}, u32[]{:S(2)}) %collective-permute-start.11) | collective-permute-done | bytes 524320 | tf_op jit(solution)/shard_map/ppermute | solution.py:623
  41.8 0.1 stack.30
  41.8 1.8 %attend2.1 = bf16[4,544,128]{2,1,0:T(8,128)(2,1)S(1)} custom-call(s32[5]{0:T(128)S(1)} %stack.27.info.refs_0_, s32[8]{0:T(128)S(1)} %copy-done.8, s32[8,33]{1,0:T(8,128)S(1)} %get-tuple-element.59.refs_2_, s32[8]{0:T(128)S(1)} %get-tuple-element.60.refs_3_, bf16[4,512,128]{2,1,0:T(8,128)(2,1)S(1)} %collective-permute-done.10.refs_4_, ...), custom_call_target="tpu_custom_call" | custom-call | tf_op jit(solution)/shard_map/attend2/pallas_call | solution.py:321
  43.6 0.0 copy-start.6
  43.6 0.0 copy-start.9
  43.7 5.1 %collective-permute-start.12 = (bf16[4,544,128]{2,1,0:T(8,128)(2,1)S(1)}, bf16[4,544,128]{2,1,0:T(8,128)(2,1)S(1)}, u32[]{:S(2)}, u32[]{:S(2)}) collective-permute-start(bf16[4,544,128]{2,1,0:T(8,128)(2,1)S(1)} %attend2.1), channel_id=1, source_target_pairs={{0,16},{1,5},{2,18},{3,7},{4,20},{5,1},{6,22},{7,3},{8,24},{9,13},... | collective-permute-start | bytes 1671176 | tf_op jit(solution)/shard_map/ppermute | solution.py:619
  48.8 2.9 %collective-permute-done.9.b_ref = bf16[4,544,128]{2,1,0:T(8,128)(2,1)S(1)} collective-permute-done((bf16[4,544,128]{2,1,0:T(8,128)(2,1)S(1)}, bf16[4,544,128]{2,1,0:T(8,128)(2,1)S(1)}, u32[]{:S(2)}, u32[]{:S(2)}) %collective-permute-start.9) | collective-permute-done | bytes 557088 | tf_op jit(solution)/shard_map/ppermute | solution.py:619
  51.7 6.3 %collective-permute-done.12.c_ref = bf16[4,544,128]{2,1,0:T(8,128)(2,1)S(1)} collective-permute-done((bf16[4,544,128]{2,1,0:T(8,128)(2,1)S(1)}, bf16[4,544,128]{2,1,0:T(8,128)(2,1)S(1)}, u32[]{:S(2)}, u32[]{:S(2)}) %collective-permute-start.12) | collective-permute-done | bytes 557088 | tf_op jit(solution)/shard_map/ppermute | solution.py:619
  58.0 0.5 join_rows.1
  58.5 2.1 %collective-permute-start.21 = (bf16[4,128,1024]{2,1,0:T(8,128)(2,1)S(1)}, bf16[4,128,1024]{2,1,0:T(8,128)(2,1)S(1)}, u32[]{:S(2)}, u32[]{:S(2)}) collective-permute-start(bf16[4,128,1024]{2,1,0:T(8,128)(2,1)S(1)} %bitcast.6), channel_id=1, source_target_pairs={{0,24},{1,7},{2,26},{3,1},{4,28},{5,3},{6,30},{7,5},{8,0},{9,15},{... | collective-permute-start | bytes 3145736 | tf_op jit(solution)/shard_map/ppermute | solution.py:619
  60.6 1.2 %collective-permute-start.14 = (bf16[544,128]{1,0:T(8,128)(2,1)S(1)}, bf16[544,128]{1,0:T(8,128)(2,1)S(1)}, u32[]{:S(2)}, u32[]{:S(2)}) collective-permute-start(bf16[544,128]{1,0:T(8,128)(2,1)S(1)} %get-tuple-element.80), channel_id=1, source_target_pairs={{0,6},{1,25},{2,0},{3,27},{4,2},{5,29},{6,4},{7,31},{8,14},{9,1},{... | collective-permute-start | bytes 417800 | tf_op jit(solution)/shard_map/ppermute | solution.py:619
  61.8 0.8 collective-permute-start.16
  62.6 1.9 %collective-permute-done.14.b_ref = bf16[544,128]{1,0:T(8,128)(2,1)S(1)} collective-permute-done((bf16[544,128]{1,0:T(8,128)(2,1)S(1)}, bf16[544,128]{1,0:T(8,128)(2,1)S(1)}, u32[]{:S(2)}, u32[]{:S(2)}) %collective-permute-start.14) | collective-permute-done | bytes 139296 | tf_op jit(solution)/shard_map/ppermute | solution.py:619
  64.5 2.8 %collective-permute-done.15.c_ref = bf16[544,128]{1,0:T(8,128)(2,1)S(1)} collective-permute-done((bf16[544,128]{1,0:T(8,128)(2,1)S(1)}, bf16[544,128]{1,0:T(8,128)(2,1)S(1)}, u32[]{:S(2)}, u32[]{:S(2)}) %collective-permute-start.15) | collective-permute-done | bytes 139296 | tf_op jit(solution)/shard_map/ppermute | solution.py:619
  67.4 1.1 collective-permute-done.16.d_ref
  68.5 0.2 join_last.1.attention
  68.7 1.3 %dense.1 = (f32[128,1024]{1,0:T(8,128)S(1)}, bf16[128,1024]{1,0:T(8,128)(2,1)S(1)}, bf16[128,1024]{1,0:T(8,128)(2,1)S(1)}, bf16[128,1024]{1,0:T(8,128)(2,1)S(1)}) custom-call(s32[5]{0:T(128)S(1)} %stack.27.info.refs_0_, bf16[128,512]{1,0:T(8,128)(2,1)S(1)} %join_last.1.attention, bf16[512,4096]{1,0:T(8,128)(2,1)S(1)} %copy-done.2, f32[4096]{0:T(1024)S(1)} %copy-done.9, ...), custom_call_target="tpu_custom_call" | custom-call | tf_op jit(solution)/shard_map/dense/pallas_call | solution.py:407
  70.0 5.5 %collective-permute-done.21.refs_3_ = bf16[4,128,1024]{2,1,0:T(8,128)(2,1)S(1)} collective-permute-done((bf16[4,128,1024]{2,1,0:T(8,128)(2,1)S(1)}, bf16[4,128,1024]{2,1,0:T(8,128)(2,1)S(1)}, u32[]{:S(2)}, u32[]{:S(2)}) %collective-permute-start.21) | collective-permute-done | bytes 1048608 | tf_op jit(solution)/shard_map/ppermute | solution.py:619
  75.5 3.3 %collective-permute-done.20.refs_1_ = bf16[4,128,1024]{2,1,0:T(8,128)(2,1)S(1)} collective-permute-done((bf16[4,128,1024]{2,1,0:T(8,128)(2,1)S(1)}, bf16[4,128,1024]{2,1,0:T(8,128)(2,1)S(1)}, u32[]{:S(2)}, u32[]{:S(2)}) %collective-permute-start.20) | collective-permute-done | bytes 1048608 | tf_op jit(solution)/shard_map/ppermute | solution.py:619
  78.7 1.6 %collective-permute-start.17 = (bf16[128,1024]{1,0:T(8,128)(2,1)S(1)}, bf16[128,1024]{1,0:T(8,128)(2,1)S(1)}, u32[]{:S(2)}, u32[]{:S(2)}) collective-permute-start(bf16[128,1024]{1,0:T(8,128)(2,1)S(1)} %get-tuple-element.84), channel_id=1, source_target_pairs={{0,32},{32,64},{64,96},{96,0},{1,33},{33,65},{65,97},{97,1},{2,34}... | collective-permute-start | bytes 786440 | tf_op jit(solution)/shard_map/ppermute | solution.py:696
  80.4 3.3 %collective-permute-start.18 = (bf16[128,1024]{1,0:T(8,128)(2,1)S(1)}, bf16[128,1024]{1,0:T(8,128)(2,1)S(1)}, u32[]{:S(2)}, u32[]{:S(2)}) collective-permute-start(bf16[128,1024]{1,0:T(8,128)(2,1)S(1)} %get-tuple-element.85), channel_id=1, source_target_pairs={{0,64},{32,96},{64,0},{96,32},{1,65},{33,97},{65,1},{97,33},{2,66}... | collective-permute-start | bytes 786440 | tf_op jit(solution)/shard_map/ppermute | solution.py:696
  83.7 0.7 collective-permute-start.19
  84.4 3.0 %collective-permute-done.17.a = bf16[128,1024]{1,0:T(8,128)(2,1)S(1)} collective-permute-done((bf16[128,1024]{1,0:T(8,128)(2,1)S(1)}, bf16[128,1024]{1,0:T(8,128)(2,1)S(1)}, u32[]{:S(2)}, u32[]{:S(2)}) %collective-permute-start.17) | collective-permute-done | bytes 262176 | tf_op jit(solution)/shard_map/ppermute | solution.py:696
  87.5 6.5 %collective-permute-done.18.b = bf16[128,1024]{1,0:T(8,128)(2,1)S(1)} collective-permute-done((bf16[128,1024]{1,0:T(8,128)(2,1)S(1)}, bf16[128,1024]{1,0:T(8,128)(2,1)S(1)}, u32[]{:S(2)}, u32[]{:S(2)}) %collective-permute-start.18) | collective-permute-done | bytes 262176 | tf_op jit(solution)/shard_map/ppermute | solution.py:696
  94.0 0.0 collective-permute-done.19.c
  94.0 0.8 join_shares.1.x0
  94.9 0.3 stack.31.refs_0_
  95.1 2.6 %collective-permute-start.23 = (bf16[4,4,128,1024]{3,2,1,0:T(8,128)(2,1)S(1)}, bf16[4,4,128,1024]{3,2,1,0:T(8,128)(2,1)S(1)}, u32[]{:S(2)}, u32[]{:S(2)}) collective-permute-start(bf16[4,4,128,1024]{3,2,1,0:T(8,128)(2,1)S(1)} %stack.31.refs_0_), channel_id=1, source_target_pairs={{0,1},{1,0},{2,3},{3,2},{4,5},{5,4},{6,7},{7,6},{8,9},{9,8},{10,11... | collective-permute-start | bytes 12582920 | tf_op jit(solution)/shard_map/ppermute | solution.py:703
  97.8 2.8 %collective-permute-start.26 = (bf16[128,1024]{1,0:T(8,128)(2,1)S(1)}, bf16[128,1024]{1,0:T(8,128)(2,1)S(1)}, u32[]{:S(2)}, u32[]{:S(2)}) collective-permute-start(bf16[128,1024]{1,0:T(8,128)(2,1)S(1)} %copy-done.3), channel_id=1, source_target_pairs={{0,96},{32,0},{64,32},{96,64},{1,97},{33,1},{65,33},{97,65},{2,98}... | collective-permute-start | bytes 786440 | tf_op jit(solution)/shard_map/ppermute | solution.py:705
  100.5 0.7 collective-permute-start.24
  101.2 4.8 %load.1.weight = bf16[4096,1536]{1,0:T(8,128)(2,1)S(1)} custom-call(bf16[4096,1536]{1,0:T(8,128)(2,1)} %src), custom_call_target="tpu_custom_call" | custom-call | tf_op jit(solution)/shard_map/load/pallas_call | solution.py:181
  106.1 5.0 %patch.1 = (bf16[13,128,512]{2,1,0:T(8,128)(2,1)}, bf16[13,128,512]{2,1,0:T(8,128)(2,1)}, s32[1]{0:T(128)}) custom-call(s32[5]{0:T(128)S(1)} %stack.27.info.refs_0_, s32[8]{0:T(128)S(1)} %copy-done.8, s32[8,36]{1,0:T(8,128)S(1)} %copy-done.13, bf16[4,4,128,1024]{3,2,1,0:T(8,128)(2,1)S(1)} %stack.31.refs_0_, ...), custom_call_target="tpu_custom_call" | custom-call | tf_op jit(solution)/shard_map/patch/pallas_call | solution.py:580
  111.1 0.5 collective-permute-done.26.x3
  111.7 3.7 %collective-permute-done.24.x1 = bf16[128,1024]{1,0:T(8,128)(2,1)} collective-permute-done((bf16[128,1024]{1,0:T(8,128)(2,1)S(1)}, bf16[128,1024]{1,0:T(8,128)(2,1)}, u32[]{:S(2)}, u32[]{:S(2)}) %collective-permute-start.24) | collective-permute-done | bytes 262176 | tf_op jit(solution)/shard_map/ppermute | solution.py:705
  115.4 4.8 %project_qkv.1 = bf16[128,1536]{1,0:T(8,128)(2,1)} custom-call(s32[5]{0:T(128)S(1)} %stack.27.info.refs_0_, s32[1]{0:T(128)} %get-tuple-element.94.token, bf16[128,1024]{1,0:T(8,128)(2,1)S(1)} %copy-done.3, bf16[128,1024]{1,0:T(8,128)(2,1)} %collective-permute-done.24.x1, bf16[128,1024]{1,0:T(8,128)(2,1)} %collective-permute-done.25.x2, ...), custom_call_target="tpu_custom_call" | custom-call | tf_op jit(solution)/shard_map/project_qkv/pallas_call | solution.py:457
  (41 shorter events, 0.2 us)
Async XLA Ops:
  0.6 9.0 %collective-permute-start.3 = (bf16[13,128,512]{2,1,0:T(8,128)(2,1)}, bf16[13,128,512]{2,1,0:T(8,128)(2,1)S(1)}, u32[]{:S(2)}, u32[]{:S(2)}) collective-permute-start(bf16[13,128,512]{2,1,0:T(8,128)(2,1)} %refs_2_.1), channel_id=1, source_target_pairs={{0,1},{1,0},{2,3},{3,2},{4,5},{5,4},{6,7},{7,6},{8,9},{9,8},{10,11... | collective-permute-start | bytes 5111816 | tf_op jit(solution)/shard_map/ppermute | solution.py:653
  2.1 7.9 %collective-permute-start.4 = (bf16[13,128,512]{2,1,0:T(8,128)(2,1)}, bf16[13,128,512]{2,1,0:T(8,128)(2,1)S(1)}, u32[]{:S(2)}, u32[]{:S(2)}) collective-permute-start(bf16[13,128,512]{2,1,0:T(8,128)(2,1)} %refs_3_.1), channel_id=1, source_target_pairs={{0,1},{1,0},{2,3},{3,2},{4,5},{5,4},{6,7},{7,6},{8,9},{9,8},{10,11... | collective-permute-start | bytes 5111816 | tf_op jit(solution)/shard_map/ppermute | solution.py:654
  2.4 1.0 copy-start.4
  3.4 0.7 copy-start.7
  4.9 14.2 %collective-permute-start.6 = (bf16[128,1024]{1,0:T(8,128)(2,1)S(1)}, bf16[128,1024]{1,0:T(8,128)(2,1)S(1)}, u32[]{:S(2)}, u32[]{:S(2)}) collective-permute-start(bf16[128,1024]{1,0:T(8,128)(2,1)S(1)} %get-tuple-element.54.refs_9_.refs_0_), channel_id=1, source_target_pairs={{0,2},{1,9},{2,0},{3,11},{4,6},{5,13},{6,4},{7,15},{8,10},{9,1},{1... | collective-permute-start | bytes 786440 | tf_op jit(solution)/shard_map/ppermute | solution.py:623
  6.3 12.8 %collective-permute-start.5 = (bf16[128,1024]{1,0:T(8,128)(2,1)S(1)}, bf16[128,1024]{1,0:T(8,128)(2,1)S(1)}, u32[]{:S(2)}, u32[]{:S(2)}) collective-permute-start(bf16[128,1024]{1,0:T(8,128)(2,1)S(1)} %get-tuple-element.54.refs_9_.refs_0_), channel_id=1, source_target_pairs={{0,1},{1,0},{2,3},{3,2},{4,5},{5,4},{6,7},{7,6},{8,9},{9,8},{10,11... | collective-permute-start | bytes 786440 | tf_op jit(solution)/shard_map/ppermute | solution.py:655
  6.9 12.1 %collective-permute-start.2 = (bf16[512,128]{1,0:T(8,128)(2,1)S(1)}, bf16[512,128]{1,0:T(8,128)(2,1)S(1)}, u32[]{:S(2)}, u32[]{:S(2)}) collective-permute-start(bf16[512,128]{1,0:T(8,128)(2,1)S(1)} %get-tuple-element.55.refs_0_), channel_id=1, source_target_pairs={{0,6},{1,25},{2,0},{3,27},{4,2},{5,29},{6,4},{7,31},{8,14},{9,1},{... | collective-permute-start | bytes 393224 | tf_op jit(solution)/shard_map/ppermute | solution.py:619
  9.7 9.4 %collective-permute-start.1 = (bf16[512,128]{1,0:T(8,128)(2,1)S(1)}, bf16[512,128]{1,0:T(8,128)(2,1)S(1)}, u32[]{:S(2)}, u32[]{:S(2)}) collective-permute-start(bf16[512,128]{1,0:T(8,128)(2,1)S(1)} %get-tuple-element.55.refs_0_), channel_id=1, source_target_pairs={{0,4},{1,17},{2,6},{3,19},{4,0},{5,21},{6,2},{7,23},{8,12},{9,25},... | collective-permute-start | bytes 393224 | tf_op jit(solution)/shard_map/ppermute | solution.py:619
  10.0 9.0 %collective-permute-start = (bf16[512,128]{1,0:T(8,128)(2,1)S(1)}, bf16[512,128]{1,0:T(8,128)(2,1)S(1)}, u32[]{:S(2)}, u32[]{:S(2)}) collective-permute-start(bf16[512,128]{1,0:T(8,128)(2,1)S(1)} %get-tuple-element.55.refs_0_), channel_id=1, source_target_pairs={{0,2},{1,9},{2,4},{3,11},{4,6},{5,13},{6,0},{7,15},{8,10},{9,17},{... | collective-permute-start | bytes 393224 | tf_op jit(solution)/shard_map/ppermute | solution.py:619
  10.7 0.7 copy-start.12
  14.3 9.4 %copy-start.1 = (bf16[13,128,512]{2,1,0:T(8,128)(2,1)S(1)}, bf16[13,128,512]{2,1,0:T(8,128)(2,1)}, u32[]{:S(2)}) copy-start(bf16[13,128,512]{2,1,0:T(8,128)(2,1)} %refs_3_.1) | copy-start | bytes 5111812
  19.0 4.8 %copy-start = (bf16[13,128,512]{2,1,0:T(8,128)(2,1)S(1)}, bf16[13,128,512]{2,1,0:T(8,128)(2,1)}, u32[]{:S(2)}) copy-start(bf16[13,128,512]{2,1,0:T(8,128)(2,1)} %refs_2_.1) | copy-start | bytes 5111812
  19.0 4.8 %copy-start.8 = (s32[8]{0:T(128)S(1)}, s32[8]{0:T(128)}, u32[]{:S(2)}) copy-start(s32[8]{0:T(128)} %lens.5) | copy-start | bytes 100
  19.1 9.6 %collective-permute-start.7 = (bf16[4,512,128]{2,1,0:T(8,128)(2,1)S(1)}, bf16[4,512,128]{2,1,0:T(8,128)(2,1)S(1)}, u32[]{:S(2)}, u32[]{:S(2)}) collective-permute-start(bf16[4,512,128]{2,1,0:T(8,128)(2,1)S(1)} %stack.28.refs_4_), channel_id=1, source_target_pairs={{0,8},{1,3},{2,10},{3,5},{4,12},{5,7},{6,14},{7,1},{8,16},{9,11},{... | collective-permute-start | bytes 1572872 | tf_op jit(solution)/shard_map/ppermute | solution.py:619
  19.5 17.8 %collective-permute-start.10 = (bf16[4,512,128]{2,1,0:T(8,128)(2,1)S(1)}, bf16[4,512,128]{2,1,0:T(8,128)(2,1)S(1)}, u32[]{:S(2)}, u32[]{:S(2)}) collective-permute-start(bf16[4,512,128]{2,1,0:T(8,128)(2,1)S(1)} %stack.28.refs_4_), channel_id=1, source_target_pairs={{0,16},{1,5},{2,18},{3,7},{4,20},{5,1},{6,22},{7,3},{8,24},{9,13},... | collective-permute-start | bytes 1572872 | tf_op jit(solution)/shard_map/ppermute | solution.py:619
  22.2 12.8 %collective-permute-start.8 = (bf16[4,512,128]{2,1,0:T(8,128)(2,1)S(1)}, bf16[4,512,128]{2,1,0:T(8,128)(2,1)S(1)}, u32[]{:S(2)}, u32[]{:S(2)}) collective-permute-start(bf16[4,512,128]{2,1,0:T(8,128)(2,1)S(1)} %stack.28.refs_4_), channel_id=1, source_target_pairs={{0,24},{1,7},{2,26},{3,1},{4,28},{5,3},{6,30},{7,5},{8,0},{9,15},{... | collective-permute-start | bytes 1572872 | tf_op jit(solution)/shard_map/ppermute | solution.py:619
  28.7 13.0 %collective-permute-start.11 = (bf16[2,128,1024]{2,1,0:T(8,128)(2,1)S(1)}, bf16[2,128,1024]{2,1,0:T(8,128)(2,1)S(1)}, u32[]{:S(2)}, u32[]{:S(2)}) collective-permute-start(bf16[2,128,1024]{2,1,0:T(8,128)(2,1)S(1)} %stack.29.refs_0_), channel_id=1, source_target_pairs={{0,6},{1,25},{2,4},{3,27},{4,2},{5,29},{6,0},{7,31},{8,14},{9,17},... | collective-permute-start | bytes 1572872 | tf_op jit(solution)/shard_map/ppermute | solution.py:623
  37.3 11.4 %collective-permute-start.13 = (bf16[4,544,128]{2,1,0:T(8,128)(2,1)S(1)}, bf16[4,544,128]{2,1,0:T(8,128)(2,1)S(1)}, u32[]{:S(2)}, u32[]{:S(2)}) collective-permute-start(bf16[4,544,128]{2,1,0:T(8,128)(2,1)S(1)} %attend3.1), channel_id=1, source_target_pairs={{0,8},{1,3},{2,10},{3,5},{4,12},{5,7},{6,14},{7,1},{8,16},{9,11},{... | collective-permute-start | bytes 1671176 | tf_op jit(solution)/shard_map/ppermute | solution.py:619
  39.8 11.9 %collective-permute-start.9 = (bf16[4,544,128]{2,1,0:T(8,128)(2,1)S(1)}, bf16[4,544,128]{2,1,0:T(8,128)(2,1)S(1)}, u32[]{:S(2)}, u32[]{:S(2)}) collective-permute-start(bf16[4,544,128]{2,1,0:T(8,128)(2,1)S(1)} %attend1.1), channel_id=1, source_target_pairs={{0,24},{1,7},{2,26},{3,1},{4,28},{5,3},{6,30},{7,5},{8,0},{9,15},{... | collective-permute-start | bytes 1671176 | tf_op jit(solution)/shard_map/ppermute | solution.py:619
  41.8 26.8 %copy-start.2 = (bf16[512,4096]{1,0:T(8,128)(2,1)S(1)}, bf16[512,4096]{1,0:T(8,128)(2,1)}, u32[]{:S(2)}) copy-start(bf16[512,4096]{1,0:T(8,128)(2,1)} %weight.1) | copy-start | bytes 12582916
  43.6 25.1 %copy-start.5 = (bf16[128,1024]{1,0:T(8,128)(2,1)S(1)}, bf16[128,1024]{1,0:T(8,128)(2,1)}, u32[]{:S(2)}) copy-start(bf16[128,1024]{1,0:T(8,128)(2,1)} %hidden.1) | copy-start | bytes 786436
  43.6 25.1 %copy-start.6 = (bf16[128,1024]{1,0:T(8,128)(2,1)S(1)}, bf16[128,1024]{1,0:T(8,128)(2,1)}, u32[]{:S(2)}) copy-start(bf16[128,1024]{1,0:T(8,128)(2,1)} %branch.1) | copy-start | bytes 786436
  43.6 25.1 %copy-start.9 = (f32[4096]{0:T(1024)S(1)}, f32[4096]{0:T(1024)}, u32[]{:S(2)}) copy-start(f32[4096]{0:T(1024)} %bias.2) | copy-start | bytes 49156
  43.7 14.3 %collective-permute-start.12 = (bf16[4,544,128]{2,1,0:T(8,128)(2,1)S(1)}, bf16[4,544,128]{2,1,0:T(8,128)(2,1)S(1)}, u32[]{:S(2)}, u32[]{:S(2)}) collective-permute-start(bf16[4,544,128]{2,1,0:T(8,128)(2,1)S(1)} %attend2.1), channel_id=1, source_target_pairs={{0,16},{1,5},{2,18},{3,7},{4,20},{5,1},{6,22},{7,3},{8,24},{9,13},... | collective-permute-start | bytes 1671176 | tf_op jit(solution)/shard_map/ppermute | solution.py:619
  58.5 17.0 %collective-permute-start.21 = (bf16[4,128,1024]{2,1,0:T(8,128)(2,1)S(1)}, bf16[4,128,1024]{2,1,0:T(8,128)(2,1)S(1)}, u32[]{:S(2)}, u32[]{:S(2)}) collective-permute-start(bf16[4,128,1024]{2,1,0:T(8,128)(2,1)S(1)} %bitcast.6), channel_id=1, source_target_pairs={{0,24},{1,7},{2,26},{3,1},{4,28},{5,3},{6,30},{7,5},{8,0},{9,15},{... | collective-permute-start | bytes 3145736 | tf_op jit(solution)/shard_map/ppermute | solution.py:619
  60.6 18.1 %collective-permute-start.20 = (bf16[4,128,1024]{2,1,0:T(8,128)(2,1)S(1)}, bf16[4,128,1024]{2,1,0:T(8,128)(2,1)S(1)}, u32[]{:S(2)}, u32[]{:S(2)}) collective-permute-start(bf16[4,128,1024]{2,1,0:T(8,128)(2,1)S(1)} %bitcast.7), channel_id=1, source_target_pairs={{0,8},{1,3},{2,10},{3,5},{4,12},{5,7},{6,14},{7,1},{8,16},{9,11},{... | collective-permute-start | bytes 3145736 | tf_op jit(solution)/shard_map/ppermute | solution.py:619
  60.6 3.9 %collective-permute-start.14 = (bf16[544,128]{1,0:T(8,128)(2,1)S(1)}, bf16[544,128]{1,0:T(8,128)(2,1)S(1)}, u32[]{:S(2)}, u32[]{:S(2)}) collective-permute-start(bf16[544,128]{1,0:T(8,128)(2,1)S(1)} %get-tuple-element.80), channel_id=1, source_target_pairs={{0,6},{1,25},{2,0},{3,27},{4,2},{5,29},{6,4},{7,31},{8,14},{9,1},{... | collective-permute-start | bytes 417800 | tf_op jit(solution)/shard_map/ppermute | solution.py:619
  61.8 5.5 %collective-permute-start.15 = (bf16[544,128]{1,0:T(8,128)(2,1)S(1)}, bf16[544,128]{1,0:T(8,128)(2,1)S(1)}, u32[]{:S(2)}, u32[]{:S(2)}) collective-permute-start(bf16[544,128]{1,0:T(8,128)(2,1)S(1)} %get-tuple-element.81), channel_id=1, source_target_pairs={{0,4},{1,17},{2,6},{3,19},{4,0},{5,21},{6,2},{7,23},{8,12},{9,25},... | collective-permute-start | bytes 417800 | tf_op jit(solution)/shard_map/ppermute | solution.py:619
  61.8 6.6 %collective-permute-start.16 = (bf16[544,128]{1,0:T(8,128)(2,1)S(1)}, bf16[544,128]{1,0:T(8,128)(2,1)S(1)}, u32[]{:S(2)}, u32[]{:S(2)}) collective-permute-start(bf16[544,128]{1,0:T(8,128)(2,1)S(1)} %get-tuple-element.82), channel_id=1, source_target_pairs={{0,2},{1,9},{2,4},{3,11},{4,6},{5,13},{6,0},{7,15},{8,10},{9,17},{... | collective-permute-start | bytes 417800 | tf_op jit(solution)/shard_map/ppermute | solution.py:619
  78.7 16.1 %collective-permute-start.22 = (bf16[4,128,1024]{2,1,0:T(8,128)(2,1)S(1)}, bf16[4,128,1024]{2,1,0:T(8,128)(2,1)S(1)}, u32[]{:S(2)}, u32[]{:S(2)}) collective-permute-start(bf16[4,128,1024]{2,1,0:T(8,128)(2,1)S(1)} %collective-permute-done.20.refs_1_), channel_id=1, source_target_pairs={{0,8},{1,3},{2,10},{3,5},{4,12},{5,7},{6,14},{7,1},{8,16},{9,11},{... | collective-permute-start | bytes 3145736 | tf_op jit(solution)/shard_map/ppermute | solution.py:619
  78.7 8.7 %collective-permute-start.17 = (bf16[128,1024]{1,0:T(8,128)(2,1)S(1)}, bf16[128,1024]{1,0:T(8,128)(2,1)S(1)}, u32[]{:S(2)}, u32[]{:S(2)}) collective-permute-start(bf16[128,1024]{1,0:T(8,128)(2,1)S(1)} %get-tuple-element.84), channel_id=1, source_target_pairs={{0,32},{32,64},{64,96},{96,0},{1,33},{33,65},{65,97},{97,1},{2,34}... | collective-permute-start | bytes 786440 | tf_op jit(solution)/shard_map/ppermute | solution.py:696
  80.4 13.6 %collective-permute-start.18 = (bf16[128,1024]{1,0:T(8,128)(2,1)S(1)}, bf16[128,1024]{1,0:T(8,128)(2,1)S(1)}, u32[]{:S(2)}, u32[]{:S(2)}) collective-permute-start(bf16[128,1024]{1,0:T(8,128)(2,1)S(1)} %get-tuple-element.85), channel_id=1, source_target_pairs={{0,64},{32,96},{64,0},{96,32},{1,65},{33,97},{65,1},{97,33},{2,66}... | collective-permute-start | bytes 786440 | tf_op jit(solution)/shard_map/ppermute | solution.py:696
  83.7 10.3 %collective-permute-start.19 = (bf16[128,1024]{1,0:T(8,128)(2,1)S(1)}, bf16[128,1024]{1,0:T(8,128)(2,1)S(1)}, u32[]{:S(2)}, u32[]{:S(2)}) collective-permute-start(bf16[128,1024]{1,0:T(8,128)(2,1)S(1)} %get-tuple-element.86), channel_id=1, source_target_pairs={{0,96},{32,0},{64,32},{96,64},{1,97},{33,1},{65,33},{97,65},{2,98}... | collective-permute-start | bytes 786440 | tf_op jit(solution)/shard_map/ppermute | solution.py:696
  94.9 2.9 %copy-start.3 = (bf16[128,1024]{1,0:T(8,128)(2,1)S(1)}, bf16[128,1024]{1,0:T(8,128)(2,1)}, u32[]{:S(2)}) copy-start(bf16[128,1024]{1,0:T(8,128)(2,1)} %join_shares.1.x0) | copy-start | bytes 786436
  95.1 11.0 %copy-start.13 = (s32[8,36]{1,0:T(8,128)S(1)}, s32[8,36]{1,0:T(8,128)}, u32[]{:S(2)}) copy-start(s32[8,36]{1,0:T(8,128)} %table.3) | copy-start | bytes 3460
  95.1 11.0 %collective-permute-start.23 = (bf16[4,4,128,1024]{3,2,1,0:T(8,128)(2,1)S(1)}, bf16[4,4,128,1024]{3,2,1,0:T(8,128)(2,1)S(1)}, u32[]{:S(2)}, u32[]{:S(2)}) collective-permute-start(bf16[4,4,128,1024]{3,2,1,0:T(8,128)(2,1)S(1)} %stack.31.refs_0_), channel_id=1, source_target_pairs={{0,1},{1,0},{2,3},{3,2},{4,5},{5,4},{6,7},{7,6},{8,9},{9,8},{10,11... | collective-permute-start | bytes 12582920 | tf_op jit(solution)/shard_map/ppermute | solution.py:703
  97.8 13.9 %collective-permute-start.26 = (bf16[128,1024]{1,0:T(8,128)(2,1)S(1)}, bf16[128,1024]{1,0:T(8,128)(2,1)S(1)}, u32[]{:S(2)}, u32[]{:S(2)}) collective-permute-start(bf16[128,1024]{1,0:T(8,128)(2,1)S(1)} %copy-done.3), channel_id=1, source_target_pairs={{0,96},{32,0},{64,32},{96,64},{1,97},{33,1},{65,33},{97,65},{2,98}... | collective-permute-start | bytes 786440 | tf_op jit(solution)/shard_map/ppermute | solution.py:705
  100.5 11.1 %collective-permute-start.25 = (bf16[128,1024]{1,0:T(8,128)(2,1)S(1)}, bf16[128,1024]{1,0:T(8,128)(2,1)}, u32[]{:S(2)}, u32[]{:S(2)}) collective-permute-start(bf16[128,1024]{1,0:T(8,128)(2,1)S(1)} %copy-done.3), channel_id=1, source_target_pairs={{0,64},{32,96},{64,0},{96,32},{1,65},{33,97},{65,1},{97,33},{2,66}... | collective-permute-start | bytes 786440 | tf_op jit(solution)/shard_map/ppermute | solution.py:705
  100.5 14.8 %collective-permute-start.24 = (bf16[128,1024]{1,0:T(8,128)(2,1)S(1)}, bf16[128,1024]{1,0:T(8,128)(2,1)}, u32[]{:S(2)}, u32[]{:S(2)}) collective-permute-start(bf16[128,1024]{1,0:T(8,128)(2,1)S(1)} %copy-done.3), channel_id=1, source_target_pairs={{0,32},{32,64},{64,96},{96,0},{1,33},{33,65},{65,97},{97,1},{2,34}... | collective-permute-start | bytes 786440 | tf_op jit(solution)/shard_map/ppermute | solution.py:705
  106.1 9.3 %copy-start.10 = (f32[4096]{0:T(1024)S(1)}, f32[4096]{0:T(1024)}, u32[]{:S(2)}) copy-start(f32[4096]{0:T(1024)} %gain.1) | copy-start | bytes 49156
  106.1 9.3 %copy-start.11 = (f32[4096]{0:T(1024)S(1)}, f32[4096]{0:T(1024)}, u32[]{:S(2)}) copy-start(f32[4096]{0:T(1024)} %shift.1) | copy-start | bytes 49156
  106.1 9.2 %copy-start.14 = (f32[1536]{0:T(1024)S(1)}, f32[1536]{0:T(1024)}, u32[]{:S(2)}) copy-start(f32[1536]{0:T(1024)} %bias.3) | copy-start | bytes 18436

commit v5 on v4

--- a/solution.py
+++ b/solution.py
@@ -216,99 +216,136 @@
     key_row = lax.broadcasted_iota(jnp.int32, (2 * PT, TOK), 0)
     lane = lax.broadcasted_iota(jnp.int32, (2 * PT, TOK), 1)
 
-    def block_loop(block, carry):
-        row = lax.bitwise_and(y - jnp.where(core == 0, step, block), 3)
-        column = lax.bitwise_and(x - jnp.where(core == 0, block, step), 3)
-        request = 2 * row + lax.div(column, 2)
-
-        def absorb(key_of, value_of, mask, guard):
-            old = stats[...]
-            scores = [
-                jnp.where(
-                    mask,
-                    jnp.dot(key_of(h), q_ref[block, head_rows(h), :], preferred_element_type=F32),
-                    NEG,
+    def absorb(sides):
+        work = [(side, h) for side in sides for h in range(LH)]
+        old = {side[0]: stats[side[0]] for side in sides}
+        scores = [
+            jnp.where(
+                side[4],
+                jnp.dot(
+                    side[2](h), q_ref[side[1], head_rows(h), :], preferred_element_type=F32
+                ),
+                NEG,
+            )
+            for side, h in work
+        ]
+        peaks = [
+            jnp.maximum(old[side[0]][h : h + 1], jnp.max(score, axis=0, keepdims=True))
+            for (side, h), score in zip(work, scores)
+        ]
+        weights = [
+            jnp.where(side[4], jnp.exp2((score - peak) * C2), 0.0)
+            for (side, h), score, peak in zip(work, scores, peaks)
+        ]
+        decays = [
+            jnp.exp2((old[side[0]][h : h + 1] - peak) * C2)
+            for (side, h), peak in zip(work, peaks)
+        ]
+        totals = [
+            old[side[0]][LH + h : LH + h + 1] * decay + jnp.sum(weight, axis=0, keepdims=True)
+            for (side, h), decay, weight in zip(work, decays, weights)
+        ]
+        for n, side in enumerate(sides):
+            rows = slice(n * LH, (n + 1) * LH)
+            stats[side[0]] = jnp.concatenate(peaks[rows] + totals[rows], axis=0)
+        added = [
+            lax.dot_general(
+                side[3](h), weight.astype(BF16), (((0,), (0,)), ((), ())),
+                preferred_element_type=F32,
+            )
+            for (side, h), weight in zip(work, weights)
+        ]
+        for (side, h), decay, add in zip(work, decays, added):
+            acc[side[0], head_rows(h), :] = acc[side[0], head_rows(h), :] * decay + add
+
+    straight = (core == 0) & (lax.bitwise_and(x, 1) == 1)
+
+    def pair_loop(j, carry):
+        blocks = (jnp.where(straight, 2 * j, j), jnp.where(straight, 2 * j + 1, 3 - j))
+        rows = [lax.bitwise_and(y - jnp.where(core == 0, step, block), 3) for block in blocks]
+        columns = [lax.bitwise_and(x - jnp.where(core == 0, block, step), 3) for block in blocks]
+        requests = [2 * row + lax.div(column, 2) for row, column in zip(rows, columns)]
+        amounts = [counts[request] for request in requests]
+        acc[...] = jnp.zeros_like(acc)
+        start = jnp.where(lax.broadcasted_iota(jnp.int32, (2 * LH, TOK), 0) < LH, NEG, 0.0)
+        stats[0] = start
+        stats[1] = start
+
+        def pages_step(i, inner):
+            sides = []
+            for t in range(2):
+                request, amount = requests[t], amounts[t]
+                first = codes[request, jnp.maximum(jnp.minimum(2 * i, amount - 1), 0)]
+                second = codes[request, jnp.maximum(jnp.minimum(2 * i + 1, amount - 1), 0)]
+                first = jnp.where(amount > 0, first, 0)
+                second = jnp.where(amount > 0, second, 0)
+                lower = jnp.where(
+                    2 * i < amount, lens[request] - lax.div(first, LIST) * PT, 0
                 )
-                for h in range(LH)
-            ]
-            peaks = [
-                jnp.maximum(old[h : h + 1], jnp.max(scores[h], axis=0, keepdims=True))
-                for h in range(LH)
-            ]
-            weights = [jnp.exp2((scores[h] - peaks[h]) * C2) for h in range(LH)]
-            if guard:
-                weights = [jnp.where(mask, w, 0.0) for w in weights]
-            decays = [jnp.exp2((old[h : h + 1] - peaks[h]) * C2) for h in range(LH)]
-            totals = [
-                old[LH + h : LH + h + 1] * decays[h] + jnp.sum(weights[h], axis=0, keepdims=True)
-                for h in range(LH)
-            ]
-            stats[...] = jnp.concatenate(peaks + totals, axis=0)
-            added = [
-                lax.dot_general(
-                    value_of(h), weights[h].astype(BF16), (((0,), (0,)), ((), ())),
-                    preferred_element_type=F32,
+                upper = jnp.where(
+                    2 * i + 1 < amount, lens[request] - lax.div(second, LIST) * PT, 0
                 )
-                for h in range(LH)
-            ]
+                mask = key_row < jnp.where(key_row < PT, lower, upper + PT)
+
+                def page_rows(own, other, code, h):
+                    slot = lax.rem(code, LIST)
+                    mine = slot < SLOTS
+                    local = jnp.where(mine, slot, slot - SLOTS)
+                    return jnp.where(
+                        mine, own[local, :, head_rows(h)], other[local, :, head_rows(h)]
+                    )
+
+                def both(own, other, h, first=first, second=second):
+                    return jnp.concatenate(
+                        [page_rows(own, other, first, h), page_rows(own, other, second, h)],
+                        axis=0,
+                    )
+
+                sides.append(
+                    (
+                        t,
+                        blocks[t],
+                        lambda h, both=both: both(k_own, k_other, h),
+                        lambda h, both=both: both(v_own, v_other, h),
+                        mask,
+                    )
+                )
+            absorb(sides)
+            return inner
+
+        most = jnp.maximum(amounts[0], amounts[1])
+        lax.fori_loop(0, lax.div(most + 1, 2), pages_step, 0)
+        if step != 2:
+            for t in range(2):
+
+                @pl.when(requests[t] == 2 * y + lax.div(x, 2))
+                def _(t=t):
+                    both = lambda cols: jnp.concatenate(
+                        [fresh_own[:, cols], fresh_other[:, cols]], axis=0
+                    )
+                    token = 2 * lax.bitwise_and(x, 1) * TOK + jnp.where(
+                        key_row < PT, key_row + core * TOK, key_row - core * TOK
+                    )
+                    query = (2 * lax.bitwise_and(columns[t], 1) + core) * TOK + lane
+                    absorb(
+                        [
+                            (
+                                t,
+                                blocks[t],
+                                lambda h: both(head_rows(h)),
+                                lambda h: both(slice(LW + h * HS, LW + (h + 1) * HS)),
+                                token <= query,
+                            )
+                        ]
+                    )
+
+        for t in range(2):
             for h in range(LH):
-                acc[head_rows(h), :] = acc[head_rows(h), :] * decays[h] + added[h]
-
-        acc[...] = jnp.zeros_like(acc)
-        stats[...] = jnp.where(lax.broadcasted_iota(jnp.int32, (2 * LH, TOK), 0) < LH, NEG, 0.0)
-        count = counts[request]
-
-        def pages_step(i, inner):
-            full = 2 * i + 1 < count
-            first = codes[request, 2 * i]
-            second = codes[request, jnp.where(full, 2 * i + 1, 2 * i)]
-            lower = lens[request] - lax.div(first, LIST) * PT
-            upper = jnp.where(full, lens[request] - lax.div(second, LIST) * PT, 0) + PT
-            mask = key_row < jnp.where(key_row < PT, lower, upper)
-
-            def page_rows(own, other, code, h):
-                slot = lax.rem(code, LIST)
-                mine = slot < SLOTS
-                local = jnp.where(mine, slot, slot - SLOTS)
-                return jnp.where(
-                    mine, own[local, :, head_rows(h)], other[local, :, head_rows(h)]
-                )
-
-            def pair(own, other, h):
-                return jnp.concatenate(
-                    [page_rows(own, other, first, h), page_rows(own, other, second, h)], axis=0
-                )
-
-            absorb(
-                lambda h: pair(k_own, k_other, h), lambda h: pair(v_own, v_other, h), mask, False
-            )
-            return inner
-
-        lax.fori_loop(0, lax.div(count + 1, 2), pages_step, 0)
-        if step != 2:
-
-            @pl.when(request == 2 * y + lax.div(x, 2))
-            def _():
-                pair = lambda cols: jnp.concatenate(
-                    [fresh_own[:, cols], fresh_other[:, cols]], axis=0
-                )
-                token = 2 * lax.bitwise_and(x, 1) * TOK + jnp.where(
-                    key_row < PT, key_row + core * TOK, key_row - core * TOK
-                )
-                query = (2 * lax.bitwise_and(column, 1) + core) * TOK + lane
-                absorb(
-                    lambda h: pair(head_rows(h)),
-                    lambda h: pair(slice(LW + h * HS, LW + (h + 1) * HS)),
-                    token <= query,
-                    True,
-                )
-
-        for h in range(LH):
-            o_ref[block, head_rows(h), :] = acc[head_rows(h), :].astype(BF16)
-        o_ref[block, LW:PIECES, :] = stat_rows(stats[...])
+                o_ref[blocks[t], head_rows(h), :] = acc[t, head_rows(h), :].astype(BF16)
+            o_ref[blocks[t], LW:PIECES, :] = stat_rows(stats[t])
         return carry
 
-    lax.fori_loop(0, 4, block_loop, 0)
+    lax.fori_loop(0, 2, pair_loop, 0)
 
 
 def attend(step, info, lens, lists, queries, caches, fresh):
@@ -323,7 +360,7 @@
         out_shape=jax.ShapeDtypeStruct((4, PIECES, TOK), BF16),
         in_specs=specs,
         out_specs=whole(),
-        scratch_shapes=[VMEM((LW, TOK), F32), VMEM((2 * LH, TOK), F32)],
+        scratch_shapes=[VMEM((2, LW, TOK), F32), VMEM((2, 2 * LH, TOK), F32)],
         compiler_params=limit(12),
         cost_estimate=pl.CostEstimate(flops=0, transcendentals=0, bytes_accessed=0),
         name="attend%d" % step,

time: 120 us -> 121 us (level)
  waiting for transfers between devices: 44.4 us -> 42.3 us
  starting transfers between devices: 37.8 us -> 39.2 us
  Pallas kernels: 34.4 us -> 35.7 us
    pallas_call x4, Pallas kernels: 8.23 us -> 10.9 us  [attend(): pl.pallas_call(body, out_shape=jax.ShapeDtypeStruct((4, PIECES, TOK), BF1...]
    ppermute x15, waiting for transfers between devices: 28.9 us -> 27 us  [send(): return lax.ppermute(array, PLANE, plane_pairs(lambda u: (u + s) % 4, stage))]
    ppermute x3, waiting for transfers between devices: 4.2 us -> 5.69 us  [on_device(): lax.ppermute(new_hidden, 'head', shift(s))]
    pallas_call x1, Pallas kernels: 5 us -> 3.59 us  [patch(): pl.pallas_call(patch_kernel, out_shape=(shape, shape, jax.ShapeDtypeStruc...]
  transfers between devices with their start and end apart: 27 -> 27, of which waited for: 14 -> 15; matrix products, arithmetic and copies ran while one was open for 0% -> 0% of each run, Pallas kernels for 24% -> 25%
where the time goes in v5:
time: 121 us
  waiting for transfers between devices  42.3 us (35%)
  starting transfers between devices  39.2 us (32%)
  Pallas kernels  35.7 us (30%)
  local copies, waits for them, and re-layouts  2.57 us (2%)
    ppermute x15, waiting for transfers between devices, send(): return lax.ppermute(array, PLANE, plane_pairs(lambda u: (u + s) % 4, stage))  27 us
    ppermute x15, starting transfers between devices, send(): return lax.ppermute(array, PLANE, plane_pairs(lambda u: (u + s) % 4, stage))  20.6 us
    pallas_call x4, Pallas kernels, attend(): pl.pallas_call(body, out_shape=jax.ShapeDtypeStruct((4, PIECES, TOK), BF1...  10.9 us
    ppermute x3, waiting for transfers between devices, on_device(): lax.ppermute(shares[s], 'head', shift(s))  9.05 us
    ppermute x3, waiting for transfers between devices, on_device(): lax.ppermute(new_hidden, 'head', shift(s))  5.69 us
    ppermute x3, starting transfers between devices, on_device(): lax.ppermute(shares[s], 'head', shift(s))  5.67 us
    pallas_call x1, Pallas kernels, load(): pl.pallas_call(load_kernel, out_shape=jax.ShapeDtypeStruct(array.shape, a...  4.84 us
    pallas_call x1, Pallas kernels, project_qkv(): pl.pallas_call(qkv_kernel, out_shape=jax.ShapeDtypeStruct((TOK, QW), BF16...  4.76 us
  transfers between devices with their start and end apart: 27, of which 15 were waited for; matrix products, arithmetic and copies ran while one was open for 0% of the time, Pallas kernels for 25%

profile of v5, /device:TPU:1, one launch (start us, length us, event | category | flops | bytes accessed | tf_op | source)
XLA Modules:
  0.0 120.7 jit_solution(17497085933976003070)
XLA Ops:
  0.6 1.5 %collective-permute-start.3 = (bf16[13,128,512]{2,1,0:T(8,128)(2,1)}, bf16[13,128,512]{2,1,0:T(8,128)(2,1)S(1)}, u32[]{:S(2)}, u32[]{:S(2)}) collective-permute-start(bf16[13,128,512]{2,1,0:T(8,128)(2,1)} %refs_2_.1), channel_id=1, source_target_pairs={{0,1},{1,0},{2,3},{3,2},{4,5},{5,4},{6,7},{7,6},{8,9},{9,8},{10,11... | collective-permute-start | bytes 5111816 | tf_op jit(solution)/shard_map/ppermute | solution.py:690
  2.1 0.1 collective-permute-start.4
  2.2 0.1 stack.27.info.refs_0_
  2.3 0.1 broadcast_in_dim.2.rate_ref
  2.4 1.0 copy-done.4
  3.4 0.7 copy-done.7
  4.1 0.8 rotary.1
  4.9 1.5 %collective-permute-start.6 = (bf16[128,1024]{1,0:T(8,128)(2,1)S(1)}, bf16[128,1024]{1,0:T(8,128)(2,1)S(1)}, u32[]{:S(2)}, u32[]{:S(2)}) collective-permute-start(bf16[128,1024]{1,0:T(8,128)(2,1)S(1)} %get-tuple-element.54.refs_9_.refs_0_), channel_id=1, source_target_pairs={{0,2},{1,9},{2,0},{3,11},{4,6},{5,13},{6,4},{7,15},{8,10},{9,1},{1... | collective-permute-start | bytes 786440 | tf_op jit(solution)/shard_map/ppermute | solution.py:660
  6.3 0.6 collective-permute-start.5
  6.9 2.7 %collective-permute-start.2 = (bf16[512,128]{1,0:T(8,128)(2,1)S(1)}, bf16[512,128]{1,0:T(8,128)(2,1)S(1)}, u32[]{:S(2)}, u32[]{:S(2)}) collective-permute-start(bf16[512,128]{1,0:T(8,128)(2,1)S(1)} %get-tuple-element.55.refs_0_), channel_id=1, source_target_pairs={{0,6},{1,25},{2,0},{3,27},{4,2},{5,29},{6,4},{7,31},{8,14},{9,1},{... | collective-permute-start | bytes 393224 | tf_op jit(solution)/shard_map/ppermute | solution.py:656
  9.7 0.3 collective-permute-start.1
  10.0 0.7 collective-permute-start
  10.7 0.7 copy-done.12
  11.4 2.9 %page_lists.1 = (s32[8,33]{1,0:T(8,128)S(1)}, s32[8]{0:T(128)S(1)}) custom-call(s32[5]{0:T(128)S(1)} %stack.27.info.refs_0_, s32[8]{0:T(128)S(1)} %copy-done.7, s32[8,36]{1,0:T(8,128)S(1)} %copy-done.12), custom_call_target="tpu_custom_call" | custom-call | tf_op jit(solution)/shard_map/page_lists/pallas_call | solution.py:125
  14.3 0.0 copy-start.1
  14.3 4.7 %pool.1 = (bf16[13,128,512]{2,1,0:T(8,128)(2,1)S(1)}, bf16[13,128,512]{2,1,0:T(8,128)(2,1)S(1)}) custom-call(bf16[13,128,512]{2,1,0:T(8,128)(2,1)S(1)} %collective-permute-done.3.k_other, bf16[13,128,512]{2,1,0:T(8,128)(2,1)S(1)} %collective-permute-done.4.v_other), custom_call_target="tpu_custom_call" | custom-call | tf_op jit(solution)/shard_map/pool/pallas_call | solution.py:152
  19.0 0.0 copy-start
  19.0 0.0 copy-start.8
  19.1 0.4 collective-permute-start.7
  19.5 2.7 %collective-permute-start.10 = (bf16[4,512,128]{2,1,0:T(8,128)(2,1)S(1)}, bf16[4,512,128]{2,1,0:T(8,128)(2,1)S(1)}, u32[]{:S(2)}, u32[]{:S(2)}) collective-permute-start(bf16[4,512,128]{2,1,0:T(8,128)(2,1)S(1)} %stack.28.refs_4_), channel_id=1, source_target_pairs={{0,16},{1,5},{2,18},{3,7},{4,20},{5,1},{6,22},{7,3},{8,24},{9,13},... | collective-permute-start | bytes 1572872 | tf_op jit(solution)/shard_map/ppermute | solution.py:656
  22.2 1.5 %collective-permute-start.8 = (bf16[4,512,128]{2,1,0:T(8,128)(2,1)S(1)}, bf16[4,512,128]{2,1,0:T(8,128)(2,1)S(1)}, u32[]{:S(2)}, u32[]{:S(2)}) collective-permute-start(bf16[4,512,128]{2,1,0:T(8,128)(2,1)S(1)} %stack.28.refs_4_), channel_id=1, source_target_pairs={{0,24},{1,7},{2,26},{3,1},{4,28},{5,3},{6,30},{7,5},{8,0},{9,15},{... | collective-permute-start | bytes 1572872 | tf_op jit(solution)/shard_map/ppermute | solution.py:656
  23.8 3.0 %attend0.1.a_ref = bf16[4,544,128]{2,1,0:T(8,128)(2,1)S(1)} custom-call(s32[5]{0:T(128)S(1)} %stack.27.info.refs_0_, s32[8]{0:T(128)S(1)} %copy-done.8, s32[8,33]{1,0:T(8,128)S(1)} %get-tuple-element.59.refs_2_, s32[8]{0:T(128)S(1)} %get-tuple-element.60.refs_3_, bf16[4,512,128]{2,1,0:T(8,128)(2,1)S(1)} %stack.28.refs_4_, bf16[13,128,512]{2,1,0:T(8,128)(2,1)S(1)} %copy-done, ...), custom_call_target="tpu_custom_call" | custom-call | tf_op jit(solution)/shard_map/attend0/pallas_call | solution.py:358
  26.8 1.9 %collective-permute-done.7.refs_4_ = bf16[4,512,128]{2,1,0:T(8,128)(2,1)S(1)} collective-permute-done((bf16[4,512,128]{2,1,0:T(8,128)(2,1)S(1)}, bf16[4,512,128]{2,1,0:T(8,128)(2,1)S(1)}, u32[]{:S(2)}, u32[]{:S(2)}) %collective-permute-start.7) | collective-permute-done | bytes 524320 | tf_op jit(solution)/shard_map/ppermute | solution.py:656
  28.7 2.0 %collective-permute-start.11 = (bf16[2,128,1024]{2,1,0:T(8,128)(2,1)S(1)}, bf16[2,128,1024]{2,1,0:T(8,128)(2,1)S(1)}, u32[]{:S(2)}, u32[]{:S(2)}) collective-permute-start(bf16[2,128,1024]{2,1,0:T(8,128)(2,1)S(1)} %stack.29.refs_0_), channel_id=1, source_target_pairs={{0,6},{1,25},{2,4},{3,27},{4,2},{5,29},{6,0},{7,31},{8,14},{9,17},... | collective-permute-start | bytes 1572872 | tf_op jit(solution)/shard_map/ppermute | solution.py:660
  30.7 2.5 %attend1.1 = bf16[4,544,128]{2,1,0:T(8,128)(2,1)S(1)} custom-call(s32[5]{0:T(128)S(1)} %stack.27.info.refs_0_, s32[8]{0:T(128)S(1)} %copy-done.8, s32[8,33]{1,0:T(8,128)S(1)} %get-tuple-element.59.refs_2_, s32[8]{0:T(128)S(1)} %get-tuple-element.60.refs_3_, bf16[4,512,128]{2,1,0:T(8,128)(2,1)S(1)} %collective-permute-done.7.refs_4_, ...), custom_call_target="tpu_custom_call" | custom-call | tf_op jit(solution)/shard_map/attend1/pallas_call | solution.py:358
  33.2 1.8 %collective-permute-done.8.refs_4_ = bf16[4,512,128]{2,1,0:T(8,128)(2,1)S(1)} collective-permute-done((bf16[4,512,128]{2,1,0:T(8,128)(2,1)S(1)}, bf16[4,512,128]{2,1,0:T(8,128)(2,1)S(1)}, u32[]{:S(2)}, u32[]{:S(2)}) %collective-permute-start.8) | collective-permute-done | bytes 524320 | tf_op jit(solution)/shard_map/ppermute | solution.py:656
  35.0 3.0 %attend3.1 = bf16[4,544,128]{2,1,0:T(8,128)(2,1)S(1)} custom-call(s32[5]{0:T(128)S(1)} %stack.27.info.refs_0_, s32[8]{0:T(128)S(1)} %copy-done.8, s32[8,33]{1,0:T(8,128)S(1)} %get-tuple-element.59.refs_2_, s32[8]{0:T(128)S(1)} %get-tuple-element.60.refs_3_, bf16[4,512,128]{2,1,0:T(8,128)(2,1)S(1)} %collective-permute-done.8.refs_4_, ...), custom_call_target="tpu_custom_call" | custom-call | tf_op jit(solution)/shard_map/attend3/pallas_call | solution.py:358
  38.0 3.2 %collective-permute-start.13 = (bf16[4,544,128]{2,1,0:T(8,128)(2,1)S(1)}, bf16[4,544,128]{2,1,0:T(8,128)(2,1)S(1)}, u32[]{:S(2)}, u32[]{:S(2)}) collective-permute-start(bf16[4,544,128]{2,1,0:T(8,128)(2,1)S(1)} %attend3.1), channel_id=1, source_target_pairs={{0,8},{1,3},{2,10},{3,5},{4,12},{5,7},{6,14},{7,1},{8,16},{9,11},{... | collective-permute-start | bytes 1671176 | tf_op jit(solution)/shard_map/ppermute | solution.py:656
  41.2 0.6 collective-permute-done.11.refs_1_
  41.8 0.1 stack.30
  41.8 2.5 %attend2.1 = bf16[4,544,128]{2,1,0:T(8,128)(2,1)S(1)} custom-call(s32[5]{0:T(128)S(1)} %stack.27.info.refs_0_, s32[8]{0:T(128)S(1)} %copy-done.8, s32[8,33]{1,0:T(8,128)S(1)} %get-tuple-element.59.refs_2_, s32[8]{0:T(128)S(1)} %get-tuple-element.60.refs_3_, bf16[4,512,128]{2,1,0:T(8,128)(2,1)S(1)} %collective-permute-done.10.refs_4_, ...), custom_call_target="tpu_custom_call" | custom-call | tf_op jit(solution)/shard_map/attend2/pallas_call | solution.py:358
  44.3 0.0 copy-start.9
  44.3 4.3 %collective-permute-start.12 = (bf16[4,544,128]{2,1,0:T(8,128)(2,1)S(1)}, bf16[4,544,128]{2,1,0:T(8,128)(2,1)S(1)}, u32[]{:S(2)}, u32[]{:S(2)}) collective-permute-start(bf16[4,544,128]{2,1,0:T(8,128)(2,1)S(1)} %attend2.1), channel_id=1, source_target_pairs={{0,16},{1,5},{2,18},{3,7},{4,20},{5,1},{6,22},{7,3},{8,24},{9,13},... | collective-permute-start | bytes 1671176 | tf_op jit(solution)/shard_map/ppermute | solution.py:656
  48.7 2.8 %collective-permute-done.9.b_ref = bf16[4,544,128]{2,1,0:T(8,128)(2,1)S(1)} collective-permute-done((bf16[4,544,128]{2,1,0:T(8,128)(2,1)S(1)}, bf16[4,544,128]{2,1,0:T(8,128)(2,1)S(1)}, u32[]{:S(2)}, u32[]{:S(2)}) %collective-permute-start.9) | collective-permute-done | bytes 557088 | tf_op jit(solution)/shard_map/ppermute | solution.py:656
  51.4 6.3 %collective-permute-done.12.c_ref = bf16[4,544,128]{2,1,0:T(8,128)(2,1)S(1)} collective-permute-done((bf16[4,544,128]{2,1,0:T(8,128)(2,1)S(1)}, bf16[4,544,128]{2,1,0:T(8,128)(2,1)S(1)}, u32[]{:S(2)}, u32[]{:S(2)}) %collective-permute-start.12) | collective-permute-done | bytes 557088 | tf_op jit(solution)/shard_map/ppermute | solution.py:656
  57.7 0.5 join_rows.1
  58.2 2.3 %collective-permute-start.21 = (bf16[4,128,1024]{2,1,0:T(8,128)(2,1)S(1)}, bf16[4,128,1024]{2,1,0:T(8,128)(2,1)S(1)}, u32[]{:S(2)}, u32[]{:S(2)}) collective-permute-start(bf16[4,128,1024]{2,1,0:T(8,128)(2,1)S(1)} %bitcast.6), channel_id=1, source_target_pairs={{0,24},{1,7},{2,26},{3,1},{4,28},{5,3},{6,30},{7,5},{8,0},{9,15},{... | collective-permute-start | bytes 3145736 | tf_op jit(solution)/shard_map/ppermute | solution.py:656
  60.5 1.6 %collective-permute-start.14 = (bf16[544,128]{1,0:T(8,128)(2,1)S(1)}, bf16[544,128]{1,0:T(8,128)(2,1)S(1)}, u32[]{:S(2)}, u32[]{:S(2)}) collective-permute-start(bf16[544,128]{1,0:T(8,128)(2,1)S(1)} %get-tuple-element.80), channel_id=1, source_target_pairs={{0,6},{1,25},{2,0},{3,27},{4,2},{5,29},{6,4},{7,31},{8,14},{9,1},{... | collective-permute-start | bytes 417800 | tf_op jit(solution)/shard_map/ppermute | solution.py:656
  62.1 0.4 collective-permute-start.15
  62.4 0.5 collective-permute-start.16
  62.9 1.8 %collective-permute-done.14.b_ref = bf16[544,128]{1,0:T(8,128)(2,1)S(1)} collective-permute-done((bf16[544,128]{1,0:T(8,128)(2,1)S(1)}, bf16[544,128]{1,0:T(8,128)(2,1)S(1)}, u32[]{:S(2)}, u32[]{:S(2)}) %collective-permute-start.14) | collective-permute-done | bytes 139296 | tf_op jit(solution)/shard_map/ppermute | solution.py:656
  64.7 2.8 %collective-permute-done.15.c_ref = bf16[544,128]{1,0:T(8,128)(2,1)S(1)} collective-permute-done((bf16[544,128]{1,0:T(8,128)(2,1)S(1)}, bf16[544,128]{1,0:T(8,128)(2,1)S(1)}, u32[]{:S(2)}, u32[]{:S(2)}) %collective-permute-start.15) | collective-permute-done | bytes 139296 | tf_op jit(solution)/shard_map/ppermute | solution.py:656
  67.6 2.2 %collective-permute-done.16.d_ref = bf16[544,128]{1,0:T(8,128)(2,1)S(1)} collective-permute-done((bf16[544,128]{1,0:T(8,128)(2,1)S(1)}, bf16[544,128]{1,0:T(8,128)(2,1)S(1)}, u32[]{:S(2)}, u32[]{:S(2)}) %collective-permute-start.16) | collective-permute-done | bytes 139296 | tf_op jit(solution)/shard_map/ppermute | solution.py:656
  69.8 0.2 join_last.1.attention
  70.0 1.3 %dense.1 = (f32[128,1024]{1,0:T(8,128)S(1)}, bf16[128,1024]{1,0:T(8,128)(2,1)S(1)}, bf16[128,1024]{1,0:T(8,128)(2,1)S(1)}, bf16[128,1024]{1,0:T(8,128)(2,1)S(1)}) custom-call(s32[5]{0:T(128)S(1)} %stack.27.info.refs_0_, bf16[128,512]{1,0:T(8,128)(2,1)S(1)} %join_last.1.attention, bf16[512,4096]{1,0:T(8,128)(2,1)S(1)} %copy-done.2, f32[4096]{0:T(1024)S(1)} %copy-done.9, ...), custom_call_target="tpu_custom_call" | custom-call | tf_op jit(solution)/shard_map/dense/pallas_call | solution.py:444
  71.3 4.1 %collective-permute-done.21.refs_3_ = bf16[4,128,1024]{2,1,0:T(8,128)(2,1)S(1)} collective-permute-done((bf16[4,128,1024]{2,1,0:T(8,128)(2,1)S(1)}, bf16[4,128,1024]{2,1,0:T(8,128)(2,1)S(1)}, u32[]{:S(2)}, u32[]{:S(2)}) %collective-permute-start.21) | collective-permute-done | bytes 1048608 | tf_op jit(solution)/shard_map/ppermute | solution.py:656
  75.4 3.3 %collective-permute-done.20.refs_1_ = bf16[4,128,1024]{2,1,0:T(8,128)(2,1)S(1)} collective-permute-done((bf16[4,128,1024]{2,1,0:T(8,128)(2,1)S(1)}, bf16[4,128,1024]{2,1,0:T(8,128)(2,1)S(1)}, u32[]{:S(2)}, u32[]{:S(2)}) %collective-permute-start.20) | collective-permute-done | bytes 1048608 | tf_op jit(solution)/shard_map/ppermute | solution.py:656
  78.6 1.6 %collective-permute-start.17 = (bf16[128,1024]{1,0:T(8,128)(2,1)S(1)}, bf16[128,1024]{1,0:T(8,128)(2,1)S(1)}, u32[]{:S(2)}, u32[]{:S(2)}) collective-permute-start(bf16[128,1024]{1,0:T(8,128)(2,1)S(1)} %get-tuple-element.84), channel_id=1, source_target_pairs={{0,32},{32,64},{64,96},{96,0},{1,33},{33,65},{65,97},{97,1},{2,34}... | collective-permute-start | bytes 786440 | tf_op jit(solution)/shard_map/ppermute | solution.py:733
  80.3 3.3 %collective-permute-start.18 = (bf16[128,1024]{1,0:T(8,128)(2,1)S(1)}, bf16[128,1024]{1,0:T(8,128)(2,1)S(1)}, u32[]{:S(2)}, u32[]{:S(2)}) collective-permute-start(bf16[128,1024]{1,0:T(8,128)(2,1)S(1)} %get-tuple-element.85), channel_id=1, source_target_pairs={{0,64},{32,96},{64,0},{96,32},{1,65},{33,97},{65,1},{97,33},{2,66}... | collective-permute-start | bytes 786440 | tf_op jit(solution)/shard_map/ppermute | solution.py:733
  83.6 0.7 collective-permute-start.19
  84.3 2.5 %collective-permute-done.17.a = bf16[128,1024]{1,0:T(8,128)(2,1)S(1)} collective-permute-done((bf16[128,1024]{1,0:T(8,128)(2,1)S(1)}, bf16[128,1024]{1,0:T(8,128)(2,1)S(1)}, u32[]{:S(2)}, u32[]{:S(2)}) %collective-permute-start.17) | collective-permute-done | bytes 262176 | tf_op jit(solution)/shard_map/ppermute | solution.py:733
  86.8 6.5 %collective-permute-done.18.b = bf16[128,1024]{1,0:T(8,128)(2,1)S(1)} collective-permute-done((bf16[128,1024]{1,0:T(8,128)(2,1)S(1)}, bf16[128,1024]{1,0:T(8,128)(2,1)S(1)}, u32[]{:S(2)}, u32[]{:S(2)}) %collective-permute-start.18) | collective-permute-done | bytes 262176 | tf_op jit(solution)/shard_map/ppermute | solution.py:733
  93.3 0.1 collective-permute-done.19.c
  93.4 0.8 join_shares.1.x0
  94.2 0.3 stack.31.refs_0_
  94.5 0.0 copy-start.13
  94.5 3.2 %collective-permute-start.23 = (bf16[4,4,128,1024]{3,2,1,0:T(8,128)(2,1)S(1)}, bf16[4,4,128,1024]{3,2,1,0:T(8,128)(2,1)S(1)}, u32[]{:S(2)}, u32[]{:S(2)}) collective-permute-start(bf16[4,4,128,1024]{3,2,1,0:T(8,128)(2,1)S(1)} %stack.31.refs_0_), channel_id=1, source_target_pairs={{0,1},{1,0},{2,3},{3,2},{4,5},{5,4},{6,7},{7,6},{8,9},{9,8},{10,11... | collective-permute-start | bytes 12582920 | tf_op jit(solution)/shard_map/ppermute | solution.py:740
  97.7 3.4 %collective-permute-start.26 = (bf16[128,1024]{1,0:T(8,128)(2,1)S(1)}, bf16[128,1024]{1,0:T(8,128)(2,1)S(1)}, u32[]{:S(2)}, u32[]{:S(2)}) collective-permute-start(bf16[128,1024]{1,0:T(8,128)(2,1)S(1)} %copy-done.3), channel_id=1, source_target_pairs={{0,96},{32,0},{64,32},{96,64},{1,97},{33,1},{65,33},{97,65},{2,98}... | collective-permute-start | bytes 786440 | tf_op jit(solution)/shard_map/ppermute | solution.py:742
  101.0 0.7 collective-permute-start.24
  101.7 4.8 %load.1.weight = bf16[4096,1536]{1,0:T(8,128)(2,1)S(1)} custom-call(bf16[4096,1536]{1,0:T(8,128)(2,1)} %src), custom_call_target="tpu_custom_call" | custom-call | tf_op jit(solution)/shard_map/load/pallas_call | solution.py:181
  106.6 3.6 %patch.1 = (bf16[13,128,512]{2,1,0:T(8,128)(2,1)}, bf16[13,128,512]{2,1,0:T(8,128)(2,1)}, s32[1]{0:T(128)}) custom-call(s32[5]{0:T(128)S(1)} %stack.27.info.refs_0_, s32[8]{0:T(128)S(1)} %copy-done.8, s32[8,36]{1,0:T(8,128)S(1)} %copy-done.13, bf16[4,4,128,1024]{3,2,1,0:T(8,128)(2,1)S(1)} %stack.31.refs_0_, ...), custom_call_target="tpu_custom_call" | custom-call | tf_op jit(solution)/shard_map/patch/pallas_call | solution.py:617
  110.2 2.1 %collective-permute-done.26.x3 = bf16[128,1024]{1,0:T(8,128)(2,1)S(1)} collective-permute-done((bf16[128,1024]{1,0:T(8,128)(2,1)S(1)}, bf16[128,1024]{1,0:T(8,128)(2,1)S(1)}, u32[]{:S(2)}, u32[]{:S(2)}) %collective-permute-start.26) | collective-permute-done | bytes 262176 | tf_op jit(solution)/shard_map/ppermute | solution.py:742
  112.3 3.6 %collective-permute-done.24.x1 = bf16[128,1024]{1,0:T(8,128)(2,1)} collective-permute-done((bf16[128,1024]{1,0:T(8,128)(2,1)S(1)}, bf16[128,1024]{1,0:T(8,128)(2,1)}, u32[]{:S(2)}, u32[]{:S(2)}) %collective-permute-start.24) | collective-permute-done | bytes 262176 | tf_op jit(solution)/shard_map/ppermute | solution.py:742
  115.9 4.8 %project_qkv.1 = bf16[128,1536]{1,0:T(8,128)(2,1)} custom-call(s32[5]{0:T(128)S(1)} %stack.27.info.refs_0_, s32[1]{0:T(128)} %get-tuple-element.94.token, bf16[128,1024]{1,0:T(8,128)(2,1)S(1)} %copy-done.3, bf16[128,1024]{1,0:T(8,128)(2,1)} %collective-permute-done.24.x1, bf16[128,1024]{1,0:T(8,128)(2,1)} %collective-permute-done.25.x2, ...), custom_call_target="tpu_custom_call" | custom-call | tf_op jit(solution)/shard_map/project_qkv/pallas_call | solution.py:494
  (41 shorter events, 0.2 us)
Async XLA Ops:
  0.6 9.0 %collective-permute-start.3 = (bf16[13,128,512]{2,1,0:T(8,128)(2,1)}, bf16[13,128,512]{2,1,0:T(8,128)(2,1)S(1)}, u32[]{:S(2)}, u32[]{:S(2)}) collective-permute-start(bf16[13,128,512]{2,1,0:T(8,128)(2,1)} %refs_2_.1), channel_id=1, source_target_pairs={{0,1},{1,0},{2,3},{3,2},{4,5},{5,4},{6,7},{7,6},{8,9},{9,8},{10,11... | collective-permute-start | bytes 5111816 | tf_op jit(solution)/shard_map/ppermute | solution.py:690
  2.1 7.9 %collective-permute-start.4 = (bf16[13,128,512]{2,1,0:T(8,128)(2,1)}, bf16[13,128,512]{2,1,0:T(8,128)(2,1)S(1)}, u32[]{:S(2)}, u32[]{:S(2)}) collective-permute-start(bf16[13,128,512]{2,1,0:T(8,128)(2,1)} %refs_3_.1), channel_id=1, source_target_pairs={{0,1},{1,0},{2,3},{3,2},{4,5},{5,4},{6,7},{7,6},{8,9},{9,8},{10,11... | collective-permute-start | bytes 5111816 | tf_op jit(solution)/shard_map/ppermute | solution.py:691
  2.4 1.0 copy-start.4
  3.4 0.7 copy-start.7
  4.9 14.2 %collective-permute-start.6 = (bf16[128,1024]{1,0:T(8,128)(2,1)S(1)}, bf16[128,1024]{1,0:T(8,128)(2,1)S(1)}, u32[]{:S(2)}, u32[]{:S(2)}) collective-permute-start(bf16[128,1024]{1,0:T(8,128)(2,1)S(1)} %get-tuple-element.54.refs_9_.refs_0_), channel_id=1, source_target_pairs={{0,2},{1,9},{2,0},{3,11},{4,6},{5,13},{6,4},{7,15},{8,10},{9,1},{1... | collective-permute-start | bytes 786440 | tf_op jit(solution)/shard_map/ppermute | solution.py:660
  6.3 12.8 %collective-permute-start.5 = (bf16[128,1024]{1,0:T(8,128)(2,1)S(1)}, bf16[128,1024]{1,0:T(8,128)(2,1)S(1)}, u32[]{:S(2)}, u32[]{:S(2)}) collective-permute-start(bf16[128,1024]{1,0:T(8,128)(2,1)S(1)} %get-tuple-element.54.refs_9_.refs_0_), channel_id=1, source_target_pairs={{0,1},{1,0},{2,3},{3,2},{4,5},{5,4},{6,7},{7,6},{8,9},{9,8},{10,11... | collective-permute-start | bytes 786440 | tf_op jit(solution)/shard_map/ppermute | solution.py:692
  6.9 12.1 %collective-permute-start.2 = (bf16[512,128]{1,0:T(8,128)(2,1)S(1)}, bf16[512,128]{1,0:T(8,128)(2,1)S(1)}, u32[]{:S(2)}, u32[]{:S(2)}) collective-permute-start(bf16[512,128]{1,0:T(8,128)(2,1)S(1)} %get-tuple-element.55.refs_0_), channel_id=1, source_target_pairs={{0,6},{1,25},{2,0},{3,27},{4,2},{5,29},{6,4},{7,31},{8,14},{9,1},{... | collective-permute-start | bytes 393224 | tf_op jit(solution)/shard_map/ppermute | solution.py:656
  9.7 9.4 %collective-permute-start.1 = (bf16[512,128]{1,0:T(8,128)(2,1)S(1)}, bf16[512,128]{1,0:T(8,128)(2,1)S(1)}, u32[]{:S(2)}, u32[]{:S(2)}) collective-permute-start(bf16[512,128]{1,0:T(8,128)(2,1)S(1)} %get-tuple-element.55.refs_0_), channel_id=1, source_target_pairs={{0,4},{1,17},{2,6},{3,19},{4,0},{5,21},{6,2},{7,23},{8,12},{9,25},... | collective-permute-start | bytes 393224 | tf_op jit(solution)/shard_map/ppermute | solution.py:656
  10.0 9.0 %collective-permute-start = (bf16[512,128]{1,0:T(8,128)(2,1)S(1)}, bf16[512,128]{1,0:T(8,128)(2,1)S(1)}, u32[]{:S(2)}, u32[]{:S(2)}) collective-permute-start(bf16[512,128]{1,0:T(8,128)(2,1)S(1)} %get-tuple-element.55.refs_0_), channel_id=1, source_target_pairs={{0,2},{1,9},{2,4},{3,11},{4,6},{5,13},{6,0},{7,15},{8,10},{9,17},{... | collective-permute-start | bytes 393224 | tf_op jit(solution)/shard_map/ppermute | solution.py:656
  10.7 0.7 copy-start.12
  14.3 9.4 %copy-start.1 = (bf16[13,128,512]{2,1,0:T(8,128)(2,1)S(1)}, bf16[13,128,512]{2,1,0:T(8,128)(2,1)}, u32[]{:S(2)}) copy-start(bf16[13,128,512]{2,1,0:T(8,128)(2,1)} %refs_3_.1) | copy-start | bytes 5111812
  19.0 4.8 %copy-start = (bf16[13,128,512]{2,1,0:T(8,128)(2,1)S(1)}, bf16[13,128,512]{2,1,0:T(8,128)(2,1)}, u32[]{:S(2)}) copy-start(bf16[13,128,512]{2,1,0:T(8,128)(2,1)} %refs_2_.1) | copy-start | bytes 5111812
  19.0 4.8 %copy-start.8 = (s32[8]{0:T(128)S(1)}, s32[8]{0:T(128)}, u32[]{:S(2)}) copy-start(s32[8]{0:T(128)} %lens.5) | copy-start | bytes 100
  19.1 9.6 %collective-permute-start.7 = (bf16[4,512,128]{2,1,0:T(8,128)(2,1)S(1)}, bf16[4,512,128]{2,1,0:T(8,128)(2,1)S(1)}, u32[]{:S(2)}, u32[]{:S(2)}) collective-permute-start(bf16[4,512,128]{2,1,0:T(8,128)(2,1)S(1)} %stack.28.refs_4_), channel_id=1, source_target_pairs={{0,8},{1,3},{2,10},{3,5},{4,12},{5,7},{6,14},{7,1},{8,16},{9,11},{... | collective-permute-start | bytes 1572872 | tf_op jit(solution)/shard_map/ppermute | solution.py:656
  19.5 18.5 %collective-permute-start.10 = (bf16[4,512,128]{2,1,0:T(8,128)(2,1)S(1)}, bf16[4,512,128]{2,1,0:T(8,128)(2,1)S(1)}, u32[]{:S(2)}, u32[]{:S(2)}) collective-permute-start(bf16[4,512,128]{2,1,0:T(8,128)(2,1)S(1)} %stack.28.refs_4_), channel_id=1, source_target_pairs={{0,16},{1,5},{2,18},{3,7},{4,20},{5,1},{6,22},{7,3},{8,24},{9,13},... | collective-permute-start | bytes 1572872 | tf_op jit(solution)/shard_map/ppermute | solution.py:656
  22.2 12.8 %collective-permute-start.8 = (bf16[4,512,128]{2,1,0:T(8,128)(2,1)S(1)}, bf16[4,512,128]{2,1,0:T(8,128)(2,1)S(1)}, u32[]{:S(2)}, u32[]{:S(2)}) collective-permute-start(bf16[4,512,128]{2,1,0:T(8,128)(2,1)S(1)} %stack.28.refs_4_), channel_id=1, source_target_pairs={{0,24},{1,7},{2,26},{3,1},{4,28},{5,3},{6,30},{7,5},{8,0},{9,15},{... | collective-permute-start | bytes 1572872 | tf_op jit(solution)/shard_map/ppermute | solution.py:656
  28.7 13.0 %collective-permute-start.11 = (bf16[2,128,1024]{2,1,0:T(8,128)(2,1)S(1)}, bf16[2,128,1024]{2,1,0:T(8,128)(2,1)S(1)}, u32[]{:S(2)}, u32[]{:S(2)}) collective-permute-start(bf16[2,128,1024]{2,1,0:T(8,128)(2,1)S(1)} %stack.29.refs_0_), channel_id=1, source_target_pairs={{0,6},{1,25},{2,4},{3,27},{4,2},{5,29},{6,0},{7,31},{8,14},{9,17},... | collective-permute-start | bytes 1572872 | tf_op jit(solution)/shard_map/ppermute | solution.py:660
  38.0 10.7 %collective-permute-start.13 = (bf16[4,544,128]{2,1,0:T(8,128)(2,1)S(1)}, bf16[4,544,128]{2,1,0:T(8,128)(2,1)S(1)}, u32[]{:S(2)}, u32[]{:S(2)}) collective-permute-start(bf16[4,544,128]{2,1,0:T(8,128)(2,1)S(1)} %attend3.1), channel_id=1, source_target_pairs={{0,8},{1,3},{2,10},{3,5},{4,12},{5,7},{6,14},{7,1},{8,16},{9,11},{... | collective-permute-start | bytes 1671176 | tf_op jit(solution)/shard_map/ppermute | solution.py:656
  41.2 10.3 %collective-permute-start.9 = (bf16[4,544,128]{2,1,0:T(8,128)(2,1)S(1)}, bf16[4,544,128]{2,1,0:T(8,128)(2,1)S(1)}, u32[]{:S(2)}, u32[]{:S(2)}) collective-permute-start(bf16[4,544,128]{2,1,0:T(8,128)(2,1)S(1)} %attend1.1), channel_id=1, source_target_pairs={{0,24},{1,7},{2,26},{3,1},{4,28},{5,3},{6,30},{7,5},{8,0},{9,15},{... | collective-permute-start | bytes 1671176 | tf_op jit(solution)/shard_map/ppermute | solution.py:656
  41.8 28.1 %copy-start.2 = (bf16[512,4096]{1,0:T(8,128)(2,1)S(1)}, bf16[512,4096]{1,0:T(8,128)(2,1)}, u32[]{:S(2)}) copy-start(bf16[512,4096]{1,0:T(8,128)(2,1)} %weight.1) | copy-start | bytes 12582916
  44.3 25.7 %copy-start.5 = (bf16[128,1024]{1,0:T(8,128)(2,1)S(1)}, bf16[128,1024]{1,0:T(8,128)(2,1)}, u32[]{:S(2)}) copy-start(bf16[128,1024]{1,0:T(8,128)(2,1)} %hidden.1) | copy-start | bytes 786436
  44.3 25.7 %copy-start.6 = (bf16[128,1024]{1,0:T(8,128)(2,1)S(1)}, bf16[128,1024]{1,0:T(8,128)(2,1)}, u32[]{:S(2)}) copy-start(bf16[128,1024]{1,0:T(8,128)(2,1)} %branch.1) | copy-start | bytes 786436
  44.3 25.7 %copy-start.9 = (f32[4096]{0:T(1024)S(1)}, f32[4096]{0:T(1024)}, u32[]{:S(2)}) copy-start(f32[4096]{0:T(1024)} %bias.2) | copy-start | bytes 49156
  44.3 13.4 %collective-permute-start.12 = (bf16[4,544,128]{2,1,0:T(8,128)(2,1)S(1)}, bf16[4,544,128]{2,1,0:T(8,128)(2,1)S(1)}, u32[]{:S(2)}, u32[]{:S(2)}) collective-permute-start(bf16[4,544,128]{2,1,0:T(8,128)(2,1)S(1)} %attend2.1), channel_id=1, source_target_pairs={{0,16},{1,5},{2,18},{3,7},{4,20},{5,1},{6,22},{7,3},{8,24},{9,13},... | collective-permute-start | bytes 1671176 | tf_op jit(solution)/shard_map/ppermute | solution.py:656
  58.2 17.2 %collective-permute-start.21 = (bf16[4,128,1024]{2,1,0:T(8,128)(2,1)S(1)}, bf16[4,128,1024]{2,1,0:T(8,128)(2,1)S(1)}, u32[]{:S(2)}, u32[]{:S(2)}) collective-permute-start(bf16[4,128,1024]{2,1,0:T(8,128)(2,1)S(1)} %bitcast.6), channel_id=1, source_target_pairs={{0,24},{1,7},{2,26},{3,1},{4,28},{5,3},{6,30},{7,5},{8,0},{9,15},{... | collective-permute-start | bytes 3145736 | tf_op jit(solution)/shard_map/ppermute | solution.py:656
  60.5 18.1 %collective-permute-start.20 = (bf16[4,128,1024]{2,1,0:T(8,128)(2,1)S(1)}, bf16[4,128,1024]{2,1,0:T(8,128)(2,1)S(1)}, u32[]{:S(2)}, u32[]{:S(2)}) collective-permute-start(bf16[4,128,1024]{2,1,0:T(8,128)(2,1)S(1)} %bitcast.7), channel_id=1, source_target_pairs={{0,8},{1,3},{2,10},{3,5},{4,12},{5,7},{6,14},{7,1},{8,16},{9,11},{... | collective-permute-start | bytes 3145736 | tf_op jit(solution)/shard_map/ppermute | solution.py:656
  60.5 4.2 %collective-permute-start.14 = (bf16[544,128]{1,0:T(8,128)(2,1)S(1)}, bf16[544,128]{1,0:T(8,128)(2,1)S(1)}, u32[]{:S(2)}, u32[]{:S(2)}) collective-permute-start(bf16[544,128]{1,0:T(8,128)(2,1)S(1)} %get-tuple-element.80), channel_id=1, source_target_pairs={{0,6},{1,25},{2,0},{3,27},{4,2},{5,29},{6,4},{7,31},{8,14},{9,1},{... | collective-permute-start | bytes 417800 | tf_op jit(solution)/shard_map/ppermute | solution.py:656
  62.1 5.5 %collective-permute-start.15 = (bf16[544,128]{1,0:T(8,128)(2,1)S(1)}, bf16[544,128]{1,0:T(8,128)(2,1)S(1)}, u32[]{:S(2)}, u32[]{:S(2)}) collective-permute-start(bf16[544,128]{1,0:T(8,128)(2,1)S(1)} %get-tuple-element.81), channel_id=1, source_target_pairs={{0,4},{1,17},{2,6},{3,19},{4,0},{5,21},{6,2},{7,23},{8,12},{9,25},... | collective-permute-start | bytes 417800 | tf_op jit(solution)/shard_map/ppermute | solution.py:656
  62.4 7.3 %collective-permute-start.16 = (bf16[544,128]{1,0:T(8,128)(2,1)S(1)}, bf16[544,128]{1,0:T(8,128)(2,1)S(1)}, u32[]{:S(2)}, u32[]{:S(2)}) collective-permute-start(bf16[544,128]{1,0:T(8,128)(2,1)S(1)} %get-tuple-element.82), channel_id=1, source_target_pairs={{0,2},{1,9},{2,4},{3,11},{4,6},{5,13},{6,0},{7,15},{8,10},{9,17},{... | collective-permute-start | bytes 417800 | tf_op jit(solution)/shard_map/ppermute | solution.py:656
  78.6 15.6 %collective-permute-start.22 = (bf16[4,128,1024]{2,1,0:T(8,128)(2,1)S(1)}, bf16[4,128,1024]{2,1,0:T(8,128)(2,1)S(1)}, u32[]{:S(2)}, u32[]{:S(2)}) collective-permute-start(bf16[4,128,1024]{2,1,0:T(8,128)(2,1)S(1)} %collective-permute-done.20.refs_1_), channel_id=1, source_target_pairs={{0,8},{1,3},{2,10},{3,5},{4,12},{5,7},{6,14},{7,1},{8,16},{9,11},{... | collective-permute-start | bytes 3145736 | tf_op jit(solution)/shard_map/ppermute | solution.py:656
  78.6 8.1 %collective-permute-start.17 = (bf16[128,1024]{1,0:T(8,128)(2,1)S(1)}, bf16[128,1024]{1,0:T(8,128)(2,1)S(1)}, u32[]{:S(2)}, u32[]{:S(2)}) collective-permute-start(bf16[128,1024]{1,0:T(8,128)(2,1)S(1)} %get-tuple-element.84), channel_id=1, source_target_pairs={{0,32},{32,64},{64,96},{96,0},{1,33},{33,65},{65,97},{97,1},{2,34}... | collective-permute-start | bytes 786440 | tf_op jit(solution)/shard_map/ppermute | solution.py:733
  80.3 13.0 %collective-permute-start.18 = (bf16[128,1024]{1,0:T(8,128)(2,1)S(1)}, bf16[128,1024]{1,0:T(8,128)(2,1)S(1)}, u32[]{:S(2)}, u32[]{:S(2)}) collective-permute-start(bf16[128,1024]{1,0:T(8,128)(2,1)S(1)} %get-tuple-element.85), channel_id=1, source_target_pairs={{0,64},{32,96},{64,0},{96,32},{1,65},{33,97},{65,1},{97,33},{2,66}... | collective-permute-start | bytes 786440 | tf_op jit(solution)/shard_map/ppermute | solution.py:733
  83.6 9.8 %collective-permute-start.19 = (bf16[128,1024]{1,0:T(8,128)(2,1)S(1)}, bf16[128,1024]{1,0:T(8,128)(2,1)S(1)}, u32[]{:S(2)}, u32[]{:S(2)}) collective-permute-start(bf16[128,1024]{1,0:T(8,128)(2,1)S(1)} %get-tuple-element.86), channel_id=1, source_target_pairs={{0,96},{32,0},{64,32},{96,64},{1,97},{33,1},{65,33},{97,65},{2,98}... | collective-permute-start | bytes 786440 | tf_op jit(solution)/shard_map/ppermute | solution.py:733
  94.2 3.5 %copy-start.3 = (bf16[128,1024]{1,0:T(8,128)(2,1)S(1)}, bf16[128,1024]{1,0:T(8,128)(2,1)}, u32[]{:S(2)}) copy-start(bf16[128,1024]{1,0:T(8,128)(2,1)} %join_shares.1.x0) | copy-start | bytes 786436
  94.5 12.2 %copy-start.13 = (s32[8,36]{1,0:T(8,128)S(1)}, s32[8,36]{1,0:T(8,128)}, u32[]{:S(2)}) copy-start(s32[8,36]{1,0:T(8,128)} %table.3) | copy-start | bytes 3460
  94.5 12.1 %collective-permute-start.23 = (bf16[4,4,128,1024]{3,2,1,0:T(8,128)(2,1)S(1)}, bf16[4,4,128,1024]{3,2,1,0:T(8,128)(2,1)S(1)}, u32[]{:S(2)}, u32[]{:S(2)}) collective-permute-start(bf16[4,4,128,1024]{3,2,1,0:T(8,128)(2,1)S(1)} %stack.31.refs_0_), channel_id=1, source_target_pairs={{0,1},{1,0},{2,3},{3,2},{4,5},{5,4},{6,7},{7,6},{8,9},{9,8},{10,11... | collective-permute-start | bytes 12582920 | tf_op jit(solution)/shard_map/ppermute | solution.py:740
  97.7 14.6 %collective-permute-start.26 = (bf16[128,1024]{1,0:T(8,128)(2,1)S(1)}, bf16[128,1024]{1,0:T(8,128)(2,1)S(1)}, u32[]{:S(2)}, u32[]{:S(2)}) collective-permute-start(bf16[128,1024]{1,0:T(8,128)(2,1)S(1)} %copy-done.3), channel_id=1, source_target_pairs={{0,96},{32,0},{64,32},{96,64},{1,97},{33,1},{65,33},{97,65},{2,98}... | collective-permute-start | bytes 786440 | tf_op jit(solution)/shard_map/ppermute | solution.py:742
  101.0 11.3 %collective-permute-start.25 = (bf16[128,1024]{1,0:T(8,128)(2,1)S(1)}, bf16[128,1024]{1,0:T(8,128)(2,1)}, u32[]{:S(2)}, u32[]{:S(2)}) collective-permute-start(bf16[128,1024]{1,0:T(8,128)(2,1)S(1)} %copy-done.3), channel_id=1, source_target_pairs={{0,64},{32,96},{64,0},{96,32},{1,65},{33,97},{65,1},{97,33},{2,66}... | collective-permute-start | bytes 786440 | tf_op jit(solution)/shard_map/ppermute | solution.py:742
  101.0 14.9 %collective-permute-start.24 = (bf16[128,1024]{1,0:T(8,128)(2,1)S(1)}, bf16[128,1024]{1,0:T(8,128)(2,1)}, u32[]{:S(2)}, u32[]{:S(2)}) collective-permute-start(bf16[128,1024]{1,0:T(8,128)(2,1)S(1)} %copy-done.3), channel_id=1, source_target_pairs={{0,32},{32,64},{64,96},{96,0},{1,33},{33,65},{65,97},{97,1},{2,34}... | collective-permute-start | bytes 786440 | tf_op jit(solution)/shard_map/ppermute | solution.py:742
  106.6 9.3 %copy-start.10 = (f32[4096]{0:T(1024)S(1)}, f32[4096]{0:T(1024)}, u32[]{:S(2)}) copy-start(f32[4096]{0:T(1024)} %gain.1) | copy-start | bytes 49156
  106.6 9.3 %copy-start.11 = (f32[4096]{0:T(1024)S(1)}, f32[4096]{0:T(1024)}, u32[]{:S(2)}) copy-start(f32[4096]{0:T(1024)} %shift.1) | copy-start | bytes 49156
  106.6 9.3 %copy-start.14 = (f32[1536]{0:T(1024)S(1)}, f32[1536]{0:T(1024)}, u32[]{:S(2)}) copy-start(f32[1536]{0:T(1024)} %bias.3) | copy-start | bytes 18436
